TPU v7x, 128 devices: a whole 4x4x4 slice. The times are simulated.
128 devices in a mesh: sub: 32 (over x, y, core), rep: 4 (over z).
Axes of the slice: x: 4, y: 4, z: 4, core: 2. Of those that a mesh axis runs over, the one named last changes fastest.
Arguments:
- loads: bfloat16 [256, 256, 1024], P('sub', 'rep'), may hold values from -6 to 6
- operators: bfloat16 [256, 1024, 1024], P('sub'), may hold values from -0.1875 to 0.1875
- owner: int32 [2048, 1], P('sub'), may hold values from 0 to 31; in each aligned block of 64 rows (0 to 63, 64 to 127, ...) at most 4 rows name the same one
- dual_block: int32 [2048], P('sub'), may hold values from 0 to 15
- scale_index: int32 [65536], P('sub'), may hold values from 0 to 3
- basis: bfloat16 [65536, 1024], P('sub'), may hold values from -0.0234375 to 0.0234375
- coarse: bfloat16 [1024, 1024], replicated, may hold values from -1.5 to 1.5
Outputs:
- start: float32 [256, 65536], P('rep', 'sub')
- resid: float32 [256, 65536], P('rep', 'sub')
Inputs may be any that keep to these rules, and one draw needn't show every extreme that they name: Among the blocks of the subdomains of one index of sub (aligned blocks of 64 rows), no owner is named more than 4 times, a bound that some block reaches.
All inputs are finite; a program needn't handle non-finite values.
Results may differ from a plain program's by a relative error of at most 0.0075.
Values may be sent and summed in bfloat16 or wider, within the bound.
No kernel may reach another device: no remote copies, remote signals or barrier semaphores. Data moves between devices by JAX's collectives and lax.ppermute only.
A program may use at most 128 MiB of HBM per device.

v0:
```python
import jax
import jax.numpy as jnp
from jax import lax
from jax.sharding import PartitionSpec as P

BLK = 128


def apply_local(inputs, operators):
    return jnp.einsum("skl,slm->skm", inputs, operators, preferred_element_type=jnp.float32).astype(
        jnp.bfloat16
    )


def make_blocks(values, width):
    count, columns, local = values.shape
    return (
        values.reshape(count, columns, local // width, width)
        .transpose(0, 2, 1, 3)
        .reshape(-1, columns, width)
    )


def from_blocks(blocks, count):
    total, columns, width = blocks.shape
    per_sub = total // count
    return (
        blocks.reshape(count, per_sub, columns, width)
        .transpose(0, 2, 1, 3)
        .reshape(count, columns, per_sub * width)
    )


def pack_slots(blocks, dests, ranks, peers, slots):
    columns, width = (blocks.shape[1], blocks.shape[2])
    return jnp.zeros((peers, slots, columns, width), jnp.bfloat16).at[dests, ranks].set(blocks)


def accumulate(received, got_ids, own_blocks, weight):
    columns, width = (received.shape[2], received.shape[3])
    flat = received.reshape(-1, columns, width).astype(jnp.float32)
    total = jnp.zeros((own_blocks, columns, width), jnp.float32).at[got_ids.reshape(-1)].add(flat)
    return total.transpose(1, 0, 2).reshape(columns, own_blocks * width) * weight[None, :]


def per_device(loads, operators, owner, dual_block, scale_index, basis, coarse):
    sub_count = loads.shape[0]
    width = BLK
    peers = lax.axis_size("sub")
    dests = owner[:, 0]
    nblocks = dests.shape[0]
    slots = max(2, 2 * nblocks // peers)
    own_blocks = basis.shape[0] // width
    positions = jnp.arange(nblocks, dtype=jnp.int32)
    earlier = positions[None, :] < positions[:, None]
    same = dests[None, :] == dests[:, None]
    ranks = jnp.sum(jnp.logical_and(earlier, same), axis=1)
    weight = 1.0 / (1.0 + scale_index.astype(jnp.float32))
    terms = apply_local(loads, operators)
    packed = pack_slots(make_blocks(terms, width), dests, ranks, peers, slots)
    id_slots = jnp.zeros((peers, slots), jnp.int32).at[dests, ranks].set(dual_block)
    received, got_ids = (
        lax.all_to_all(packed, "sub", split_axis=0, concat_axis=0, tiled=True),
        lax.all_to_all(id_slots, "sub", split_axis=0, concat_axis=0, tiled=True),
    )
    dual = accumulate(received, got_ids, own_blocks, weight)
    coeff = jnp.dot(dual.astype(jnp.bfloat16), basis, preferred_element_type=jnp.float32)
    summed = lax.psum(coeff, "sub")
    solved = jnp.dot(
        summed.astype(jnp.bfloat16), coarse, preferred_element_type=jnp.float32
    ).astype(jnp.bfloat16)
    start = lax.dot_general(
        solved, basis, (((1,), (1,)), ((), ())), preferred_element_type=jnp.float32
    )
    columns = start.shape[0]
    start_blocks = start.astype(jnp.bfloat16).reshape(columns, own_blocks, width).transpose(1, 0, 2)
    requested = start_blocks[got_ids]
    returned = lax.all_to_all(requested, "sub", split_axis=0, concat_axis=0, tiled=True)
    picked = returned[dests, ranks]
    local = from_blocks(picked, sub_count)
    again = apply_local(local, operators)
    received_again = lax.all_to_all(
        pack_slots(make_blocks(again, width), dests, ranks, peers, slots),
        "sub",
        split_axis=0,
        concat_axis=0,
        tiled=True,
    )
    applied = accumulate(received_again, got_ids, own_blocks, weight)
    return (start, dual - applied)


def solution(mesh):
    return jax.shard_map(
        per_device,
        mesh=mesh,
        in_specs=(
            P("sub", "rep", None),
            P("sub", None, None),
            P("sub", None),
            P("sub"),
            P("sub"),
            P("sub", None),
            P(),
        ),
        out_specs=(P("rep", "sub"), P("rep", "sub")),
        check_vma=False,
    )
```

profile of v0, /device:TPU:1, one launch (start us, length us, event | category | flops | bytes accessed | tf_op | source)
XLA Modules:
  0.0 336.0 jit_solution(8166071477639882503)
XLA Ops:
  0.6 0.0 copy-start
  0.6 1.0 convert_reduce_fusion
  1.6 0.7 fusion.15
  2.3 5.7 %scatter_fusion = s32[32,4]{0,1:T(4,128)S(1)} fusion(s32[32,4]{0,1:T(4,128)S(1)} %broadcast.75, s32[64]{0:T(128)S(1)} %get-tuple-element.2, s32[64]{0:T(128)} %param.10), kind=kCustom, calls=%fused_computation.2 | custom fusion | bytes 1280 | tf_op jit(solution)/shard_map/scatter | solution.py:61
  8.1 0.7 copy.33
  8.8 8.6 %all-to-all-start = ((s32[32,1,4]{2,1,0:T(1,128)}), s32[32,1,4]{2,1,0:T(1,128)S(1)}, u32[]{:S(2)}, u32[]{:S(2)}) async-start(s32[32,1,4]{2,1,0:T(1,128)} %copy.33), calls=%async_computation | async-start | bytes 32768 | tf_op jit(solution)/shard_map/all_to_all | solution.py:64
  17.4 9.1 %fusion = bf16[8,8,8,8,128]{4,3,2,1,0:T(8,128)(2,1)S(1)} fusion(bf16[8,64,1024]{2,1,0:T(8,128)(2,1)} %param.7, bf16[8,1024,1024]{2,1,0:T(8,128)(2,1)} %param.8), kind=kOutput, calls=%fused_computation.11 | convolution fusion | flops 1074266112 | bytes 18874368 | tf_op jit(solution)/shard_map/skl,slm->skm/dot_general | solution.py:10
  26.5 0.3 copy.63
  26.8 1.9 broadcast.81.clone
  28.7 8.9 %scatter_fusion.1 = bf16[32,4,64,128]{3,2,1,0:T(8,128)(2,1)} fusion(bf16[32,4,64,128]{3,2,1,0:T(8,128)(2,1)} %broadcast.81.clone, s32[64]{0:T(128)S(1)} %get-tuple-element.2, bf16[64,64,128]{2,1,0:T(8,128)(2,1)S(1)} %bitcast.87), kind=kCustom, calls=%fused_computation.3 | custom fusion | bytes 3146240 | tf_op jit(solution)/shard_map/scatter | solution.py:36
  37.5 0.0 copy-start.1
  37.5 0.0 all-to-all-done
  37.5 7.6 %all-to-all-start.1 = ((bf16[32,4,64,128]{3,2,1,0:T(8,128)(2,1)}), bf16[32,4,64,128]{3,2,1,0:T(8,128)(2,1)}, u32[]{:S(2)}, u32[]{:S(2)}) async-start(bf16[32,4,64,128]{3,2,1,0:T(8,128)(2,1)} %scatter_fusion.1), calls=%async_computation.1 | async-start | bytes 4194304 | tf_op jit(solution)/shard_map/all_to_all | solution.py:63
  45.1 0.0 copy-done.1
  45.1 0.5 broadcast.184
  45.6 0.7 reduce.3
  46.3 0.1 reshape.115
  46.4 0.1 copy.37
  46.5 0.1 copy.38
  46.6 0.1 reshape.129
  46.8 26.7 %all-to-all-done.1 = bf16[32,4,64,128]{3,2,1,0:T(8,128)(2,1)} async-done(((bf16[32,4,64,128]{3,2,1,0:T(8,128)(2,1)}), bf16[32,4,64,128]{3,2,1,0:T(8,128)(2,1)}, u32[]{:S(2)}, u32[]{:S(2)}) %all-to-all-start.1) | async-done | bytes 2097184 | tf_op jit(solution)/shard_map/all_to_all | solution.py:63
  73.5 4.0 %bitcast_convert_fusion.1 = f32[128,64,128]{2,1,0:T(8,128)} fusion(bf16[32,4,64,128]{3,2,1,0:T(8,128)(2,1)} %all-to-all-done.1), kind=kLoop, calls=%fused_computation.8 | loop fusion | flops 1048576 | bytes 6291456 | tf_op jit(solution)/shard_map/convert_element_type | solution.py:41
  77.5 13.5 %scatter_fusion.2 = f32[16,64,128]{2,1,0:T(8,128)S(1)} fusion(f32[16,64,128]{2,1,0:T(8,128)S(1)} %broadcast.74.clone, s32[128]{0:T(128)S(1)} %fusion.14, f32[128,64,128]{2,1,0:T(8,128)} %bitcast_convert_fusion.1), kind=kCustom, calls=%fused_computation.4 | custom fusion | flops 1048576 | bytes 12583424 | tf_op jit(solution)/shard_map/scatter-add | solution.py:42
  91.0 3.0 fusion.7
  94.1 121.1 %all-reduce.1 = bf16[64,1024]{1,0:T(8,128)(2,1)S(1)} all-reduce(f32[64,1024]{1,0:T(8,128)S(1)} %fusion.7), channel_id=1, replica_groups=mesh['sub'=32,'rep'=4] {'sub'}, use_global_device_ids=true, to_apply=%region_4.0 | all-reduce | flops 65536 | bytes 393216 | tf_op jit(solution)/shard_map/psum | solution.py:68
  215.2 0.0 copy-done
  215.2 4.8 %fusion.2 = f32[64,2048]{1,0:T(8,128)} fusion(bf16[2048,1024]{1,0:T(8,128)(2,1)} %param.12, bf16[1024,1024]{1,0:T(8,128)(2,1)S(1)} %copy-done, bf16[64,1024]{1,0:T(8,128)(2,1)S(1)} %all-reduce.1), kind=kOutput, calls=%fused_computation.14 | convolution fusion | flops 402718720 | bytes 6946816 | tf_op jit(solution)/shard_map/dot_general | solution.py:72
  220.0 1.1 bitcast_bitcast_fusion
  221.1 2.1 gather_fusion
  223.2 38.3 %all_to_all.27 = bf16[32,4,64,128]{3,2,1,0:T(8,128)(2,1)} all-to-all(bf16[32,4,64,128]{3,2,1,0:T(8,128)(2,1)} %bitcast.85), channel_id=1, replica_groups=mesh['sub'=32,'rep'=4] {'sub'}, dimensions={0} | all-to-all | bytes 4194304 | tf_op jit(solution)/shard_map/all_to_all | solution.py:78
  261.5 3.3 gather_fusion.1
  264.8 9.1 %fusion.1 = bf16[8,8,8,8,128]{4,3,2,1,0:T(8,128)(2,1)S(1)} fusion(bf16[8,1024,1024]{2,1,0:T(8,128)(2,1)} %param.8, bf16[8,8,8,8,128]{4,3,2,1,0:T(8,128)(2,1)} %bitcast.88), kind=kOutput, calls=%fused_computation.12 | convolution fusion | flops 1074266112 | bytes 18874368 | tf_op jit(solution)/shard_map/skl,slm->skm/dot_general | solution.py:10
  273.9 1.3 copy.62
  275.2 1.9 broadcast.81
  277.1 9.8 %scatter_fusion.3 = bf16[32,4,64,128]{3,2,1,0:T(8,128)(2,1)} fusion(bf16[32,4,64,128]{3,2,1,0:T(8,128)(2,1)} %broadcast.81, s32[64]{0:T(128)S(1)} %get-tuple-element.2, bf16[64,64,128]{2,1,0:T(8,128)(2,1)} %bitcast.86), kind=kCustom, calls=%fused_computation.5 | custom fusion | bytes 3146240 | tf_op jit(solution)/shard_map/scatter | solution.py:36
  286.9 32.1 %all_to_all.28 = bf16[32,4,64,128]{3,2,1,0:T(8,128)(2,1)S(1)} all-to-all(bf16[32,4,64,128]{3,2,1,0:T(8,128)(2,1)} %scatter_fusion.3), channel_id=1, replica_groups=mesh['sub'=32,'rep'=4] {'sub'}, dimensions={0} | all-to-all | bytes 4194304 | tf_op jit(solution)/shard_map/all_to_all | solution.py:82
  319.0 2.5 bitcast_convert_fusion
  321.5 13.5 %scatter_fusion.4 = f32[16,64,128]{2,1,0:T(8,128)S(1)} fusion(f32[16,64,128]{2,1,0:T(8,128)S(1)} %broadcast.74, s32[128]{0:T(128)S(1)} %fusion.14, f32[128,64,128]{2,1,0:T(8,128)} %bitcast_convert_fusion), kind=kCustom, calls=%fused_computation.6 | custom fusion | flops 1048576 | bytes 12583424 | tf_op jit(solution)/shard_map/scatter-add | solution.py:42
  335.1 0.9 fusion.5
  (7 shorter events, 0.1 us)
Async XLA Ops:
  0.6 214.6 %copy-start = (bf16[1024,1024]{1,0:T(8,128)(2,1)S(1)}, bf16[1024,1024]{1,0:T(8,128)(2,1)}, u32[]{:S(2)}) copy-start(bf16[1024,1024]{1,0:T(8,128)(2,1)} %param.13) | copy-start | bytes 6291460
  8.8 28.8 %all-to-all-start = ((s32[32,1,4]{2,1,0:T(1,128)}), s32[32,1,4]{2,1,0:T(1,128)S(1)}, u32[]{:S(2)}, u32[]{:S(2)}) async-start(s32[32,1,4]{2,1,0:T(1,128)} %copy.33), calls=%async_computation | async-start | bytes 32768 | tf_op jit(solution)/shard_map/all_to_all | solution.py:64
  37.5 7.6 %copy-start.1 = (s32[2048]{0:T(1024)S(1)}, s32[2048]{0:T(1024)}, u32[]{:S(2)}) copy-start(s32[2048]{0:T(1024)} %param.11) | copy-start | bytes 24580
  37.5 35.9 %all-to-all-start.1 = ((bf16[32,4,64,128]{3,2,1,0:T(8,128)(2,1)}), bf16[32,4,64,128]{3,2,1,0:T(8,128)(2,1)}, u32[]{:S(2)}, u32[]{:S(2)}) async-start(bf16[32,4,64,128]{3,2,1,0:T(8,128)(2,1)} %scatter_fusion.1), calls=%async_computation.1 | async-start | bytes 4194304 | tf_op jit(solution)/shard_map/all_to_all | solution.py:63
where the time goes:
time: 338 us; the launch traced here: 336 us
  blocking collectives  191 us (57%)
  other arithmetic  37.9 us (11%)
  local copies, waits for them, and re-layouts  36.8 us (11%)
  waiting for transfers between devices  26.7 us (8%)
  matrix products  26.1 us (8%)
  starting transfers between devices  16.2 us (5%)
    psum x1, blocking collectives, per_device(): summed = lax.psum(coeff, 'sub')  121 us
    all_to_all x1, blocking collectives, per_device(): lax.all_to_all(requested, 'sub', split_axis=0, concat_axis=0, tiled=True)  38.3 us
    all_to_all x1, blocking collectives, per_device(): lax.all_to_all(pack_slots(make_blocks(again, width), dests, ranks, peers,...  32.1 us
    scatter-add x2, other arithmetic, accumulate(): jnp.zeros((own_blocks, columns, width), jnp.float32).at[got_ids.reshape(-1)]  27.1 us
    all_to_all x1, waiting for transfers between devices, per_device(): lax.all_to_all(packed, 'sub', split_axis=0, concat_axis=0, tiled=True)  26.7 us
    scatter x2, local copies, waits for them, and re-layouts, pack_slots(): jnp.zeros((peers, slots, columns, width), jnp.bfloat16).at[dests, ranks]  18.7 us
    dot_general x2, matrix products, apply_local(): jnp.einsum('skl,slm->skm', inputs, operators, preferred_element_type=jnp....  18.3 us
    all_to_all x1, starting transfers between devices, per_device(): lax.all_to_all(id_slots, 'sub', split_axis=0, concat_axis=0, tiled=True)  8.59 us
  transfers between devices with their start and end apart: 2, of which 1 were waited for; matrix products, arithmetic and copies ran while one was open for 6% of the time, Pallas kernels for 0%

commit v1 on v0

v1 whole, which is shorter than its diff:
```python
import jax
import jax.numpy as jnp
from jax import lax
from jax.experimental import pallas as pl
from jax.experimental.pallas import tpu as pltpu
from jax.sharding import PartitionSpec as P

BLK = 128
PEERS = 32
CAP = 4
COLS = 64
L = 1024
BPS = 8
NSUB = 8
NBLK = NSUB * BPS
OB = 16
NB = 1024
IDROWS = 8
SLOTROWS = CAP * COLS
BF = jnp.bfloat16
F32 = jnp.float32
ANY = pl.BlockSpec(memory_space=pl.ANY)
SMEM = pl.BlockSpec(memory_space=pltpu.SMEM)
LIMIT = 56 * 1024 * 1024


def params(**kw):
    return pltpu.CompilerParams(vmem_limit_bytes=LIMIT, **kw)


def block_copy(obuf, out, pos, sem, i):
    p = pos[i]
    return pltpu.make_async_copy(
        obuf.at[i],
        out.at[p // CAP, pl.ds(pl.multiple_of((p % CAP) * COLS, COLS), COLS)],
        sem.at[i],
    )


def send_rows(prod, s, obuf, out, pos, sem):
    for j in range(BPS):
        obuf[s * BPS + j] = prod[:, j * BLK : (j + 1) * BLK].astype(BF)
    for j in range(BPS):
        block_copy(obuf, out, pos, sem, s * BPS + j).start()


def wait_rows(obuf, out, pos, sem):
    def body(i, c):
        block_copy(obuf, out, pos, sem, i).wait()
        return c

    lax.fori_loop(0, NBLK, body, 0)


def first_kernel(owner, dual_block, loads, ops, out, pos, count, obuf, idbuf, sem, idsem):
    s = pl.program_id(0)

    @pl.when(s == 0)
    def _():
        def zero(i, c):
            count[i] = 0
            return c

        lax.fori_loop(0, PEERS, zero, 0)
        row = lax.broadcasted_iota(jnp.int32, (PEERS, BLK), 0)
        lane = lax.broadcasted_iota(jnp.int32, (PEERS, BLK), 1)
        flat = row * CAP + lane
        flat = jnp.where(lane < CAP, flat, -1)

        def rank(i, ids):
            d = owner[i]
            r = count[d]
            count[d] = r + 1
            p = d * CAP + r
            pos[i] = p
            return jnp.where(flat == p, dual_block[i], ids)

        ids = lax.fori_loop(0, NBLK, rank, jnp.full((PEERS, BLK), -1, jnp.int32))
        idbuf[...] = jnp.broadcast_to(ids.astype(F32)[:, None, :], (PEERS, IDROWS, BLK)).astype(BF)
        pltpu.make_async_copy(idbuf, out.at[:, pl.ds(SLOTROWS, IDROWS)], idsem).start()

    prod = jnp.dot(loads[0], ops[0], preferred_element_type=F32)
    send_rows(prod, s, obuf, out, pos, sem)

    @pl.when(s == NSUB - 1)
    def _():
        pltpu.make_async_copy(idbuf, out.at[:, pl.ds(SLOTROWS, IDROWS)], idsem).wait()
        wait_rows(obuf, out, pos, sem)


def first_apply(owner, dual_block, loads, operators):
    return pl.pallas_call(
        first_kernel,
        out_shape=(
            jax.ShapeDtypeStruct((PEERS, SLOTROWS + IDROWS, BLK), BF),
            jax.ShapeDtypeStruct((NBLK,), jnp.int32),
        ),
        grid_spec=pltpu.PrefetchScalarGridSpec(
            num_scalar_prefetch=2,
            grid=(NSUB,),
            in_specs=[
                pl.BlockSpec((1, COLS, L), lambda s, o, d: (s, 0, 0)),
                pl.BlockSpec((1, L, L), lambda s, o, d: (s, 0, 0)),
            ],
            out_specs=[ANY, SMEM],
            scratch_shapes=[
                pltpu.SMEM((PEERS,), jnp.int32),
                pltpu.VMEM((NBLK, COLS, BLK), BF),
                pltpu.VMEM((PEERS, IDROWS, BLK), BF),
                pltpu.SemaphoreType.DMA((NBLK,)),
                pltpu.SemaphoreType.DMA,
            ],
        ),
        compiler_params=params(),
        name="first_apply",
    )(owner, dual_block, loads, operators)


def second_kernel(pos, back, ops, out, local, obuf, sem):
    s = pl.program_id(0)
    for j in range(BPS):
        p = pos[s * BPS + j]
        local[:, j * BLK : (j + 1) * BLK] = back[
            p // CAP, pl.ds(pl.multiple_of((p % CAP) * COLS, COLS), COLS), :
        ]
    prod = jnp.dot(local[...], ops[0], preferred_element_type=F32)
    send_rows(prod, s, obuf, out, pos, sem)

    @pl.when(s == NSUB - 1)
    def _():
        wait_rows(obuf, out, pos, sem)


def second_apply(pos, back, operators):
    return pl.pallas_call(
        second_kernel,
        out_shape=jax.ShapeDtypeStruct((PEERS, SLOTROWS, BLK), BF),
        grid_spec=pltpu.PrefetchScalarGridSpec(
            num_scalar_prefetch=1,
            grid=(NSUB,),
            in_specs=[
                pl.BlockSpec((PEERS, SLOTROWS, BLK), lambda s, p: (0, 0, 0)),
                pl.BlockSpec((1, L, L), lambda s, p: (s, 0, 0)),
            ],
            out_specs=ANY,
            scratch_shapes=[
                pltpu.VMEM((COLS, L), BF),
                pltpu.VMEM((NBLK, COLS, BLK), BF),
                pltpu.SemaphoreType.DMA((NBLK,)),
            ],
        ),
        compiler_params=params(),
        name="second_apply",
    )(pos, back, operators)


def add_slots(received, ids, total):
    total[...] = jnp.zeros_like(total)

    def peer(p, c):
        for q in range(CAP):
            g = ids[p, q]

            @pl.when(g >= 0)
            def _():
                total[g] = total[g] + received[p, q * COLS : (q + 1) * COLS, :].astype(F32)

        return c

    lax.fori_loop(0, PEERS, peer, 0)


def project_kernel(received, scale, basis, coarse, dual, partial, ids_out, total, narrow, basis_v, coarse_v, idv, ids, sem):
    basis_copy = pltpu.make_async_copy(basis, basis_v, sem.at[0])
    coarse_copy = pltpu.make_async_copy(coarse, coarse_v, sem.at[1])
    basis_copy.start()
    coarse_copy.start()
    idv[...] = received[:, SLOTROWS : SLOTROWS + IDROWS, :].astype(F32)[:, 0, :].astype(jnp.int32)
    ids_copy = pltpu.make_async_copy(idv, ids, sem.at[2])
    ids_copy.start()
    ids_out[...] = idv[...]
    ids_copy.wait()
    add_slots(received, ids, total)
    weight = 1.0 / (1.0 + scale[...].astype(F32))
    for b in range(OB):
        owned = total[b] * weight[b : b + 1, :]
        dual[b] = owned
        narrow[:, b * BLK : (b + 1) * BLK] = owned.astype(BF)
    basis_copy.wait()
    coeff = jnp.dot(narrow[...], basis_v[...], preferred_element_type=F32)
    high = coeff.astype(BF)
    low = (coeff - high.astype(F32)).astype(BF)
    coarse_copy.wait()
    both = jnp.dot(jnp.concatenate([high, low], axis=0), coarse_v[...], preferred_element_type=F32)
    solved = both[:COLS] + both[COLS:]
    for a in range(8):
        for b in range(4):
            partial[a * 4 + b] = solved[a * 8 : (a + 1) * 8, b * 256 : (b + 1) * 256]


def project(received, scale, basis, coarse):
    return pl.pallas_call(
        project_kernel,
        out_shape=(
            jax.ShapeDtypeStruct((OB, COLS, BLK), F32),
            jax.ShapeDtypeStruct((PEERS, 8, 256), F32),
            jax.ShapeDtypeStruct((PEERS, BLK), jnp.int32),
        ),
        in_specs=[
            pl.BlockSpec(memory_space=pltpu.VMEM),
            pl.BlockSpec(memory_space=pltpu.VMEM),
            ANY,
            ANY,
        ],
        out_specs=[pl.BlockSpec(memory_space=pltpu.VMEM)] * 3,
        scratch_shapes=[
            pltpu.VMEM((OB, COLS, BLK), F32),
            pltpu.VMEM((COLS, OB * BLK), BF),
            pltpu.VMEM((OB * BLK, NB), BF),
            pltpu.VMEM((NB, NB), BF),
            pltpu.VMEM((PEERS, BLK), jnp.int32),
            pltpu.SMEM((PEERS, BLK), jnp.int32),
            pltpu.SemaphoreType.DMA((3,)),
        ],
        compiler_params=params(),
        name="project",
    )(received, scale, basis, coarse)


def reduce_kernel(parts, out):
    total = parts[0]
    for p in range(1, PEERS):
        total = total + parts[p]
    out[...] = jnp.broadcast_to(total.astype(BF)[None], out.shape)


def reduce_parts(parts):
    return pl.pallas_call(
        reduce_kernel,
        out_shape=jax.ShapeDtypeStruct((PEERS, 8, 256), BF),
        compiler_params=params(),
        name="reduce_parts",
    )(parts)


STEPS = 4
ROWS = OB * BLK // STEPS


def start_kernel(ids, gathered, basis, start, out, solved, blocks, sem):
    n = pl.program_id(0)

    @pl.when(n == 0)
    def _():
        for a in range(8):
            for b in range(4):
                solved[a * 8 : (a + 1) * 8, b * 256 : (b + 1) * 256] = gathered[a * 4 + b]

    value = lax.dot_general(
        solved[...], basis[...], (((1,), (1,)), ((), ())), preferred_element_type=F32
    )
    start[...] = value
    for k in range(ROWS // BLK):
        blocks[n * (ROWS // BLK) + k] = value[:, k * BLK : (k + 1) * BLK].astype(BF)

    def copy(p, q, g):
        return pltpu.make_async_copy(
            blocks.at[g], out.at[p, pl.ds(q * COLS, COLS)], sem.at[p * CAP + q]
        )

    @pl.when(n == STEPS - 1)
    def _():
        def begin(p, c):
            for q in range(CAP):
                g = ids[p, q]

                @pl.when(g >= 0)
                def _():
                    copy(p, q, g).start()

            return c

        def finish(p, c):
            for q in range(CAP):
                g = ids[p, q]

                @pl.when(g >= 0)
                def _():
                    copy(p, q, g).wait()

            return c

        lax.fori_loop(0, PEERS, begin, 0)
        lax.fori_loop(0, PEERS, finish, 0)


def start_values(ids, gathered, basis):
    return pl.pallas_call(
        start_kernel,
        out_shape=(
            jax.ShapeDtypeStruct((COLS, OB * BLK), F32),
            jax.ShapeDtypeStruct((PEERS, SLOTROWS, BLK), BF),
        ),
        grid_spec=pltpu.PrefetchScalarGridSpec(
            num_scalar_prefetch=1,
            grid=(STEPS,),
            in_specs=[
                pl.BlockSpec((PEERS, 8, 256), lambda n, i: (0, 0, 0)),
                pl.BlockSpec((ROWS, NB), lambda n, i: (n, 0)),
            ],
            out_specs=[pl.BlockSpec((COLS, ROWS), lambda n, i: (0, n)), ANY],
            scratch_shapes=[
                pltpu.VMEM((COLS, NB), BF),
                pltpu.VMEM((OB, COLS, BLK), BF),
                pltpu.SemaphoreType.DMA((PEERS * CAP,)),
            ],
        ),
        compiler_params=params(),
        name="start_values",
    )(ids, gathered, basis)


def resid_kernel(ids, received, scale, dual, resid, total):
    add_slots(received, ids, total)
    weight = 1.0 / (1.0 + scale[...].astype(F32))
    for b in range(OB):
        resid[:, b * BLK : (b + 1) * BLK] = dual[b] - total[b] * weight[b : b + 1, :]


def residual(ids, received, scale, dual):
    return pl.pallas_call(
        resid_kernel,
        out_shape=jax.ShapeDtypeStruct((COLS, OB * BLK), F32),
        in_specs=[SMEM] + [pl.BlockSpec(memory_space=pltpu.VMEM)] * 3,
        out_specs=pl.BlockSpec(memory_space=pltpu.VMEM),
        scratch_shapes=[pltpu.VMEM((OB, COLS, BLK), F32)],
        compiler_params=params(),
        name="residual",
    )(ids, received, scale, dual)


def exchange(values):
    return lax.all_to_all(values, "sub", split_axis=0, concat_axis=0, tiled=True)


def per_device(loads, operators, owner, dual_block, scale_index, basis, coarse):
    scale = scale_index.reshape(OB, BLK)
    packed, pos = first_apply(owner.reshape(NBLK), dual_block, loads, operators)
    received = exchange(packed)
    dual, partial, ids = project(received, scale, basis, coarse)
    gathered = exchange(reduce_parts(exchange(partial)))
    start, requested = start_values(ids, gathered, basis)
    again = second_apply(pos, exchange(requested), operators)
    return (start, residual(ids, exchange(again), scale, dual))


def solution(mesh):
    return jax.shard_map(
        per_device,
        mesh=mesh,
        in_specs=(
            P("sub", "rep", None),
            P("sub", None, None),
            P("sub", None),
            P("sub"),
            P("sub"),
            P("sub", None),
            P(),
        ),
        out_specs=(P("rep", "sub"), P("rep", "sub")),
        check_vma=False,
    )
```

time: 338 us -> 177 us (0.52)
  blocking collectives: 191 us -> 130 us
  Pallas kernels: 0 us -> 44.9 us
  other arithmetic: 37.9 us -> 0 us
  local copies, waits for them, and re-layouts: 36.8 us -> 0 us
  waiting for transfers between devices: 26.7 us -> 0 us
  matrix products: 26.1 us -> 0 us
  starting transfers between devices: 16.2 us -> 0 us
    psum x1 -> x0, blocking collectives: 121 us -> none  [per_device(): summed = lax.psum(coeff, 'sub')]
    all_to_all x2 -> x5, blocking collectives: 70.4 us -> 130 us  [exchange(): lax.all_to_all(values, 'sub', split_axis=0, concat_axis=0, tiled=True)]
    pallas_call x0 -> x6, Pallas kernels: none -> 44.9 us  [the longest x1 12.9 us: first_apply(): pl.pallas_call(first_kernel, out_shape=(jax.ShapeDtypeStruct((PEERS, SLOT...]
    scatter-add x2 -> x0, other arithmetic: 27.1 us -> none  [accumulate(): jnp.zeros((own_blocks, columns, width), jnp.float32).at[got_ids.reshape(-1)]]
    all_to_all x2 -> x0, waiting for transfers between devices: 26.7 us -> none  [the longest x1 26.7 us: per_device(): lax.all_to_all(packed, 'sub', split_axis=0, concat_axis=0, tiled=True)]
    dot_general x4 -> x0, matrix products: 26.1 us -> none  [the longest x2 18.3 us: apply_local(): jnp.einsum('skl,slm->skm', inputs, operators, preferred_element_type=jnp....]
    scatter x3 -> x0, local copies, waits for them, and re-layouts: 24.4 us -> none  [the longest x2 18.7 us: pack_slots(): jnp.zeros((peers, slots, columns, width), jnp.bfloat16).at[dests, ranks]]
    all_to_all x2 -> x0, starting transfers between devices: 16.2 us -> none  [the longest x1 8.59 us: per_device(): lax.all_to_all(id_slots, 'sub', split_axis=0, concat_axis=0, tiled=True)]
  transfers between devices with their start and end apart: 2 -> 0, of which waited for: 1 -> 0; matrix products, arithmetic and copies ran while one was open for 6% -> 0% of each run, Pallas kernels for 0% -> 0%
where the time goes in v1:
time: 177 us; the launch traced here: 176 us
  blocking collectives  130 us (73%)
  Pallas kernels  44.9 us (25%)
    all_to_all x5, blocking collectives, exchange(): lax.all_to_all(values, 'sub', split_axis=0, concat_axis=0, tiled=True)  130 us
    pallas_call x1, Pallas kernels, first_apply(): pl.pallas_call(first_kernel, out_shape=(jax.ShapeDtypeStruct((PEERS, SLOT...  12.9 us
    pallas_call x1, Pallas kernels, second_apply(): pl.pallas_call(second_kernel, out_shape=jax.ShapeDtypeStruct((PEERS, SLOT...  12.2 us
    pallas_call x1, Pallas kernels, start_values(): pl.pallas_call(start_kernel, out_shape=(jax.ShapeDtypeStruct((COLS, OB *...  8.1 us
    pallas_call x1, Pallas kernels, project(): pl.pallas_call(project_kernel, out_shape=(jax.ShapeDtypeStruct((OB, COLS,...  6.03 us
    pallas_call x1, Pallas kernels, residual(): pl.pallas_call(resid_kernel, out_shape=jax.ShapeDtypeStruct((COLS, OB * B...  3.98 us

profile of v1, /device:TPU:1, one launch (start us, length us, event | category | flops | bytes accessed | tf_op | source)
XLA Modules:
  0.0 175.6 jit_solution(2846027027142402570)
XLA Ops:
  0.6 12.9 %first_apply.1 = (bf16[32,264,128]{2,1,0:T(8,128)(2,1)}, s32[64]{0:T(128)}) custom-call(s32[64]{0:T(128)} %bitcast.4, s32[64]{0:T(128)} %dual_block.1, bf16[8,64,1024]{2,1,0:T(8,128)(2,1)} %loads.1, bf16[8,1024,1024]{2,1,0:T(8,128)(2,1)} %ops.3), custom_call_target="tpu_custom_call" | custom-call | tf_op jit(solution)/shard_map/first_apply/pallas_call | solution.py:92
  13.6 38.4 %all_to_all.25.received = bf16[32,264,128]{2,1,0:T(8,128)(2,1)} all-to-all(bf16[32,264,128]{2,1,0:T(8,128)(2,1)} %get-tuple-element.9), channel_id=1, replica_groups=mesh['sub'=32,'rep'=4] {'sub'}, dimensions={0} | all-to-all | bytes 4325376 | tf_op jit(solution)/shard_map/all_to_all | solution.py:343
  51.9 6.0 %project.1 = (f32[16,64,128]{2,1,0:T(8,128)}, f32[32,8,256]{2,1,0:T(8,128)}, s32[32,128]{1,0:T(8,128)}) custom-call(bf16[32,264,128]{2,1,0:T(8,128)(2,1)} %all_to_all.25.received, s32[16,128]{1,0:T(8,128)} %bitcast.2, bf16[2048,1024]{1,0:T(8,128)(2,1)} %basis.3, bf16[1024,1024]{1,0:T(8,128)(2,1)} %coarse.1), custom_call_target="tpu_custom_call" | custom-call | tf_op jit(solution)/shard_map/project/pallas_call | solution.py:202
  58.0 13.7 %all_to_all.26.parts = f32[32,8,256]{2,1,0:T(8,128)} all-to-all(f32[32,8,256]{2,1,0:T(8,128)} %get-tuple-element.11), channel_id=1, replica_groups=mesh['sub'=32,'rep'=4] {'sub'}, dimensions={0} | all-to-all | bytes 524288 | tf_op jit(solution)/shard_map/all_to_all | solution.py:343
  71.7 1.6 reduce_parts.1
  73.4 12.2 %all_to_all.27.gathered = bf16[32,8,256]{2,1,0:T(8,128)(2,1)} all-to-all(bf16[32,8,256]{2,1,0:T(8,128)(2,1)} %reduce_parts.1), channel_id=1, replica_groups=mesh['sub'=32,'rep'=4] {'sub'}, dimensions={0} | all-to-all | bytes 262144 | tf_op jit(solution)/shard_map/all_to_all | solution.py:343
  85.6 8.1 %start_values.1 = (f32[64,2048]{1,0:T(8,128)}, bf16[32,256,128]{2,1,0:T(8,128)(2,1)}) custom-call(s32[32,128]{1,0:T(8,128)} %get-tuple-element.10.ids, bf16[32,8,256]{2,1,0:T(8,128)(2,1)} %all_to_all.27.gathered, bf16[2048,1024]{1,0:T(8,128)(2,1)} %basis.3), custom_call_target="tpu_custom_call" | custom-call | tf_op jit(solution)/shard_map/start_values/pallas_call | solution.py:298
  93.7 33.0 %all_to_all.28.back = bf16[32,256,128]{2,1,0:T(8,128)(2,1)} all-to-all(bf16[32,256,128]{2,1,0:T(8,128)(2,1)} %get-tuple-element.14), channel_id=1, replica_groups=mesh['sub'=32,'rep'=4] {'sub'}, dimensions={0} | all-to-all | bytes 4194304 | tf_op jit(solution)/shard_map/all_to_all | solution.py:343
  126.7 12.2 %second_apply.1 = bf16[32,256,128]{2,1,0:T(8,128)(2,1)} custom-call(s32[64]{0:T(128)} %get-tuple-element.13.pos, bf16[32,256,128]{2,1,0:T(8,128)(2,1)} %all_to_all.28.back, bf16[8,1024,1024]{2,1,0:T(8,128)(2,1)} %ops.3), custom_call_target="tpu_custom_call" | custom-call | tf_op jit(solution)/shard_map/second_apply/pallas_call | solution.py:135
  138.9 32.8 %all_to_all.29.received = bf16[32,256,128]{2,1,0:T(8,128)(2,1)} all-to-all(bf16[32,256,128]{2,1,0:T(8,128)(2,1)} %second_apply.1), channel_id=1, replica_groups=mesh['sub'=32,'rep'=4] {'sub'}, dimensions={0} | all-to-all | bytes 4194304 | tf_op jit(solution)/shard_map/all_to_all | solution.py:343
  171.6 4.0 %residual.1 = f32[64,2048]{1,0:T(8,128)} custom-call(s32[32,128]{1,0:T(8,128)} %get-tuple-element.10.ids, bf16[32,256,128]{2,1,0:T(8,128)(2,1)} %all_to_all.29.received, s32[16,128]{1,0:T(8,128)} %bitcast.3, f32[16,64,128]{2,1,0:T(8,128)} %get-tuple-element.15.dual), custom_call_target="tpu_custom_call" | custom-call | tf_op jit(solution)/shard_map/residual/pallas_call | solution.py:331

commit v2 on v0

v2 whole, which is shorter than its diff:
```python
import jax
import jax.numpy as jnp
from jax import lax
from jax.experimental import pallas as pl
from jax.experimental.pallas import tpu as pltpu
from jax.sharding import PartitionSpec as P

BLK = 128
PEERS = 32
CAP = 4
COLS = 64
L = 1024
BPS = 8
NSUB = 8
NBLK = NSUB * BPS
OB = 16
NB = 1024
IDROWS = 8
SLOTROWS = CAP * COLS
BF = jnp.bfloat16
F32 = jnp.float32
HBM = pl.BlockSpec(memory_space=pl.ANY)
SMEM = pl.BlockSpec(memory_space=pltpu.SMEM)
VMEM = pl.BlockSpec(memory_space=pltpu.VMEM)
AHEAD = 4


def params(mib):
    return pltpu.CompilerParams(vmem_limit_bytes=mib * 1024 * 1024)


def in_hbm(x):
    return pltpu.with_memory_space_constraint(x, pltpu.HBM)


def in_vmem(x):
    return pltpu.with_memory_space_constraint(x, pltpu.VMEM)


def slot(ref, p):
    return ref.at[p // CAP, pl.ds(pl.multiple_of((p % CAP) * COLS, COLS), COLS)]


def first_kernel(owner, dual_block, loads, ops, out, pos, ops_v, count, loads_v, sem, load_sem):
    load_copy = pltpu.make_async_copy(loads, loads_v, load_sem)
    copies = [pltpu.make_async_copy(ops.at[s], ops_v.at[s], sem.at[s]) for s in range(NSUB)]
    load_copy.start()
    for s in range(AHEAD):
        copies[s].start()

    def zero(i, c):
        count[i] = 0
        return c

    lax.fori_loop(0, PEERS, zero, 0)
    row = lax.broadcasted_iota(jnp.int32, (PEERS, BLK), 0)
    lane = lax.broadcasted_iota(jnp.int32, (PEERS, BLK), 1)
    flat = jnp.where(lane < CAP, row * CAP + lane, -1)

    def rank(i, ids):
        d = owner[i]
        r = count[d]
        count[d] = r + 1
        p = d * CAP + r
        pos[i] = p
        return jnp.where(flat == p, dual_block[i], ids)

    ids = lax.fori_loop(0, NBLK, rank, jnp.full((PEERS, BLK), -1, jnp.int32))
    out[:, SLOTROWS : SLOTROWS + IDROWS, :] = jnp.broadcast_to(
        ids.astype(F32)[:, None, :], (PEERS, IDROWS, BLK)
    ).astype(BF)
    load_copy.wait()
    for s in range(NSUB):
        copies[s].wait()
        if s + AHEAD < NSUB:
            copies[s + AHEAD].start()
        prod = jnp.dot(loads_v[s], ops_v[s], preferred_element_type=F32)
        for j in range(BPS):
            slot(out, pos[s * BPS + j])[...] = prod[:, j * BLK : (j + 1) * BLK].astype(BF)


def first_apply(owner, dual_block, loads, operators):
    return pl.pallas_call(
        first_kernel,
        out_shape=(
            pltpu.VMEM((PEERS, SLOTROWS + IDROWS, BLK), BF),
            jax.ShapeDtypeStruct((NBLK,), jnp.int32),
            pltpu.VMEM((NSUB, L, L), BF),
        ),
        in_specs=[SMEM, SMEM, HBM, HBM],
        out_specs=[VMEM, SMEM, VMEM],
        scratch_shapes=[
            pltpu.SMEM((PEERS,), jnp.int32),
            pltpu.VMEM((NSUB, COLS, L), BF),
            pltpu.SemaphoreType.DMA((NSUB,)),
            pltpu.SemaphoreType.DMA,
        ],
        compiler_params=params(8),
        name="first_apply",
    )(owner, dual_block, in_hbm(loads), in_hbm(operators))


def second_kernel(pos, back, ops, out, local):
    for s in range(NSUB):
        for j in range(BPS):
            local[s, :, j * BLK : (j + 1) * BLK] = slot(back, pos[s * BPS + j])[...]
    for s in range(NSUB):
        prod = jnp.dot(local[s], ops[s], preferred_element_type=F32)
        for j in range(BPS):
            slot(out, pos[s * BPS + j])[...] = prod[:, j * BLK : (j + 1) * BLK].astype(BF)


def second_apply(pos, back, operators):
    return pl.pallas_call(
        second_kernel,
        out_shape=pltpu.VMEM((PEERS, SLOTROWS, BLK), BF),
        in_specs=[SMEM, VMEM, VMEM],
        out_specs=VMEM,
        scratch_shapes=[pltpu.VMEM((NSUB, COLS, L), BF)],
        compiler_params=params(8),
        name="second_apply",
    )(pos, in_vmem(back), in_vmem(operators))


def add_slots(received, ids, totals):
    for q in range(CAP):
        totals[q][...] = jnp.zeros(totals[q].shape, F32)

    def peer(p, c):
        for q in range(CAP):
            g = ids[p, q]
            g = jnp.where(g < 0, OB, g)
            totals[q][g] = totals[q][g] + received[p, q * COLS : (q + 1) * COLS, :].astype(F32)
        return c

    lax.fori_loop(0, PEERS, peer, 0, unroll=2)


def sum_totals(totals, b):
    return (totals[0][b] + totals[1][b]) + (totals[2][b] + totals[3][b])


TOTALS = [pltpu.VMEM((OB + 1, COLS, BLK), F32)] * CAP


def project_kernel(received, scale, basis, coarse, dual, partial, ids_out, t0, t1, t2, t3, narrow, idv, ids, sem):
    totals = (t0, t1, t2, t3)
    idv[...] = received[:, SLOTROWS : SLOTROWS + IDROWS, :].astype(F32)[:, 0, :].astype(jnp.int32)
    ids_copy = pltpu.make_async_copy(idv, ids, sem)
    ids_copy.start()
    ids_out[...] = idv[...]
    ids_copy.wait()
    add_slots(received, ids, totals)
    weight = 1.0 / (1.0 + scale[...].astype(F32))
    for b in range(OB):
        owned = sum_totals(totals, b) * weight[b : b + 1, :]
        dual[b] = owned
        narrow[:, b * BLK : (b + 1) * BLK] = owned.astype(BF)
    coeff = jnp.dot(narrow[...], basis[...], preferred_element_type=F32)
    high = coeff.astype(BF)
    low = (coeff - high.astype(F32)).astype(BF)
    both = jnp.dot(jnp.concatenate([high, low], axis=0), coarse[...], preferred_element_type=F32)
    solved = both[:COLS] + both[COLS:]
    for a in range(8):
        for b in range(4):
            partial[a * 4 + b] = solved[a * 8 : (a + 1) * 8, b * 256 : (b + 1) * 256]


def project(received, scale, basis, coarse):
    return pl.pallas_call(
        project_kernel,
        out_shape=(
            pltpu.VMEM((OB, COLS, BLK), F32),
            pltpu.VMEM((PEERS, 8, 256), F32),
            jax.ShapeDtypeStruct((PEERS, BLK), jnp.int32),
        ),
        in_specs=[VMEM] * 4,
        out_specs=[VMEM] * 3,
        scratch_shapes=TOTALS
        + [
            pltpu.VMEM((COLS, OB * BLK), BF),
            pltpu.VMEM((PEERS, BLK), jnp.int32),
            pltpu.SMEM((PEERS, BLK), jnp.int32),
            pltpu.SemaphoreType.DMA,
        ],
        compiler_params=params(8),
        name="project",
    )(in_vmem(received), scale, in_vmem(basis), in_vmem(coarse))


def reduce_kernel(parts, out):
    total = parts[0]
    for p in range(1, PEERS):
        total = total + parts[p]
    out[...] = jnp.broadcast_to(total.astype(BF)[None], out.shape)


def reduce_parts(parts):
    return pl.pallas_call(
        reduce_kernel,
        out_shape=pltpu.VMEM((PEERS, 8, 256), BF),
        in_specs=[VMEM],
        out_specs=VMEM,
        compiler_params=params(4),
        name="reduce_parts",
    )(in_vmem(parts))


def start_kernel(ids, gathered, basis, start, out, solved, blocks):
    for a in range(8):
        for b in range(4):
            solved[a * 8 : (a + 1) * 8, b * 256 : (b + 1) * 256] = gathered[a * 4 + b]
    value = lax.dot_general(
        solved[...], basis[...], (((1,), (1,)), ((), ())), preferred_element_type=F32
    )
    start[...] = value
    for k in range(OB):
        blocks[k] = value[:, k * BLK : (k + 1) * BLK].astype(BF)

    def peer(p, c):
        for q in range(CAP):
            g = jnp.maximum(ids[p, q], 0)
            out[p, q * COLS : (q + 1) * COLS, :] = blocks[g]
        return c

    lax.fori_loop(0, PEERS, peer, 0, unroll=2)


def start_values(ids, gathered, basis):
    return pl.pallas_call(
        start_kernel,
        out_shape=(
            jax.ShapeDtypeStruct((COLS, OB * BLK), F32),
            pltpu.VMEM((PEERS, SLOTROWS, BLK), BF),
        ),
        in_specs=[SMEM, VMEM, VMEM],
        out_specs=[VMEM, VMEM],
        scratch_shapes=[
            pltpu.VMEM((COLS, NB), BF),
            pltpu.VMEM((OB, COLS, BLK), BF),
        ],
        compiler_params=params(8),
        name="start_values",
    )(ids, in_vmem(gathered), in_vmem(basis))


def resid_kernel(ids, received, scale, dual, resid, t0, t1, t2, t3):
    totals = (t0, t1, t2, t3)
    add_slots(received, ids, totals)
    weight = 1.0 / (1.0 + scale[...].astype(F32))
    for b in range(OB):
        resid[:, b * BLK : (b + 1) * BLK] = dual[b] - sum_totals(totals, b) * weight[b : b + 1, :]


def residual(ids, received, scale, dual):
    return pl.pallas_call(
        resid_kernel,
        out_shape=jax.ShapeDtypeStruct((COLS, OB * BLK), F32),
        in_specs=[SMEM] + [VMEM] * 3,
        out_specs=VMEM,
        scratch_shapes=TOTALS,
        compiler_params=params(8),
        name="residual",
    )(ids, in_vmem(received), scale, in_vmem(dual))


def exchange(values):
    return lax.all_to_all(values, "sub", split_axis=0, concat_axis=0, tiled=True)


def per_device(loads, operators, owner, dual_block, scale_index, basis, coarse):
    scale = scale_index.reshape(OB, BLK)
    packed, pos, ops_v = first_apply(owner.reshape(NBLK), dual_block, loads, operators)
    received = exchange(packed)
    dual, partial, ids = project(received, scale, basis, coarse)
    gathered = exchange(reduce_parts(exchange(partial)))
    start, requested = start_values(ids, gathered, basis)
    again = second_apply(pos, exchange(requested), ops_v)
    return (start, residual(ids, exchange(again), scale, dual))


def solution(mesh):
    return jax.shard_map(
        per_device,
        mesh=mesh,
        in_specs=(
            P("sub", "rep", None),
            P("sub", None, None),
            P("sub", None),
            P("sub"),
            P("sub"),
            P("sub", None),
            P(),
        ),
        out_specs=(P("rep", "sub"), P("rep", "sub")),
        check_vma=False,
    )
```

time: 338 us -> 148 us (0.44)
  blocking collectives: 191 us -> 126 us
  other arithmetic: 37.9 us -> 0 us
  local copies, waits for them, and re-layouts: 36.8 us -> 1.32 us
  waiting for transfers between devices: 26.7 us -> 0 us
  matrix products: 26.1 us -> 0 us
  Pallas kernels: 0 us -> 19.9 us
  starting transfers between devices: 16.2 us -> 0 us
    psum x1 -> x0, blocking collectives: 121 us -> none  [per_device(): summed = lax.psum(coeff, 'sub')]
    all_to_all x2 -> x5, blocking collectives: 70.4 us -> 126 us  [exchange(): lax.all_to_all(values, 'sub', split_axis=0, concat_axis=0, tiled=True)]
    scatter-add x2 -> x0, other arithmetic: 27.1 us -> none  [accumulate(): jnp.zeros((own_blocks, columns, width), jnp.float32).at[got_ids.reshape(-1)]]
    all_to_all x2 -> x0, waiting for transfers between devices: 26.7 us -> none  [the longest x1 26.7 us: per_device(): lax.all_to_all(packed, 'sub', split_axis=0, concat_axis=0, tiled=True)]
    dot_general x4 -> x0, matrix products: 26.1 us -> none  [the longest x2 18.3 us: apply_local(): jnp.einsum('skl,slm->skm', inputs, operators, preferred_element_type=jnp....]
    scatter x3 -> x0, local copies, waits for them, and re-layouts: 24.4 us -> none  [the longest x2 18.7 us: pack_slots(): jnp.zeros((peers, slots, columns, width), jnp.bfloat16).at[dests, ranks]]
    pallas_call x0 -> x6, Pallas kernels: none -> 19.9 us  [the longest x1 8.08 us: first_apply(): pl.pallas_call(first_kernel, out_shape=(pltpu.VMEM((PEERS, SLOTROWS + IDR...]
    all_to_all x2 -> x0, starting transfers between devices: 16.2 us -> none  [the longest x1 8.59 us: per_device(): lax.all_to_all(id_slots, 'sub', split_axis=0, concat_axis=0, tiled=True)]
  transfers between devices with their start and end apart: 2 -> 0, of which waited for: 1 -> 0; matrix products, arithmetic and copies ran while one was open for 6% -> 0% of each run, Pallas kernels for 0% -> 0%
where the time goes in v2:
time: 148 us
  blocking collectives  126 us (85%)
  Pallas kernels  19.9 us (13%)
    all_to_all x5, blocking collectives, exchange(): lax.all_to_all(values, 'sub', split_axis=0, concat_axis=0, tiled=True)  126 us
    pallas_call x1, Pallas kernels, first_apply(): pl.pallas_call(first_kernel, out_shape=(pltpu.VMEM((PEERS, SLOTROWS + IDR...  8.08 us
    pallas_call x1, Pallas kernels, second_apply(): pl.pallas_call(second_kernel, out_shape=pltpu.VMEM((PEERS, SLOTROWS, BLK)...  3.61 us
    pallas_call x1, Pallas kernels, start_values(): pl.pallas_call(start_kernel, out_shape=(jax.ShapeDtypeStruct((COLS, OB *...  3.25 us

profile of v2, /device:TPU:1, one launch (start us, length us, event | category | flops | bytes accessed | tf_op | source)
XLA Modules:
  0.0 147.5 jit_solution(9306960522298103777)
XLA Ops:
  0.6 0.0 copy-start.3
  0.6 0.6 copy-done.3
  1.3 0.0 copy-start.4
  1.3 0.7 copy-done.4
  1.9 0.0 copy-start.1
  1.9 8.1 %first_apply.1 = (bf16[32,264,128]{2,1,0:T(8,128)(2,1)S(1)}, s32[64]{0:T(128)S(1)}, bf16[8,1024,1024]{2,1,0:T(8,128)(2,1)S(1)}) custom-call(s32[64]{0:T(128)S(1)} %bitcast.4, s32[64]{0:T(128)S(1)} %copy-done.4, bf16[8,64,1024]{2,1,0:T(8,128)(2,1)} %loads.1, bf16[8,1024,1024]{2,1,0:T(8,128)(2,1)} %ops.1), custom_call_target="tpu_custom_call" | custom-call | tf_op jit(solution)/shard_map/first_apply/pallas_call | solution.py:83
  10.0 0.0 copy-start
  10.0 0.0 copy-start.2
  10.1 38.3 %all_to_all.25.received = bf16[32,264,128]{2,1,0:T(8,128)(2,1)S(1)} all-to-all(bf16[32,264,128]{2,1,0:T(8,128)(2,1)S(1)} %get-tuple-element.10), channel_id=1, replica_groups=mesh['sub'=32,'rep'=4] {'sub'}, dimensions={0} | all-to-all | bytes 4325376 | tf_op jit(solution)/shard_map/all_to_all | solution.py:268
  48.4 0.0 copy-done.1
  48.4 0.0 copy-done
  48.4 0.0 copy-done.2
  48.4 2.7 %project.1 = (f32[16,64,128]{2,1,0:T(8,128)S(1)}, f32[32,8,256]{2,1,0:T(8,128)S(1)}, s32[32,128]{1,0:T(8,128)S(1)}) custom-call(bf16[32,264,128]{2,1,0:T(8,128)(2,1)S(1)} %all_to_all.25.received, s32[16,128]{1,0:T(8,128)S(1)} %bitcast.2, bf16[2048,1024]{1,0:T(8,128)(2,1)S(1)} %copy-done, bf16[1024,1024]{1,0:T(8,128)(2,1)S(1)} %copy-done.1), custom_call_target="tpu_custom_call" | custom-call | tf_op jit(solution)/shard_map/project/pallas_call | solution.py:170
  51.0 12.5 %all_to_all.26.parts = f32[32,8,256]{2,1,0:T(8,128)S(1)} all-to-all(f32[32,8,256]{2,1,0:T(8,128)S(1)} %get-tuple-element.12), channel_id=1, replica_groups=mesh['sub'=32,'rep'=4] {'sub'}, dimensions={0} | all-to-all | bytes 524288 | tf_op jit(solution)/shard_map/all_to_all | solution.py:268
  63.6 11.2 %all_to_all.27.gathered = bf16[32,8,256]{2,1,0:T(8,128)(2,1)S(1)} all-to-all(bf16[32,8,256]{2,1,0:T(8,128)(2,1)S(1)} %reduce_parts.1), channel_id=1, replica_groups=mesh['sub'=32,'rep'=4] {'sub'}, dimensions={0} | all-to-all | bytes 262144 | tf_op jit(solution)/shard_map/all_to_all | solution.py:268
  74.8 3.2 %start_values.1 = (f32[64,2048]{1,0:T(8,128)}, bf16[32,256,128]{2,1,0:T(8,128)(2,1)S(1)}) custom-call(s32[32,128]{1,0:T(8,128)S(1)} %get-tuple-element.11.ids, bf16[32,8,256]{2,1,0:T(8,128)(2,1)S(1)} %all_to_all.27.gathered, bf16[2048,1024]{1,0:T(8,128)(2,1)S(1)} %copy-done), custom_call_target="tpu_custom_call" | custom-call | tf_op jit(solution)/shard_map/start_values/pallas_call | solution.py:230
  78.0 31.7 %all_to_all.28.back = bf16[32,256,128]{2,1,0:T(8,128)(2,1)S(1)} all-to-all(bf16[32,256,128]{2,1,0:T(8,128)(2,1)S(1)} %get-tuple-element.15), channel_id=1, replica_groups=mesh['sub'=32,'rep'=4] {'sub'}, dimensions={0} | all-to-all | bytes 4194304 | tf_op jit(solution)/shard_map/all_to_all | solution.py:268
  109.7 3.6 %second_apply.1 = bf16[32,256,128]{2,1,0:T(8,128)(2,1)S(1)} custom-call(s32[64]{0:T(128)S(1)} %get-tuple-element.14.pos, bf16[32,256,128]{2,1,0:T(8,128)(2,1)S(1)} %all_to_all.28.back, bf16[8,1024,1024]{2,1,0:T(8,128)(2,1)S(1)} %get-tuple-element.16.ops), custom_call_target="tpu_custom_call" | custom-call | tf_op jit(solution)/shard_map/second_apply/pallas_call | solution.py:114
  113.3 31.9 %all_to_all.29.received = bf16[32,256,128]{2,1,0:T(8,128)(2,1)S(1)} all-to-all(bf16[32,256,128]{2,1,0:T(8,128)(2,1)S(1)} %second_apply.1), channel_id=1, replica_groups=mesh['sub'=32,'rep'=4] {'sub'}, dimensions={0} | all-to-all | bytes 4194304 | tf_op jit(solution)/shard_map/all_to_all | solution.py:268
  145.2 2.3 %residual.1 = f32[64,2048]{1,0:T(8,128)} custom-call(s32[32,128]{1,0:T(8,128)S(1)} %get-tuple-element.11.ids, bf16[32,256,128]{2,1,0:T(8,128)(2,1)S(1)} %all_to_all.29.received, s32[16,128]{1,0:T(8,128)S(1)} %bitcast.3, f32[16,64,128]{2,1,0:T(8,128)S(1)} %get-tuple-element.17.dual), custom_call_target="tpu_custom_call" | custom-call | tf_op jit(solution)/shard_map/residual/pallas_call | solution.py:256
  (1 shorter events, 0.0 us)
Async XLA Ops:
  0.6 0.7 copy-start.3
  1.3 0.7 copy-start.4
  1.9 46.4 %copy-start.1 = (bf16[1024,1024]{1,0:T(8,128)(2,1)S(1)}, bf16[1024,1024]{1,0:T(8,128)(2,1)}, u32[]{:S(2)}) copy-start(bf16[1024,1024]{1,0:T(8,128)(2,1)} %coarse.1) | copy-start | bytes 6291460
  10.0 38.3 %copy-start = (bf16[2048,1024]{1,0:T(8,128)(2,1)S(1)}, bf16[2048,1024]{1,0:T(8,128)(2,1)}, u32[]{:S(2)}) copy-start(bf16[2048,1024]{1,0:T(8,128)(2,1)} %basis.3) | copy-start | bytes 12582916
  10.0 38.3 %copy-start.2 = (s32[2048]{0:T(1024)S(1)}, s32[2048]{0:T(1024)}, u32[]{:S(2)}) copy-start(s32[2048]{0:T(1024)} %param.11) | copy-start | bytes 24580

commit v3 on v2

--- a/solution.py
+++ b/solution.py
@@ -9,6 +9,7 @@
 PEERS = 32
 CAP = 4
 COLS = 64
+HALF = COLS // 2
 L = 1024
 BPS = 8
 NSUB = 8
@@ -41,7 +42,11 @@
     return ref.at[p // CAP, pl.ds(pl.multiple_of((p % CAP) * COLS, COLS), COLS)]
 
 
-def first_kernel(owner, dual_block, loads, ops, out, pos, ops_v, count, loads_v, sem, load_sem):
+def first_kernel(owner_h, block_h, loads, ops, out, pos, ops_v, owner, dual_block, count, loads_v, sem, load_sem, idx_sem):
+    owner_copy = pltpu.make_async_copy(owner_h, owner, idx_sem.at[0])
+    block_copy = pltpu.make_async_copy(block_h, dual_block, idx_sem.at[1])
+    owner_copy.start()
+    block_copy.start()
     load_copy = pltpu.make_async_copy(loads, loads_v, load_sem)
     copies = [pltpu.make_async_copy(ops.at[s], ops_v.at[s], sem.at[s]) for s in range(NSUB)]
     load_copy.start()
@@ -53,6 +58,8 @@
         return c
 
     lax.fori_loop(0, PEERS, zero, 0)
+    owner_copy.wait()
+    block_copy.wait()
     row = lax.broadcasted_iota(jnp.int32, (PEERS, BLK), 0)
     lane = lax.broadcasted_iota(jnp.int32, (PEERS, BLK), 1)
     flat = jnp.where(lane < CAP, row * CAP + lane, -1)
@@ -87,17 +94,20 @@
             jax.ShapeDtypeStruct((NBLK,), jnp.int32),
             pltpu.VMEM((NSUB, L, L), BF),
         ),
-        in_specs=[SMEM, SMEM, HBM, HBM],
+        in_specs=[HBM] * 4,
         out_specs=[VMEM, SMEM, VMEM],
         scratch_shapes=[
+            pltpu.SMEM((NBLK,), jnp.int32),
+            pltpu.SMEM((NBLK,), jnp.int32),
             pltpu.SMEM((PEERS,), jnp.int32),
             pltpu.VMEM((NSUB, COLS, L), BF),
             pltpu.SemaphoreType.DMA((NSUB,)),
             pltpu.SemaphoreType.DMA,
+            pltpu.SemaphoreType.DMA((2,)),
         ],
         compiler_params=params(8),
         name="first_apply",
-    )(owner, dual_block, in_hbm(loads), in_hbm(operators))
+    )(in_hbm(owner), in_hbm(dual_block), in_hbm(loads), in_hbm(operators))
 
 
 def second_kernel(pos, back, ops, out, local):
@@ -143,7 +153,7 @@
 TOTALS = [pltpu.VMEM((OB + 1, COLS, BLK), F32)] * CAP
 
 
-def project_kernel(received, scale, basis, coarse, dual, partial, ids_out, t0, t1, t2, t3, narrow, idv, ids, sem):
+def project_kernel(received, scale, basis, coarse, dual, keep, send, ids_out, t0, t1, t2, t3, narrow, solved, idv, ids, sem):
     totals = (t0, t1, t2, t3)
     idv[...] = received[:, SLOTROWS : SLOTROWS + IDROWS, :].astype(F32)[:, 0, :].astype(jnp.int32)
     ids_copy = pltpu.make_async_copy(idv, ids, sem)
@@ -160,10 +170,11 @@
     high = coeff.astype(BF)
     low = (coeff - high.astype(F32)).astype(BF)
     both = jnp.dot(jnp.concatenate([high, low], axis=0), coarse[...], preferred_element_type=F32)
-    solved = both[:COLS] + both[COLS:]
-    for a in range(8):
-        for b in range(4):
-            partial[a * 4 + b] = solved[a * 8 : (a + 1) * 8, b * 256 : (b + 1) * 256]
+    solved[0] = both[:HALF] + both[COLS : COLS + HALF]
+    solved[1] = both[HALF:COLS] + both[COLS + HALF :]
+    core = lax.axis_index("sub") % 2
+    keep[...] = solved[core]
+    send[...] = solved[1 - core]
 
 
 def project(received, scale, basis, coarse):
@@ -171,14 +182,16 @@
         project_kernel,
         out_shape=(
             pltpu.VMEM((OB, COLS, BLK), F32),
-            pltpu.VMEM((PEERS, 8, 256), F32),
+            pltpu.VMEM((HALF, NB), F32),
+            pltpu.VMEM((HALF, NB), F32),
             jax.ShapeDtypeStruct((PEERS, BLK), jnp.int32),
         ),
         in_specs=[VMEM] * 4,
-        out_specs=[VMEM] * 3,
+        out_specs=[VMEM] * 4,
         scratch_shapes=TOTALS
         + [
             pltpu.VMEM((COLS, OB * BLK), BF),
+            pltpu.VMEM((2, HALF, NB), F32),
             pltpu.VMEM((PEERS, BLK), jnp.int32),
             pltpu.SMEM((PEERS, BLK), jnp.int32),
             pltpu.SemaphoreType.DMA,
@@ -188,30 +201,46 @@
     )(in_vmem(received), scale, in_vmem(basis), in_vmem(coarse))
 
 
-def reduce_kernel(parts, out):
-    total = parts[0]
-    for p in range(1, PEERS):
-        total = total + parts[p]
-    out[...] = jnp.broadcast_to(total.astype(BF)[None], out.shape)
-
-
-def reduce_parts(parts):
-    return pl.pallas_call(
-        reduce_kernel,
-        out_shape=pltpu.VMEM((PEERS, 8, 256), BF),
-        in_specs=[VMEM],
-        out_specs=VMEM,
+def add_kernel(own, *refs):
+    total = own[...]
+    for other in refs[:-2]:
+        total = total + other[...].astype(F32)
+    refs[-2][...] = total
+    refs[-1][...] = total.astype(BF)
+
+
+def add_parts(own, others):
+    return pl.pallas_call(
+        add_kernel,
+        out_shape=(pltpu.VMEM((HALF, NB), F32), pltpu.VMEM((HALF, NB), BF)),
+        in_specs=[VMEM] * (1 + len(others)),
+        out_specs=[VMEM] * 2,
         compiler_params=params(4),
-        name="reduce_parts",
-    )(in_vmem(parts))
-
-
-def start_kernel(ids, gathered, basis, start, out, solved, blocks):
-    for a in range(8):
-        for b in range(4):
-            solved[a * 8 : (a + 1) * 8, b * 256 : (b + 1) * 256] = gathered[a * 4 + b]
+        name="add_parts",
+    )(in_vmem(own), *[in_vmem(o) for o in others])
+
+
+def shifted(values, dx, dy, dc):
+    pairs = []
+    for i in range(PEERS):
+        x, y, c = i // 8, i // 2 % 4, i % 2
+        pairs.append((i, (x + dx) % 4 * 8 + (y + dy) % 4 * 2 + (c + dc) % 2))
+    return lax.ppermute(values, "sub", pairs)
+
+
+def sum_over_owners(keep, send):
+    total, narrow = add_parts(keep, [shifted(send, 0, 0, 1)])
+    total, narrow = add_parts(total, [shifted(narrow, k, 0, 0) for k in (2, 1, 3)])
+    total, narrow = add_parts(total, [shifted(narrow, 0, k, 0) for k in (2, 1, 3)])
+    return narrow, shifted(narrow, 0, 0, 1)
+
+
+def start_kernel(ids, own, other, basis, start, out, solved, blocks):
+    core = lax.axis_index("sub") % 2
+    solved[core] = own[...]
+    solved[1 - core] = other[...]
     value = lax.dot_general(
-        solved[...], basis[...], (((1,), (1,)), ((), ())), preferred_element_type=F32
+        solved[...].reshape(COLS, NB), basis[...], (((1,), (1,)), ((), ())), preferred_element_type=F32
     )
     start[...] = value
     for k in range(OB):
@@ -226,22 +255,22 @@
     lax.fori_loop(0, PEERS, peer, 0, unroll=2)
 
 
-def start_values(ids, gathered, basis):
+def start_values(ids, own, other, basis):
     return pl.pallas_call(
         start_kernel,
         out_shape=(
             jax.ShapeDtypeStruct((COLS, OB * BLK), F32),
             pltpu.VMEM((PEERS, SLOTROWS, BLK), BF),
         ),
-        in_specs=[SMEM, VMEM, VMEM],
+        in_specs=[SMEM, VMEM, VMEM, VMEM],
         out_specs=[VMEM, VMEM],
         scratch_shapes=[
-            pltpu.VMEM((COLS, NB), BF),
+            pltpu.VMEM((2, HALF, NB), BF),
             pltpu.VMEM((OB, COLS, BLK), BF),
         ],
         compiler_params=params(8),
         name="start_values",
-    )(ids, in_vmem(gathered), in_vmem(basis))
+    )(ids, in_vmem(own), in_vmem(other), in_vmem(basis))
 
 
 def resid_kernel(ids, received, scale, dual, resid, t0, t1, t2, t3):
@@ -272,9 +301,9 @@
     scale = scale_index.reshape(OB, BLK)
     packed, pos, ops_v = first_apply(owner.reshape(NBLK), dual_block, loads, operators)
     received = exchange(packed)
-    dual, partial, ids = project(received, scale, basis, coarse)
-    gathered = exchange(reduce_parts(exchange(partial)))
-    start, requested = start_values(ids, gathered, basis)
+    dual, keep, send, ids = project(received, scale, basis, coarse)
+    own, other = sum_over_owners(keep, send)
+    start, requested = start_values(ids, own, other, basis)
     again = second_apply(pos, exchange(requested), ops_v)
     return (start, residual(ids, exchange(again), scale, dual))
 

time: 148 us -> 144 us (0.973)
  blocking collectives: 126 us -> 104 us
  waiting for transfers between devices: 0 us -> 9.59 us
  starting transfers between devices: 0 us -> 8.89 us
    all_to_all x5 -> x3, blocking collectives: 126 us -> 104 us  [exchange(): lax.all_to_all(values, 'sub', split_axis=0, concat_axis=0, tiled=True)]
    ppermute x0 -> x8, waiting for transfers between devices: none -> 9.59 us  [shifted(): return lax.ppermute(values, 'sub', pairs)]
    ppermute x0 -> x8, starting transfers between devices: none -> 8.89 us  [shifted(): return lax.ppermute(values, 'sub', pairs)]
  transfers between devices with their start and end apart: 0 -> 8, of which waited for: 0 -> 8; matrix products, arithmetic and copies ran while one was open for 0% -> 0% of each run, Pallas kernels for 0% -> 0%
where the time goes in v3:
time: 144 us; the launch traced here: 143 us
  blocking collectives  104 us (72%)
  Pallas kernels  20.2 us (14%)
  waiting for transfers between devices  9.59 us (7%)
  starting transfers between devices  8.89 us (6%)
    all_to_all x3, blocking collectives, exchange(): lax.all_to_all(values, 'sub', split_axis=0, concat_axis=0, tiled=True)  104 us
    ppermute x8, waiting for transfers between devices, shifted(): return lax.ppermute(values, 'sub', pairs)  9.59 us
    ppermute x8, starting transfers between devices, shifted(): return lax.ppermute(values, 'sub', pairs)  8.89 us
    pallas_call x1, Pallas kernels, first_apply(): pl.pallas_call(first_kernel, out_shape=(pltpu.VMEM((PEERS, SLOTROWS + IDR...  7.65 us
    pallas_call x1, Pallas kernels, second_apply(): pl.pallas_call(second_kernel, out_shape=pltpu.VMEM((PEERS, SLOTROWS, BLK)...  3.61 us
    pallas_call x1, Pallas kernels, start_values(): pl.pallas_call(start_kernel, out_shape=(jax.ShapeDtypeStruct((COLS, OB *...  3.25 us
  transfers between devices with their start and end apart: 8, of which 8 were waited for; matrix products, arithmetic and copies ran while one was open for 0% of the time, Pallas kernels for 0%

profile of v3, /device:TPU:1, one launch (start us, length us, event | category | flops | bytes accessed | tf_op | source)
XLA Modules:
  0.0 143.5 jit_solution(13381745505270232802)
XLA Ops:
  0.6 0.0 copy-start.1
  0.6 7.6 %first_apply.1 = (bf16[32,264,128]{2,1,0:T(8,128)(2,1)S(1)}, s32[64]{0:T(128)S(1)}, bf16[8,1024,1024]{2,1,0:T(8,128)(2,1)S(1)}) custom-call(s32[64]{0:T(128)} %bitcast.4, s32[64]{0:T(128)} %block_h.1, bf16[8,64,1024]{2,1,0:T(8,128)(2,1)} %loads.1, bf16[8,1024,1024]{2,1,0:T(8,128)(2,1)} %ops.1), custom_call_target="tpu_custom_call" | custom-call | tf_op jit(solution)/shard_map/first_apply/pallas_call | solution.py:90
  8.3 0.0 copy-start
  8.3 0.0 copy-start.2
  8.3 38.3 %all_to_all.15.received = bf16[32,264,128]{2,1,0:T(8,128)(2,1)S(1)} all-to-all(bf16[32,264,128]{2,1,0:T(8,128)(2,1)S(1)} %get-tuple-element.16), channel_id=1, replica_groups=mesh['sub'=32,'rep'=4] {'sub'}, dimensions={0} | all-to-all | bytes 4325376 | tf_op jit(solution)/shard_map/all_to_all | solution.py:297
  46.6 0.0 copy-done.1
  46.6 0.0 copy-done
  46.6 0.0 copy-done.2
  46.6 2.7 %project.1 = (f32[16,64,128]{2,1,0:T(8,128)S(1)}, f32[32,1024]{1,0:T(8,128)S(1)}, f32[32,1024]{1,0:T(8,128)S(1)}, s32[32,128]{1,0:T(8,128)S(1)}) custom-call(bf16[32,264,128]{2,1,0:T(8,128)(2,1)S(1)} %all_to_all.15.received, s32[16,128]{1,0:T(8,128)S(1)} %bitcast.2, bf16[2048,1024]{1,0:T(8,128)(2,1)S(1)} %copy-done, bf16[1024,1024]{1,0:T(8,128)(2,1)S(1)} %copy-done.1), custom_call_target="tpu_custom_call" | custom-call | tf_op jit(solution)/shard_map/project/pallas_call | solution.py:181
  49.3 0.5 collective-permute-start
  49.8 1.0 collective-permute-done.refs_0_
  50.8 0.9 collective-permute-start.3
  51.7 0.6 collective-permute-start.2
  52.3 1.0 collective-permute-start.1
  53.3 0.7 collective-permute-done.3.refs_2_
  54.0 2.1 %collective-permute-done.2.refs_1_ = bf16[32,1024]{1,0:T(8,128)(2,1)S(1)} collective-permute-done((bf16[32,1024]{1,0:T(8,128)(2,1)S(1)}, bf16[32,1024]{1,0:T(8,128)(2,1)S(1)}, u32[]{:S(2)}, u32[]{:S(2)}) %collective-permute-start.2) | collective-permute-done | bytes 65568 | tf_op jit(solution)/shard_map/ppermute | solution.py:228
  56.0 1.0 collective-permute-done.1.refs_0_
  57.0 1.0 collective-permute-start.6
  58.0 0.6 collective-permute-start.5
  58.6 0.8 collective-permute-start.4
  59.4 0.9 collective-permute-done.6.refs_2_
  60.2 2.1 %collective-permute-done.5.refs_1_ = bf16[32,1024]{1,0:T(8,128)(2,1)S(1)} collective-permute-done((bf16[32,1024]{1,0:T(8,128)(2,1)S(1)}, bf16[32,1024]{1,0:T(8,128)(2,1)S(1)}, u32[]{:S(2)}, u32[]{:S(2)}) %collective-permute-start.5) | collective-permute-done | bytes 65568 | tf_op jit(solution)/shard_map/ppermute | solution.py:228
  62.3 1.0 collective-permute-done.4.refs_0_
  63.4 0.7 add_parts.5
  64.0 3.6 %collective-permute-start.7 = (bf16[32,1024]{1,0:T(8,128)(2,1)S(1)}, bf16[32,1024]{1,0:T(8,128)(2,1)S(1)}, u32[]{:S(2)}, u32[]{:S(2)}) collective-permute-start(bf16[32,1024]{1,0:T(8,128)(2,1)S(1)} %get-tuple-element.24.own), channel_id=1, source_target_pairs={{0,4},{4,0},{8,12},{12,8},{16,20},{20,16},{24,28},{28,24},{32,36},... | collective-permute-start | bytes 196616 | tf_op jit(solution)/shard_map/ppermute | solution.py:228
  67.6 0.9 collective-permute-done.7.other
  68.5 3.3 %start_values.1 = (f32[64,2048]{1,0:T(8,128)}, bf16[32,256,128]{2,1,0:T(8,128)(2,1)S(1)}) custom-call(s32[32,128]{1,0:T(8,128)S(1)} %get-tuple-element.17.ids, bf16[32,1024]{1,0:T(8,128)(2,1)S(1)} %get-tuple-element.24.own, bf16[32,1024]{1,0:T(8,128)(2,1)S(1)} %collective-permute-done.7.other, bf16[2048,1024]{1,0:T(8,128)(2,1)S(1)} %copy-done), custom_call_target="tpu_custom_call" | custom-call | tf_op jit(solution)/shard_map/start_values/pallas_call | solution.py:259
  71.8 33.9 %all_to_all.16.back = bf16[32,256,128]{2,1,0:T(8,128)(2,1)S(1)} all-to-all(bf16[32,256,128]{2,1,0:T(8,128)(2,1)S(1)} %get-tuple-element.27), channel_id=1, replica_groups=mesh['sub'=32,'rep'=4] {'sub'}, dimensions={0} | all-to-all | bytes 4194304 | tf_op jit(solution)/shard_map/all_to_all | solution.py:297
  105.7 3.6 %second_apply.1 = bf16[32,256,128]{2,1,0:T(8,128)(2,1)S(1)} custom-call(s32[64]{0:T(128)S(1)} %get-tuple-element.26.pos, bf16[32,256,128]{2,1,0:T(8,128)(2,1)S(1)} %all_to_all.16.back, bf16[8,1024,1024]{2,1,0:T(8,128)(2,1)S(1)} %get-tuple-element.28.ops), custom_call_target="tpu_custom_call" | custom-call | tf_op jit(solution)/shard_map/second_apply/pallas_call | solution.py:124
  109.3 31.9 %all_to_all.17.received = bf16[32,256,128]{2,1,0:T(8,128)(2,1)S(1)} all-to-all(bf16[32,256,128]{2,1,0:T(8,128)(2,1)S(1)} %second_apply.1), channel_id=1, replica_groups=mesh['sub'=32,'rep'=4] {'sub'}, dimensions={0} | all-to-all | bytes 4194304 | tf_op jit(solution)/shard_map/all_to_all | solution.py:297
  141.2 2.3 %residual.1 = f32[64,2048]{1,0:T(8,128)} custom-call(s32[32,128]{1,0:T(8,128)S(1)} %get-tuple-element.17.ids, bf16[32,256,128]{2,1,0:T(8,128)(2,1)S(1)} %all_to_all.17.received, s32[16,128]{1,0:T(8,128)S(1)} %bitcast.3, f32[16,64,128]{2,1,0:T(8,128)S(1)} %get-tuple-element.29.dual), custom_call_target="tpu_custom_call" | custom-call | tf_op jit(solution)/shard_map/residual/pallas_call | solution.py:285
  (2 shorter events, 0.1 us)
Async XLA Ops:
  0.6 46.0 %copy-start.1 = (bf16[1024,1024]{1,0:T(8,128)(2,1)S(1)}, bf16[1024,1024]{1,0:T(8,128)(2,1)}, u32[]{:S(2)}) copy-start(bf16[1024,1024]{1,0:T(8,128)(2,1)} %coarse.1) | copy-start | bytes 6291460
  8.3 38.3 %copy-start = (bf16[2048,1024]{1,0:T(8,128)(2,1)S(1)}, bf16[2048,1024]{1,0:T(8,128)(2,1)}, u32[]{:S(2)}) copy-start(bf16[2048,1024]{1,0:T(8,128)(2,1)} %basis.3) | copy-start | bytes 12582916
  8.3 38.3 %copy-start.2 = (s32[2048]{0:T(1024)S(1)}, s32[2048]{0:T(1024)}, u32[]{:S(2)}) copy-start(s32[2048]{0:T(1024)} %param.11) | copy-start | bytes 24580
  49.3 1.5 %collective-permute-start = (f32[32,1024]{1,0:T(8,128)S(1)}, f32[32,1024]{1,0:T(8,128)S(1)}, u32[]{:S(2)}, u32[]{:S(2)}) collective-permute-start(f32[32,1024]{1,0:T(8,128)S(1)} %get-tuple-element.19), channel_id=1, source_target_pairs={{0,4},{4,0},{8,12},{12,8},{16,20},{20,16},{24,28},{28,24},{32,36},... | collective-permute-start | bytes 393224 | tf_op jit(solution)/shard_map/ppermute | solution.py:228
  50.8 3.2 %collective-permute-start.3 = (bf16[32,1024]{1,0:T(8,128)(2,1)S(1)}, bf16[32,1024]{1,0:T(8,128)(2,1)S(1)}, u32[]{:S(2)}, u32[]{:S(2)}) collective-permute-start(bf16[32,1024]{1,0:T(8,128)(2,1)S(1)} %get-tuple-element.21), channel_id=1, source_target_pairs={{0,96},{4,100},{8,104},{12,108},{16,112},{20,116},{24,120},{28,124... | collective-permute-start | bytes 196616 | tf_op jit(solution)/shard_map/ppermute | solution.py:228
  51.7 4.3 %collective-permute-start.2 = (bf16[32,1024]{1,0:T(8,128)(2,1)S(1)}, bf16[32,1024]{1,0:T(8,128)(2,1)S(1)}, u32[]{:S(2)}, u32[]{:S(2)}) collective-permute-start(bf16[32,1024]{1,0:T(8,128)(2,1)S(1)} %get-tuple-element.21), channel_id=1, source_target_pairs={{0,32},{4,36},{8,40},{12,44},{16,48},{20,52},{24,56},{28,60},{32,6... | collective-permute-start | bytes 196616 | tf_op jit(solution)/shard_map/ppermute | solution.py:228
  52.3 4.7 %collective-permute-start.1 = (bf16[32,1024]{1,0:T(8,128)(2,1)S(1)}, bf16[32,1024]{1,0:T(8,128)(2,1)S(1)}, u32[]{:S(2)}, u32[]{:S(2)}) collective-permute-start(bf16[32,1024]{1,0:T(8,128)(2,1)S(1)} %get-tuple-element.21), channel_id=1, source_target_pairs={{0,64},{4,68},{8,72},{12,76},{16,80},{20,84},{24,88},{28,92},{32,9... | collective-permute-start | bytes 196616 | tf_op jit(solution)/shard_map/ppermute | solution.py:228
  57.0 3.2 %collective-permute-start.6 = (bf16[32,1024]{1,0:T(8,128)(2,1)S(1)}, bf16[32,1024]{1,0:T(8,128)(2,1)S(1)}, u32[]{:S(2)}, u32[]{:S(2)}) collective-permute-start(bf16[32,1024]{1,0:T(8,128)(2,1)S(1)} %get-tuple-element.23), channel_id=1, source_target_pairs={{0,24},{4,28},{8,0},{12,4},{16,8},{20,12},{24,16},{28,20},{32,56},... | collective-permute-start | bytes 196616 | tf_op jit(solution)/shard_map/ppermute | solution.py:228
  58.0 4.3 %collective-permute-start.5 = (bf16[32,1024]{1,0:T(8,128)(2,1)S(1)}, bf16[32,1024]{1,0:T(8,128)(2,1)S(1)}, u32[]{:S(2)}, u32[]{:S(2)}) collective-permute-start(bf16[32,1024]{1,0:T(8,128)(2,1)S(1)} %get-tuple-element.23), channel_id=1, source_target_pairs={{0,8},{4,12},{8,16},{12,20},{16,24},{20,28},{24,0},{28,4},{32,40},... | collective-permute-start | bytes 196616 | tf_op jit(solution)/shard_map/ppermute | solution.py:228
  58.6 4.8 %collective-permute-start.4 = (bf16[32,1024]{1,0:T(8,128)(2,1)S(1)}, bf16[32,1024]{1,0:T(8,128)(2,1)S(1)}, u32[]{:S(2)}, u32[]{:S(2)}) collective-permute-start(bf16[32,1024]{1,0:T(8,128)(2,1)S(1)} %get-tuple-element.23), channel_id=1, source_target_pairs={{0,16},{4,20},{8,24},{12,28},{16,0},{20,4},{24,8},{28,12},{32,48},... | collective-permute-start | bytes 196616 | tf_op jit(solution)/shard_map/ppermute | solution.py:228
  64.0 4.5 %collective-permute-start.7 = (bf16[32,1024]{1,0:T(8,128)(2,1)S(1)}, bf16[32,1024]{1,0:T(8,128)(2,1)S(1)}, u32[]{:S(2)}, u32[]{:S(2)}) collective-permute-start(bf16[32,1024]{1,0:T(8,128)(2,1)S(1)} %get-tuple-element.24.own), channel_id=1, source_target_pairs={{0,4},{4,0},{8,12},{12,8},{16,20},{20,16},{24,28},{28,24},{32,36},... | collective-permute-start | bytes 196616 | tf_op jit(solution)/shard_map/ppermute | solution.py:228

commit v4 on v3

--- a/solution.py
+++ b/solution.py
@@ -1,3 +1,5 @@
+import functools
+
 import jax
 import jax.numpy as jnp
 from jax import lax
@@ -15,6 +17,7 @@
 NSUB = 8
 NBLK = NSUB * BPS
 OB = 16
+MERGE = OB * BLK // 2
 NB = 1024
 IDROWS = 8
 SLOTROWS = CAP * COLS
@@ -132,6 +135,25 @@
     )(pos, in_vmem(back), in_vmem(operators))
 
 
+def merge_kernel(part, coarse, basis, after, merged):
+    for k in range(4):
+        rows = slice(part * MERGE + k * 256, part * MERGE + (k + 1) * 256)
+        merged[:, k * 256 : (k + 1) * 256] = lax.dot_general(
+            coarse[...], basis[rows, :], (((1,), (1,)), ((), ())), preferred_element_type=F32
+        ).astype(BF)
+
+
+def merge(part, coarse, basis, after):
+    return pl.pallas_call(
+        functools.partial(merge_kernel, part),
+        out_shape=pltpu.VMEM((NB, MERGE), BF),
+        in_specs=[VMEM] * 3,
+        out_specs=VMEM,
+        compiler_params=params(6),
+        name="merge",
+    )(in_vmem(coarse), in_vmem(basis), in_vmem(after))
+
+
 def add_slots(received, ids, totals):
     for q in range(CAP):
         totals[q][...] = jnp.zeros(totals[q].shape, F32)
@@ -153,7 +175,9 @@
 TOTALS = [pltpu.VMEM((OB + 1, COLS, BLK), F32)] * CAP
 
 
-def project_kernel(received, scale, basis, coarse, dual, keep, send, ids_out, t0, t1, t2, t3, narrow, solved, idv, ids, sem):
+def project_kernel(received, scale, basis, coarse, dual, keep, send, ids_out, coarse_v, t0, t1, t2, t3, narrow, coeff, idv, ids, sem, coarse_sem):
+    coarse_copy = pltpu.make_async_copy(coarse, coarse_v, coarse_sem)
+    coarse_copy.start()
     totals = (t0, t1, t2, t3)
     idv[...] = received[:, SLOTROWS : SLOTROWS + IDROWS, :].astype(F32)[:, 0, :].astype(jnp.int32)
     ids_copy = pltpu.make_async_copy(idv, ids, sem)
@@ -166,15 +190,13 @@
         owned = sum_totals(totals, b) * weight[b : b + 1, :]
         dual[b] = owned
         narrow[:, b * BLK : (b + 1) * BLK] = owned.astype(BF)
-    coeff = jnp.dot(narrow[...], basis[...], preferred_element_type=F32)
-    high = coeff.astype(BF)
-    low = (coeff - high.astype(F32)).astype(BF)
-    both = jnp.dot(jnp.concatenate([high, low], axis=0), coarse[...], preferred_element_type=F32)
-    solved[0] = both[:HALF] + both[COLS : COLS + HALF]
-    solved[1] = both[HALF:COLS] + both[COLS + HALF :]
+    product = jnp.dot(narrow[...], basis[...], preferred_element_type=F32)
+    coeff[0] = product[:HALF]
+    coeff[1] = product[HALF:]
     core = lax.axis_index("sub") % 2
-    keep[...] = solved[core]
-    send[...] = solved[1 - core]
+    keep[...] = coeff[core]
+    send[...] = coeff[1 - core]
+    coarse_copy.wait()
 
 
 def project(received, scale, basis, coarse):
@@ -185,9 +207,10 @@
             pltpu.VMEM((HALF, NB), F32),
             pltpu.VMEM((HALF, NB), F32),
             jax.ShapeDtypeStruct((PEERS, BLK), jnp.int32),
+            pltpu.VMEM((NB, NB), BF),
         ),
-        in_specs=[VMEM] * 4,
-        out_specs=[VMEM] * 4,
+        in_specs=[VMEM] * 3 + [HBM],
+        out_specs=[VMEM] * 5,
         scratch_shapes=TOTALS
         + [
             pltpu.VMEM((COLS, OB * BLK), BF),
@@ -195,29 +218,32 @@
             pltpu.VMEM((PEERS, BLK), jnp.int32),
             pltpu.SMEM((PEERS, BLK), jnp.int32),
             pltpu.SemaphoreType.DMA,
+            pltpu.SemaphoreType.DMA,
         ],
         compiler_params=params(8),
         name="project",
-    )(in_vmem(received), scale, in_vmem(basis), in_vmem(coarse))
-
-
-def add_kernel(own, *refs):
-    total = own[...]
-    for other in refs[:-2]:
+    )(in_vmem(received), scale, in_vmem(basis), in_hbm(coarse))
+
+
+def add_kernel(count, inputs, *refs):
+    total = refs[0][...]
+    for other in refs[1:count]:
         total = total + other[...].astype(F32)
-    refs[-2][...] = total
-    refs[-1][...] = total.astype(BF)
-
-
-def add_parts(own, others):
-    return pl.pallas_call(
-        add_kernel,
-        out_shape=(pltpu.VMEM((HALF, NB), F32), pltpu.VMEM((HALF, NB), BF)),
-        in_specs=[VMEM] * (1 + len(others)),
-        out_specs=[VMEM] * 2,
+    for out in refs[inputs:]:
+        out[...] = total.astype(out.dtype)
+
+
+def add_parts(own, others, types, after=()):
+    count = 1 + len(others)
+    inputs = count + len(after)
+    return pl.pallas_call(
+        functools.partial(add_kernel, count, inputs),
+        out_shape=[pltpu.VMEM((HALF, NB), t) for t in types],
+        in_specs=[VMEM] * inputs,
+        out_specs=[VMEM] * len(types),
         compiler_params=params(4),
         name="add_parts",
-    )(in_vmem(own), *[in_vmem(o) for o in others])
+    )(in_vmem(own), *[in_vmem(o) for o in (*others, *after)])
 
 
 def shifted(values, dx, dy, dc):
@@ -228,23 +254,27 @@
     return lax.ppermute(values, "sub", pairs)
 
 
-def sum_over_owners(keep, send):
-    total, narrow = add_parts(keep, [shifted(send, 0, 0, 1)])
-    total, narrow = add_parts(total, [shifted(narrow, k, 0, 0) for k in (2, 1, 3)])
-    total, narrow = add_parts(total, [shifted(narrow, 0, k, 0) for k in (2, 1, 3)])
-    return narrow, shifted(narrow, 0, 0, 1)
-
-
-def start_kernel(ids, own, other, basis, start, out, solved, blocks):
+def sum_over_owners(keep, send, coarse, basis):
+    both = (F32, BF)
+    total, narrow = add_parts(keep, [shifted(send, 0, 0, 1)], both)
+    first = merge(0, coarse, basis, narrow)
+    others = [shifted(narrow, k, 0, 0) for k in (3, 1, 2)]
+    total, narrow = add_parts(total, others, both, (first,))
+    second = merge(1, coarse, basis, narrow)
+    others = [shifted(narrow, 0, k, 0) for k in (3, 1, 2)]
+    (narrow,) = add_parts(total, others, (BF,), (second,))
+    return narrow, shifted(narrow, 0, 0, 1), first, second
+
+
+def start_kernel(ids, own, other, first, second, start, out, coeff, blocks):
     core = lax.axis_index("sub") % 2
-    solved[core] = own[...]
-    solved[1 - core] = other[...]
-    value = lax.dot_general(
-        solved[...].reshape(COLS, NB), basis[...], (((1,), (1,)), ((), ())), preferred_element_type=F32
-    )
-    start[...] = value
-    for k in range(OB):
-        blocks[k] = value[:, k * BLK : (k + 1) * BLK].astype(BF)
+    coeff[core] = own[...]
+    coeff[1 - core] = other[...]
+    for part, merged in enumerate((first, second)):
+        value = jnp.dot(coeff[...].reshape(COLS, NB), merged[...], preferred_element_type=F32)
+        start[:, part * MERGE : (part + 1) * MERGE] = value
+        for k in range(MERGE // BLK):
+            blocks[part * (MERGE // BLK) + k] = value[:, k * BLK : (k + 1) * BLK].astype(BF)
 
     def peer(p, c):
         for q in range(CAP):
@@ -255,14 +285,14 @@
     lax.fori_loop(0, PEERS, peer, 0, unroll=2)
 
 
-def start_values(ids, own, other, basis):
+def start_values(ids, own, other, first, second):
     return pl.pallas_call(
         start_kernel,
         out_shape=(
             jax.ShapeDtypeStruct((COLS, OB * BLK), F32),
             pltpu.VMEM((PEERS, SLOTROWS, BLK), BF),
         ),
-        in_specs=[SMEM, VMEM, VMEM, VMEM],
+        in_specs=[SMEM] + [VMEM] * 4,
         out_specs=[VMEM, VMEM],
         scratch_shapes=[
             pltpu.VMEM((2, HALF, NB), BF),
@@ -270,7 +300,7 @@
         ],
         compiler_params=params(8),
         name="start_values",
-    )(ids, in_vmem(own), in_vmem(other), in_vmem(basis))
+    )(ids, in_vmem(own), in_vmem(other), in_vmem(first), in_vmem(second))
 
 
 def resid_kernel(ids, received, scale, dual, resid, t0, t1, t2, t3):
@@ -301,9 +331,9 @@
     scale = scale_index.reshape(OB, BLK)
     packed, pos, ops_v = first_apply(owner.reshape(NBLK), dual_block, loads, operators)
     received = exchange(packed)
-    dual, keep, send, ids = project(received, scale, basis, coarse)
-    own, other = sum_over_owners(keep, send)
-    start, requested = start_values(ids, own, other, basis)
+    dual, keep, send, ids, coarse_v = project(received, scale, basis, coarse)
+    own, other, first, second = sum_over_owners(keep, send, coarse_v, basis)
+    start, requested = start_values(ids, own, other, first, second)
     again = second_apply(pos, exchange(requested), ops_v)
     return (start, residual(ids, exchange(again), scale, dual))
 

time: 144 us -> 142 us (0.986)
  waiting for transfers between devices: 9.59 us -> 2.33 us
  Pallas kernels: 20.2 us -> 23.3 us
    ppermute x8, waiting for transfers between devices: 9.59 us -> 2.33 us  [shifted(): return lax.ppermute(values, 'sub', pairs)]
    pallas_call x3 -> x5, Pallas kernels: 0.74 us -> 4.82 us  [the longest x2 4.74 us: merge(): pl.pallas_call(functools.partial(merge_kernel, part), out_shape=pltpu.VME...]
  transfers between devices with their start and end apart: 8 -> 8, of which waited for: 8 -> 3; matrix products, arithmetic and copies ran while one was open for 0% -> 0% of each run, Pallas kernels for 0% -> 3%
where the time goes in v4:
time: 142 us; the launch traced here: 141 us
  blocking collectives  105 us (74%)
  Pallas kernels  23.3 us (16%)
  starting transfers between devices  9.62 us (7%)
  waiting for transfers between devices  2.33 us (2%)
    all_to_all x3, blocking collectives, exchange(): lax.all_to_all(values, 'sub', split_axis=0, concat_axis=0, tiled=True)  105 us
    ppermute x8, starting transfers between devices, shifted(): return lax.ppermute(values, 'sub', pairs)  9.62 us
    pallas_call x1, Pallas kernels, first_apply(): pl.pallas_call(first_kernel, out_shape=(pltpu.VMEM((PEERS, SLOTROWS + IDR...  7.47 us
    pallas_call x2, Pallas kernels, merge(): pl.pallas_call(functools.partial(merge_kernel, part), out_shape=pltpu.VME...  4.74 us
    pallas_call x1, Pallas kernels, second_apply(): pl.pallas_call(second_kernel, out_shape=pltpu.VMEM((PEERS, SLOTROWS, BLK)...  3.61 us
  transfers between devices with their start and end apart: 8, of which 3 were waited for; matrix products, arithmetic and copies ran while one was open for 0% of the time, Pallas kernels for 3%

profile of v4, /device:TPU:1, one launch (start us, length us, event | category | flops | bytes accessed | tf_op | source)
XLA Modules:
  0.0 141.3 jit_solution(2483026932978903483)
XLA Ops:
  0.6 7.5 %first_apply.1 = (bf16[32,264,128]{2,1,0:T(8,128)(2,1)S(1)}, s32[64]{0:T(128)S(1)}, bf16[8,1024,1024]{2,1,0:T(8,128)(2,1)S(1)}) custom-call(s32[64]{0:T(128)} %bitcast.4, s32[64]{0:T(128)} %block_h.1, bf16[8,64,1024]{2,1,0:T(8,128)(2,1)} %loads.1, bf16[8,1024,1024]{2,1,0:T(8,128)(2,1)} %ops.1), custom_call_target="tpu_custom_call" | custom-call | tf_op jit(solution)/shard_map/first_apply/pallas_call | solution.py:93
  8.1 0.0 copy-start
  8.1 0.0 copy-start.1
  8.1 38.3 %all_to_all.15.received = bf16[32,264,128]{2,1,0:T(8,128)(2,1)S(1)} all-to-all(bf16[32,264,128]{2,1,0:T(8,128)(2,1)S(1)} %get-tuple-element.16), channel_id=1, replica_groups=mesh['sub'=32,'rep'=4] {'sub'}, dimensions={0} | all-to-all | bytes 4325376 | tf_op jit(solution)/shard_map/all_to_all | solution.py:327
  46.4 0.0 copy-done
  46.4 0.0 copy-done.1
  46.4 2.4 %project.1 = (f32[16,64,128]{2,1,0:T(8,128)S(1)}, f32[32,1024]{1,0:T(8,128)S(1)}, f32[32,1024]{1,0:T(8,128)S(1)}, s32[32,128]{1,0:T(8,128)S(1)}, bf16[1024,1024]{1,0:T(8,128)(2,1)S(1)}) custom-call(bf16[32,264,128]{2,1,0:T(8,128)(2,1)S(1)} %all_to_all.15.received, s32[16,128]{1,0:T(8,128)S(1)} %bitcast.2, bf16[2048,1024]{1,0:T(8,128)(2,1)S(1)} %copy-done, ...), custom_call_target="tpu_custom_call" | custom-call | tf_op jit(solution)/shard_map/project/pallas_call | solution.py:203
  48.8 0.5 collective-permute-start
  49.3 1.0 collective-permute-done.refs_1_
  50.3 1.1 collective-permute-start.3
  51.3 0.5 collective-permute-start.2
  51.8 2.2 %collective-permute-start.1 = (bf16[32,1024]{1,0:T(8,128)(2,1)S(1)}, bf16[32,1024]{1,0:T(8,128)(2,1)S(1)}, u32[]{:S(2)}, u32[]{:S(2)}) collective-permute-start(bf16[32,1024]{1,0:T(8,128)(2,1)S(1)} %get-tuple-element.21.after), channel_id=1, source_target_pairs={{0,96},{4,100},{8,104},{12,108},{16,112},{20,116},{24,120},{28,124... | collective-permute-start | bytes 196616 | tf_op jit(solution)/shard_map/ppermute | solution.py:254
  54.0 2.4 %merge.2.refs_4_.first = bf16[1024,1024]{1,0:T(8,128)(2,1)S(1)} custom-call(bf16[1024,1024]{1,0:T(8,128)(2,1)S(1)} %get-tuple-element.22.coarse, bf16[2048,1024]{1,0:T(8,128)(2,1)S(1)} %copy-done, bf16[32,1024]{1,0:T(8,128)(2,1)S(1)} %get-tuple-element.21.after), custom_call_target="tpu_custom_call" | custom-call | tf_op jit(solution)/shard_map/merge/pallas_call | solution.py:147
  56.4 0.0 collective-permute-done.3.refs_3_
  56.4 0.4 collective-permute-done.2.refs_2_
  56.8 0.0 collective-permute-done.1.refs_1_
  56.9 0.9 collective-permute-start.6
  57.8 0.7 collective-permute-start.5
  58.4 2.0 %collective-permute-start.4 = (bf16[32,1024]{1,0:T(8,128)(2,1)S(1)}, bf16[32,1024]{1,0:T(8,128)(2,1)S(1)}, u32[]{:S(2)}, u32[]{:S(2)}) collective-permute-start(bf16[32,1024]{1,0:T(8,128)(2,1)S(1)} %get-tuple-element.24.after), channel_id=1, source_target_pairs={{0,24},{4,28},{8,0},{12,4},{16,8},{20,12},{24,16},{28,20},{32,56},... | collective-permute-start | bytes 196616 | tf_op jit(solution)/shard_map/ppermute | solution.py:254
  60.4 2.4 %merge.3.refs_4_.second = bf16[1024,1024]{1,0:T(8,128)(2,1)S(1)} custom-call(bf16[1024,1024]{1,0:T(8,128)(2,1)S(1)} %get-tuple-element.22.coarse, bf16[2048,1024]{1,0:T(8,128)(2,1)S(1)} %copy-done, bf16[32,1024]{1,0:T(8,128)(2,1)S(1)} %get-tuple-element.24.after), custom_call_target="tpu_custom_call" | custom-call | tf_op jit(solution)/shard_map/merge/pallas_call | solution.py:147
  62.8 0.0 collective-permute-done.6.refs_3_
  62.8 0.0 collective-permute-done.5.refs_2_
  62.8 0.0 collective-permute-done.4.refs_1_
  62.9 1.9 %collective-permute-start.7 = (bf16[32,1024]{1,0:T(8,128)(2,1)S(1)}, bf16[32,1024]{1,0:T(8,128)(2,1)S(1)}, u32[]{:S(2)}, u32[]{:S(2)}) collective-permute-start(bf16[32,1024]{1,0:T(8,128)(2,1)S(1)} %add_parts.5.own), channel_id=1, source_target_pairs={{0,4},{4,0},{8,12},{12,8},{16,20},{20,16},{24,28},{28,24},{32,36},... | collective-permute-start | bytes 196616 | tf_op jit(solution)/shard_map/ppermute | solution.py:254
  64.7 0.9 collective-permute-done.7.other
  65.6 2.7 %start_values.1 = (f32[64,2048]{1,0:T(8,128)}, bf16[32,256,128]{2,1,0:T(8,128)(2,1)S(1)}) custom-call(s32[32,128]{1,0:T(8,128)S(1)} %get-tuple-element.17.ids, bf16[32,1024]{1,0:T(8,128)(2,1)S(1)} %add_parts.5.own, bf16[32,1024]{1,0:T(8,128)(2,1)S(1)} %collective-permute-done.7.other, bf16[1024,1024]{1,0:T(8,128)(2,1)S(1)} %merge.2.refs_4_.first, ...), custom_call_target="tpu_custom_call" | custom-call | tf_op jit(solution)/shard_map/start_values/pallas_call | solution.py:289
  68.4 35.1 %all_to_all.16.back = bf16[32,256,128]{2,1,0:T(8,128)(2,1)S(1)} all-to-all(bf16[32,256,128]{2,1,0:T(8,128)(2,1)S(1)} %get-tuple-element.27), channel_id=1, replica_groups=mesh['sub'=32,'rep'=4] {'sub'}, dimensions={0} | all-to-all | bytes 4194304 | tf_op jit(solution)/shard_map/all_to_all | solution.py:327
  103.5 3.6 %second_apply.1 = bf16[32,256,128]{2,1,0:T(8,128)(2,1)S(1)} custom-call(s32[64]{0:T(128)S(1)} %get-tuple-element.26.pos, bf16[32,256,128]{2,1,0:T(8,128)(2,1)S(1)} %all_to_all.16.back, bf16[8,1024,1024]{2,1,0:T(8,128)(2,1)S(1)} %get-tuple-element.28.ops), custom_call_target="tpu_custom_call" | custom-call | tf_op jit(solution)/shard_map/second_apply/pallas_call | solution.py:127
  107.1 31.9 %all_to_all.17.received = bf16[32,256,128]{2,1,0:T(8,128)(2,1)S(1)} all-to-all(bf16[32,256,128]{2,1,0:T(8,128)(2,1)S(1)} %second_apply.1), channel_id=1, replica_groups=mesh['sub'=32,'rep'=4] {'sub'}, dimensions={0} | all-to-all | bytes 4194304 | tf_op jit(solution)/shard_map/all_to_all | solution.py:327
  139.0 2.3 %residual.1 = f32[64,2048]{1,0:T(8,128)} custom-call(s32[32,128]{1,0:T(8,128)S(1)} %get-tuple-element.17.ids, bf16[32,256,128]{2,1,0:T(8,128)(2,1)S(1)} %all_to_all.17.received, s32[16,128]{1,0:T(8,128)S(1)} %bitcast.3, f32[16,64,128]{2,1,0:T(8,128)S(1)} %get-tuple-element.29.dual), custom_call_target="tpu_custom_call" | custom-call | tf_op jit(solution)/shard_map/residual/pallas_call | solution.py:315
  (3 shorter events, 0.1 us)
Async XLA Ops:
  8.1 38.3 %copy-start = (bf16[2048,1024]{1,0:T(8,128)(2,1)S(1)}, bf16[2048,1024]{1,0:T(8,128)(2,1)}, u32[]{:S(2)}) copy-start(bf16[2048,1024]{1,0:T(8,128)(2,1)} %basis.5) | copy-start | bytes 12582916
  8.1 38.3 %copy-start.1 = (s32[2048]{0:T(1024)S(1)}, s32[2048]{0:T(1024)}, u32[]{:S(2)}) copy-start(s32[2048]{0:T(1024)} %param.11) | copy-start | bytes 24580
  48.8 1.5 %collective-permute-start = (f32[32,1024]{1,0:T(8,128)S(1)}, f32[32,1024]{1,0:T(8,128)S(1)}, u32[]{:S(2)}, u32[]{:S(2)}) collective-permute-start(f32[32,1024]{1,0:T(8,128)S(1)} %get-tuple-element.19), channel_id=1, source_target_pairs={{0,4},{4,0},{8,12},{12,8},{16,20},{20,16},{24,28},{28,24},{32,36},... | collective-permute-start | bytes 393224 | tf_op jit(solution)/shard_map/ppermute | solution.py:254
  50.3 6.1 %collective-permute-start.3 = (bf16[32,1024]{1,0:T(8,128)(2,1)S(1)}, bf16[32,1024]{1,0:T(8,128)(2,1)S(1)}, u32[]{:S(2)}, u32[]{:S(2)}) collective-permute-start(bf16[32,1024]{1,0:T(8,128)(2,1)S(1)} %get-tuple-element.21.after), channel_id=1, source_target_pairs={{0,64},{4,68},{8,72},{12,76},{16,80},{20,84},{24,88},{28,92},{32,9... | collective-permute-start | bytes 196616 | tf_op jit(solution)/shard_map/ppermute | solution.py:254
  51.3 5.5 %collective-permute-start.2 = (bf16[32,1024]{1,0:T(8,128)(2,1)S(1)}, bf16[32,1024]{1,0:T(8,128)(2,1)S(1)}, u32[]{:S(2)}, u32[]{:S(2)}) collective-permute-start(bf16[32,1024]{1,0:T(8,128)(2,1)S(1)} %get-tuple-element.21.after), channel_id=1, source_target_pairs={{0,32},{4,36},{8,40},{12,44},{16,48},{20,52},{24,56},{28,60},{32,6... | collective-permute-start | bytes 196616 | tf_op jit(solution)/shard_map/ppermute | solution.py:254
  51.8 5.0 %collective-permute-start.1 = (bf16[32,1024]{1,0:T(8,128)(2,1)S(1)}, bf16[32,1024]{1,0:T(8,128)(2,1)S(1)}, u32[]{:S(2)}, u32[]{:S(2)}) collective-permute-start(bf16[32,1024]{1,0:T(8,128)(2,1)S(1)} %get-tuple-element.21.after), channel_id=1, source_target_pairs={{0,96},{4,100},{8,104},{12,108},{16,112},{20,116},{24,120},{28,124... | collective-permute-start | bytes 196616 | tf_op jit(solution)/shard_map/ppermute | solution.py:254
  56.9 5.9 %collective-permute-start.6 = (bf16[32,1024]{1,0:T(8,128)(2,1)S(1)}, bf16[32,1024]{1,0:T(8,128)(2,1)S(1)}, u32[]{:S(2)}, u32[]{:S(2)}) collective-permute-start(bf16[32,1024]{1,0:T(8,128)(2,1)S(1)} %get-tuple-element.24.after), channel_id=1, source_target_pairs={{0,16},{4,20},{8,24},{12,28},{16,0},{20,4},{24,8},{28,12},{32,48},... | collective-permute-start | bytes 196616 | tf_op jit(solution)/shard_map/ppermute | solution.py:254
  57.8 5.1 %collective-permute-start.5 = (bf16[32,1024]{1,0:T(8,128)(2,1)S(1)}, bf16[32,1024]{1,0:T(8,128)(2,1)S(1)}, u32[]{:S(2)}, u32[]{:S(2)}) collective-permute-start(bf16[32,1024]{1,0:T(8,128)(2,1)S(1)} %get-tuple-element.24.after), channel_id=1, source_target_pairs={{0,8},{4,12},{8,16},{12,20},{16,24},{20,28},{24,0},{28,4},{32,40},... | collective-permute-start | bytes 196616 | tf_op jit(solution)/shard_map/ppermute | solution.py:254
  58.4 4.4 %collective-permute-start.4 = (bf16[32,1024]{1,0:T(8,128)(2,1)S(1)}, bf16[32,1024]{1,0:T(8,128)(2,1)S(1)}, u32[]{:S(2)}, u32[]{:S(2)}) collective-permute-start(bf16[32,1024]{1,0:T(8,128)(2,1)S(1)} %get-tuple-element.24.after), channel_id=1, source_target_pairs={{0,24},{4,28},{8,0},{12,4},{16,8},{20,12},{24,16},{28,20},{32,56},... | collective-permute-start | bytes 196616 | tf_op jit(solution)/shard_map/ppermute | solution.py:254
  62.9 2.8 %collective-permute-start.7 = (bf16[32,1024]{1,0:T(8,128)(2,1)S(1)}, bf16[32,1024]{1,0:T(8,128)(2,1)S(1)}, u32[]{:S(2)}, u32[]{:S(2)}) collective-permute-start(bf16[32,1024]{1,0:T(8,128)(2,1)S(1)} %add_parts.5.own), channel_id=1, source_target_pairs={{0,4},{4,0},{8,12},{12,8},{16,20},{20,16},{24,28},{28,24},{32,36},... | collective-permute-start | bytes 196616 | tf_op jit(solution)/shard_map/ppermute | solution.py:254

commit v5 on v4

--- a/solution.py
+++ b/solution.py
@@ -26,7 +26,6 @@
 HBM = pl.BlockSpec(memory_space=pl.ANY)
 SMEM = pl.BlockSpec(memory_space=pltpu.SMEM)
 VMEM = pl.BlockSpec(memory_space=pltpu.VMEM)
-AHEAD = 4
 
 
 def params(mib):
@@ -51,10 +50,18 @@
     owner_copy.start()
     block_copy.start()
     load_copy = pltpu.make_async_copy(loads, loads_v, load_sem)
-    copies = [pltpu.make_async_copy(ops.at[s], ops_v.at[s], sem.at[s]) for s in range(NSUB)]
+    copies = [pltpu.make_async_copy(ops.at[s], ops_v.at[s], sem.at[s]) for s in range(NSUB - 1)]
+    copies += [
+        pltpu.make_async_copy(
+            ops.at[NSUB - 1, pl.ds(h * (L // 2), L // 2)],
+            ops_v.at[NSUB - 1, pl.ds(h * (L // 2), L // 2)],
+            sem.at[NSUB - 1 + h],
+        )
+        for h in range(2)
+    ]
     load_copy.start()
-    for s in range(AHEAD):
-        copies[s].start()
+    for c in copies:
+        c.start()
 
     def zero(i, c):
         count[i] = 0
@@ -82,9 +89,15 @@
     load_copy.wait()
     for s in range(NSUB):
         copies[s].wait()
-        if s + AHEAD < NSUB:
-            copies[s + AHEAD].start()
-        prod = jnp.dot(loads_v[s], ops_v[s], preferred_element_type=F32)
+        if s < NSUB - 1:
+            prod = jnp.dot(loads_v[s], ops_v[s], preferred_element_type=F32)
+        else:
+            half = L // 2
+            prod = jnp.dot(loads_v[s, :, :half], ops_v[s, :half], preferred_element_type=F32)
+            copies[s + 1].wait()
+            prod = prod + jnp.dot(
+                loads_v[s, :, half:], ops_v[s, half:], preferred_element_type=F32
+            )
         for j in range(BPS):
             slot(out, pos[s * BPS + j])[...] = prod[:, j * BLK : (j + 1) * BLK].astype(BF)
 
@@ -104,7 +117,7 @@
             pltpu.SMEM((NBLK,), jnp.int32),
             pltpu.SMEM((PEERS,), jnp.int32),
             pltpu.VMEM((NSUB, COLS, L), BF),
-            pltpu.SemaphoreType.DMA((NSUB,)),
+            pltpu.SemaphoreType.DMA((NSUB + 1,)),
             pltpu.SemaphoreType.DMA,
             pltpu.SemaphoreType.DMA((2,)),
         ],
@@ -154,10 +167,12 @@
     )(in_vmem(coarse), in_vmem(basis), in_vmem(after))
 
 
-def add_slots(received, ids, totals):
+def zero_totals(totals):
     for q in range(CAP):
         totals[q][...] = jnp.zeros(totals[q].shape, F32)
 
+
+def add_slots(received, ids, totals):
     def peer(p, c):
         for q in range(CAP):
             g = ids[p, q]
@@ -183,6 +198,7 @@
     ids_copy = pltpu.make_async_copy(idv, ids, sem)
     ids_copy.start()
     ids_out[...] = idv[...]
+    zero_totals(totals)
     ids_copy.wait()
     add_slots(received, ids, totals)
     weight = 1.0 / (1.0 + scale[...].astype(F32))
@@ -206,7 +222,7 @@
             pltpu.VMEM((OB, COLS, BLK), F32),
             pltpu.VMEM((HALF, NB), F32),
             pltpu.VMEM((HALF, NB), F32),
-            jax.ShapeDtypeStruct((PEERS, BLK), jnp.int32),
+            pltpu.VMEM((PEERS, BLK), jnp.int32),
             pltpu.VMEM((NB, NB), BF),
         ),
         in_specs=[VMEM] * 3 + [HBM],
@@ -246,35 +262,47 @@
     )(in_vmem(own), *[in_vmem(o) for o in (*others, *after)])
 
 
-def shifted(values, dx, dy, dc):
-    pairs = []
-    for i in range(PEERS):
-        x, y, c = i // 8, i // 2 % 4, i % 2
-        pairs.append((i, (x + dx) % 4 * 8 + (y + dy) % 4 * 2 + (c + dc) % 2))
+def swapped(values, kx, ky, kc):
+    pairs = [(i, i ^ (kx * 8 + ky * 2 + kc)) for i in range(PEERS)]
     return lax.ppermute(values, "sub", pairs)
 
 
 def sum_over_owners(keep, send, coarse, basis):
     both = (F32, BF)
-    total, narrow = add_parts(keep, [shifted(send, 0, 0, 1)], both)
+    total, narrow = add_parts(keep, [swapped(send, 0, 0, 1)], both)
     first = merge(0, coarse, basis, narrow)
-    others = [shifted(narrow, k, 0, 0) for k in (3, 1, 2)]
+    others = [swapped(narrow, k, 0, 0) for k in (3, 1, 2)]
     total, narrow = add_parts(total, others, both, (first,))
     second = merge(1, coarse, basis, narrow)
-    others = [shifted(narrow, 0, k, 0) for k in (3, 1, 2)]
+    others = [swapped(narrow, 0, k, 0) for k in (3, 1, 2)]
     (narrow,) = add_parts(total, others, (BF,), (second,))
-    return narrow, shifted(narrow, 0, 0, 1), first, second
-
-
-def start_kernel(ids, own, other, first, second, start, out, coeff, blocks):
+    return narrow, swapped(narrow, 0, 0, 1), first, second
+
+
+PIECES = 4
+PIECE = OB * BLK // PIECES
+
+
+def start_kernel(ids_v, own, other, first, second, start, out, coeff, blocks, value, ids, sem, ids_sem):
+    ids_copy = pltpu.make_async_copy(ids_v, ids, ids_sem)
+    ids_copy.start()
     core = lax.axis_index("sub") % 2
     coeff[core] = own[...]
     coeff[1 - core] = other[...]
-    for part, merged in enumerate((first, second)):
-        value = jnp.dot(coeff[...].reshape(COLS, NB), merged[...], preferred_element_type=F32)
-        start[:, part * MERGE : (part + 1) * MERGE] = value
-        for k in range(MERGE // BLK):
-            blocks[part * (MERGE // BLK) + k] = value[:, k * BLK : (k + 1) * BLK].astype(BF)
+    copies = []
+    for n in range(PIECES):
+        merged = (first, second)[n // 2]
+        cols = slice(n % 2 * PIECE, (n % 2 + 1) * PIECE)
+        value[n] = jnp.dot(
+            coeff[...].reshape(COLS, NB), merged[:, cols], preferred_element_type=F32
+        )
+        copies.append(
+            pltpu.make_async_copy(value.at[n], start.at[:, pl.ds(n * PIECE, PIECE)], sem.at[n])
+        )
+        copies[n].start()
+        for k in range(PIECE // BLK):
+            blocks[n * (PIECE // BLK) + k] = value[n, :, k * BLK : (k + 1) * BLK].astype(BF)
+    ids_copy.wait()
 
     def peer(p, c):
         for q in range(CAP):
@@ -283,6 +311,8 @@
         return c
 
     lax.fori_loop(0, PEERS, peer, 0, unroll=2)
+    for c in copies:
+        c.wait()
 
 
 def start_values(ids, own, other, first, second):
@@ -292,35 +322,60 @@
             jax.ShapeDtypeStruct((COLS, OB * BLK), F32),
             pltpu.VMEM((PEERS, SLOTROWS, BLK), BF),
         ),
-        in_specs=[SMEM] + [VMEM] * 4,
-        out_specs=[VMEM, VMEM],
+        in_specs=[VMEM] * 5,
+        out_specs=[HBM, VMEM],
         scratch_shapes=[
             pltpu.VMEM((2, HALF, NB), BF),
             pltpu.VMEM((OB, COLS, BLK), BF),
+            pltpu.VMEM((PIECES, COLS, PIECE), F32),
+            pltpu.SMEM((PEERS, BLK), jnp.int32),
+            pltpu.SemaphoreType.DMA((PIECES,)),
+            pltpu.SemaphoreType.DMA,
         ],
         compiler_params=params(8),
         name="start_values",
-    )(ids, in_vmem(own), in_vmem(other), in_vmem(first), in_vmem(second))
-
-
-def resid_kernel(ids, received, scale, dual, resid, t0, t1, t2, t3):
+    )(in_vmem(ids), in_vmem(own), in_vmem(other), in_vmem(first), in_vmem(second))
+
+
+def resid_kernel(ids_v, received, scale, dual, resid, t0, t1, t2, t3, value, ids, sem, ids_sem):
+    ids_copy = pltpu.make_async_copy(ids_v, ids, ids_sem)
+    ids_copy.start()
     totals = (t0, t1, t2, t3)
+    zero_totals(totals)
+    weight = 1.0 / (1.0 + scale[...].astype(F32))
+    ids_copy.wait()
     add_slots(received, ids, totals)
-    weight = 1.0 / (1.0 + scale[...].astype(F32))
-    for b in range(OB):
-        resid[:, b * BLK : (b + 1) * BLK] = dual[b] - sum_totals(totals, b) * weight[b : b + 1, :]
+    copies = []
+    for n in range(PIECES):
+        for k in range(PIECE // BLK):
+            b = n * (PIECE // BLK) + k
+            value[n, :, k * BLK : (k + 1) * BLK] = (
+                dual[b] - sum_totals(totals, b) * weight[b : b + 1, :]
+            )
+        copies.append(
+            pltpu.make_async_copy(value.at[n], resid.at[:, pl.ds(n * PIECE, PIECE)], sem.at[n])
+        )
+        copies[n].start()
+    for c in copies:
+        c.wait()
 
 
 def residual(ids, received, scale, dual):
     return pl.pallas_call(
         resid_kernel,
         out_shape=jax.ShapeDtypeStruct((COLS, OB * BLK), F32),
-        in_specs=[SMEM] + [VMEM] * 3,
-        out_specs=VMEM,
-        scratch_shapes=TOTALS,
+        in_specs=[VMEM] * 4,
+        out_specs=HBM,
+        scratch_shapes=TOTALS
+        + [
+            pltpu.VMEM((PIECES, COLS, PIECE), F32),
+            pltpu.SMEM((PEERS, BLK), jnp.int32),
+            pltpu.SemaphoreType.DMA((PIECES,)),
+            pltpu.SemaphoreType.DMA,
+        ],
         compiler_params=params(8),
         name="residual",
-    )(ids, in_vmem(received), scale, in_vmem(dual))
+    )(in_vmem(ids), in_vmem(received), scale, in_vmem(dual))
 
 
 def exchange(values):

time: 142 us -> 142 us (level)
  blocking collectives: 105 us -> 103 us
    pallas_call x1, Pallas kernels: 7.47 us -> 10.2 us  [first_apply(): pl.pallas_call(first_kernel, out_shape=(pltpu.VMEM((PEERS, SLOTROWS + IDR...]
    all_to_all x3, blocking collectives: 105 us -> 103 us  [exchange(): lax.all_to_all(values, 'sub', split_axis=0, concat_axis=0, tiled=True)]
  transfers between devices with their start and end apart: 8 -> 8, of which waited for: 3 -> 4; matrix products, arithmetic and copies ran while one was open for 0% -> 0% of each run, Pallas kernels for 3% -> 3%
where the time goes in v5:
time: 142 us
  blocking collectives  103 us (73%)
  Pallas kernels  24.7 us (17%)
  starting transfers between devices  10.5 us (7%)
  waiting for transfers between devices  2.72 us (2%)
    all_to_all x3, blocking collectives, exchange(): lax.all_to_all(values, 'sub', split_axis=0, concat_axis=0, tiled=True)  103 us
    ppermute x8, starting transfers between devices, swapped(): return lax.ppermute(values, 'sub', pairs)  10.5 us
    pallas_call x1, Pallas kernels, first_apply(): pl.pallas_call(first_kernel, out_shape=(pltpu.VMEM((PEERS, SLOTROWS + IDR...  10.2 us
    pallas_call x2, Pallas kernels, merge(): pl.pallas_call(functools.partial(merge_kernel, part), out_shape=pltpu.VME...  4.74 us
    pallas_call x1, Pallas kernels, second_apply(): pl.pallas_call(second_kernel, out_shape=pltpu.VMEM((PEERS, SLOTROWS, BLK)...  3.61 us
  transfers between devices with their start and end apart: 8, of which 4 were waited for; matrix products, arithmetic and copies ran while one was open for 0% of the time, Pallas kernels for 3%

profile of v5, /device:TPU:1, one launch (start us, length us, event | category | flops | bytes accessed | tf_op | source)
XLA Modules:
  0.0 142.3 jit_solution(16437740370170318315)
XLA Ops:
  0.6 10.2 %first_apply.1 = (bf16[32,264,128]{2,1,0:T(8,128)(2,1)S(1)}, s32[64]{0:T(128)S(1)}, bf16[8,1024,1024]{2,1,0:T(8,128)(2,1)S(1)}) custom-call(s32[64]{0:T(128)} %bitcast.4, s32[64]{0:T(128)} %block_h.1, bf16[8,64,1024]{2,1,0:T(8,128)(2,1)} %loads.1, bf16[8,1024,1024]{2,1,0:T(8,128)(2,1)} %ops.1), custom_call_target="tpu_custom_call" | custom-call | tf_op jit(solution)/shard_map/first_apply/pallas_call | solution.py:106
  10.8 0.0 copy-start
  10.8 0.0 copy-start.1
  10.8 38.3 %all_to_all.15.received = bf16[32,264,128]{2,1,0:T(8,128)(2,1)S(1)} all-to-all(bf16[32,264,128]{2,1,0:T(8,128)(2,1)S(1)} %get-tuple-element.16), channel_id=1, replica_groups=mesh['sub'=32,'rep'=4] {'sub'}, dimensions={0} | all-to-all | bytes 4325376 | tf_op jit(solution)/shard_map/all_to_all | solution.py:382
  49.1 0.0 copy-done
  49.1 0.0 copy-done.1
  49.1 2.4 %project.1 = (f32[16,64,128]{2,1,0:T(8,128)S(1)}, f32[32,1024]{1,0:T(8,128)S(1)}, f32[32,1024]{1,0:T(8,128)S(1)}, s32[32,128]{1,0:T(8,128)S(1)}, bf16[1024,1024]{1,0:T(8,128)(2,1)S(1)}) custom-call(bf16[32,264,128]{2,1,0:T(8,128)(2,1)S(1)} %all_to_all.15.received, s32[16,128]{1,0:T(8,128)S(1)} %bitcast.2, bf16[2048,1024]{1,0:T(8,128)(2,1)S(1)} %copy-done, ...), custom_call_target="tpu_custom_call" | custom-call | tf_op jit(solution)/shard_map/project/pallas_call | solution.py:219
  51.5 0.5 collective-permute-start
  52.0 1.0 collective-permute-done.refs_1_
  53.0 1.0 collective-permute-start.3
  54.0 0.5 collective-permute-start.2
  54.5 1.8 %collective-permute-start.1 = (bf16[32,1024]{1,0:T(8,128)(2,1)S(1)}, bf16[32,1024]{1,0:T(8,128)(2,1)S(1)}, u32[]{:S(2)}, u32[]{:S(2)}) collective-permute-start(bf16[32,1024]{1,0:T(8,128)(2,1)S(1)} %get-tuple-element.21.after), channel_id=1, source_target_pairs={{0,96},{4,100},{8,104},{12,108},{16,112},{20,116},{24,120},{28,124... | collective-permute-start | bytes 196616 | tf_op jit(solution)/shard_map/ppermute | solution.py:267
  56.3 2.4 %merge.2.refs_4_.first = bf16[1024,1024]{1,0:T(8,128)(2,1)S(1)} custom-call(bf16[1024,1024]{1,0:T(8,128)(2,1)S(1)} %get-tuple-element.22.coarse, bf16[2048,1024]{1,0:T(8,128)(2,1)S(1)} %copy-done, bf16[32,1024]{1,0:T(8,128)(2,1)S(1)} %get-tuple-element.21.after), custom_call_target="tpu_custom_call" | custom-call | tf_op jit(solution)/shard_map/merge/pallas_call | solution.py:160
  58.7 0.0 collective-permute-done.3.refs_3_
  58.7 0.0 collective-permute-done.2.refs_2_
  58.7 0.7 collective-permute-done.1.refs_1_
  59.4 0.8 collective-permute-start.6
  60.3 0.7 collective-permute-start.5
  61.0 1.8 %collective-permute-start.4 = (bf16[32,1024]{1,0:T(8,128)(2,1)S(1)}, bf16[32,1024]{1,0:T(8,128)(2,1)S(1)}, u32[]{:S(2)}, u32[]{:S(2)}) collective-permute-start(bf16[32,1024]{1,0:T(8,128)(2,1)S(1)} %get-tuple-element.24.after), channel_id=1, source_target_pairs={{0,24},{4,28},{8,16},{12,20},{16,8},{20,12},{24,0},{28,4},{32,56},... | collective-permute-start | bytes 196616 | tf_op jit(solution)/shard_map/ppermute | solution.py:267
  62.8 2.4 %merge.3.refs_4_.second = bf16[1024,1024]{1,0:T(8,128)(2,1)S(1)} custom-call(bf16[1024,1024]{1,0:T(8,128)(2,1)S(1)} %get-tuple-element.22.coarse, bf16[2048,1024]{1,0:T(8,128)(2,1)S(1)} %copy-done, bf16[32,1024]{1,0:T(8,128)(2,1)S(1)} %get-tuple-element.24.after), custom_call_target="tpu_custom_call" | custom-call | tf_op jit(solution)/shard_map/merge/pallas_call | solution.py:160
  65.1 0.0 collective-permute-done.6.refs_3_
  65.1 0.0 collective-permute-done.5.refs_2_
  65.2 0.1 collective-permute-done.4.refs_1_
  65.3 3.3 %collective-permute-start.7 = (bf16[32,1024]{1,0:T(8,128)(2,1)S(1)}, bf16[32,1024]{1,0:T(8,128)(2,1)S(1)}, u32[]{:S(2)}, u32[]{:S(2)}) collective-permute-start(bf16[32,1024]{1,0:T(8,128)(2,1)S(1)} %add_parts.5.own), channel_id=1, source_target_pairs={{0,4},{4,0},{8,12},{12,8},{16,20},{20,16},{24,28},{28,24},{32,36},... | collective-permute-start | bytes 196616 | tf_op jit(solution)/shard_map/ppermute | solution.py:267
  68.7 0.9 collective-permute-done.7.other
  69.6 1.7 %start_values.1 = (f32[64,2048]{1,0:T(8,128)}, bf16[32,256,128]{2,1,0:T(8,128)(2,1)S(1)}) custom-call(s32[32,128]{1,0:T(8,128)S(1)} %get-tuple-element.17.ids_v, bf16[32,1024]{1,0:T(8,128)(2,1)S(1)} %add_parts.5.own, bf16[32,1024]{1,0:T(8,128)(2,1)S(1)} %collective-permute-done.7.other, bf16[1024,1024]{1,0:T(8,128)(2,1)S(1)} %merge.2.refs_4_.first, ...), custom_call_target="tpu_custom_call" | custom-call | tf_op jit(solution)/shard_map/start_values/pallas_call | solution.py:319
  71.2 33.3 %all_to_all.16.back = bf16[32,256,128]{2,1,0:T(8,128)(2,1)S(1)} all-to-all(bf16[32,256,128]{2,1,0:T(8,128)(2,1)S(1)} %get-tuple-element.27), channel_id=1, replica_groups=mesh['sub'=32,'rep'=4] {'sub'}, dimensions={0} | all-to-all | bytes 4194304 | tf_op jit(solution)/shard_map/all_to_all | solution.py:382
  104.5 3.6 %second_apply.1 = bf16[32,256,128]{2,1,0:T(8,128)(2,1)S(1)} custom-call(s32[64]{0:T(128)S(1)} %get-tuple-element.26.pos, bf16[32,256,128]{2,1,0:T(8,128)(2,1)S(1)} %all_to_all.16.back, bf16[8,1024,1024]{2,1,0:T(8,128)(2,1)S(1)} %get-tuple-element.28.ops), custom_call_target="tpu_custom_call" | custom-call | tf_op jit(solution)/shard_map/second_apply/pallas_call | solution.py:140
  108.1 31.9 %all_to_all.17.received = bf16[32,256,128]{2,1,0:T(8,128)(2,1)S(1)} all-to-all(bf16[32,256,128]{2,1,0:T(8,128)(2,1)S(1)} %second_apply.1), channel_id=1, replica_groups=mesh['sub'=32,'rep'=4] {'sub'}, dimensions={0} | all-to-all | bytes 4194304 | tf_op jit(solution)/shard_map/all_to_all | solution.py:382
  140.0 2.1 %residual.1 = f32[64,2048]{1,0:T(8,128)} custom-call(s32[32,128]{1,0:T(8,128)S(1)} %get-tuple-element.17.ids_v, bf16[32,256,128]{2,1,0:T(8,128)(2,1)S(1)} %all_to_all.17.received, s32[16,128]{1,0:T(8,128)S(1)} %bitcast.3, f32[16,64,128]{2,1,0:T(8,128)S(1)} %get-tuple-element.29.dual), custom_call_target="tpu_custom_call" | custom-call | tf_op jit(solution)/shard_map/residual/pallas_call | solution.py:364
  (3 shorter events, 0.1 us)
Async XLA Ops:
  10.8 38.3 %copy-start = (bf16[2048,1024]{1,0:T(8,128)(2,1)S(1)}, bf16[2048,1024]{1,0:T(8,128)(2,1)}, u32[]{:S(2)}) copy-start(bf16[2048,1024]{1,0:T(8,128)(2,1)} %basis.5) | copy-start | bytes 12582916
  10.8 38.3 %copy-start.1 = (s32[2048]{0:T(1024)S(1)}, s32[2048]{0:T(1024)}, u32[]{:S(2)}) copy-start(s32[2048]{0:T(1024)} %param.11) | copy-start | bytes 24580
  51.5 1.5 %collective-permute-start = (f32[32,1024]{1,0:T(8,128)S(1)}, f32[32,1024]{1,0:T(8,128)S(1)}, u32[]{:S(2)}, u32[]{:S(2)}) collective-permute-start(f32[32,1024]{1,0:T(8,128)S(1)} %get-tuple-element.19), channel_id=1, source_target_pairs={{0,4},{4,0},{8,12},{12,8},{16,20},{20,16},{24,28},{28,24},{32,36},... | collective-permute-start | bytes 393224 | tf_op jit(solution)/shard_map/ppermute | solution.py:267
  53.0 5.7 %collective-permute-start.3 = (bf16[32,1024]{1,0:T(8,128)(2,1)S(1)}, bf16[32,1024]{1,0:T(8,128)(2,1)S(1)}, u32[]{:S(2)}, u32[]{:S(2)}) collective-permute-start(bf16[32,1024]{1,0:T(8,128)(2,1)S(1)} %get-tuple-element.21.after), channel_id=1, source_target_pairs={{0,64},{4,68},{8,72},{12,76},{16,80},{20,84},{24,88},{28,92},{32,9... | collective-permute-start | bytes 196616 | tf_op jit(solution)/shard_map/ppermute | solution.py:267
  54.0 4.7 %collective-permute-start.2 = (bf16[32,1024]{1,0:T(8,128)(2,1)S(1)}, bf16[32,1024]{1,0:T(8,128)(2,1)S(1)}, u32[]{:S(2)}, u32[]{:S(2)}) collective-permute-start(bf16[32,1024]{1,0:T(8,128)(2,1)S(1)} %get-tuple-element.21.after), channel_id=1, source_target_pairs={{0,32},{4,36},{8,40},{12,44},{16,48},{20,52},{24,56},{28,60},{32,0... | collective-permute-start | bytes 196616 | tf_op jit(solution)/shard_map/ppermute | solution.py:267
  54.5 4.9 %collective-permute-start.1 = (bf16[32,1024]{1,0:T(8,128)(2,1)S(1)}, bf16[32,1024]{1,0:T(8,128)(2,1)S(1)}, u32[]{:S(2)}, u32[]{:S(2)}) collective-permute-start(bf16[32,1024]{1,0:T(8,128)(2,1)S(1)} %get-tuple-element.21.after), channel_id=1, source_target_pairs={{0,96},{4,100},{8,104},{12,108},{16,112},{20,116},{24,120},{28,124... | collective-permute-start | bytes 196616 | tf_op jit(solution)/shard_map/ppermute | solution.py:267
  59.4 5.7 %collective-permute-start.6 = (bf16[32,1024]{1,0:T(8,128)(2,1)S(1)}, bf16[32,1024]{1,0:T(8,128)(2,1)S(1)}, u32[]{:S(2)}, u32[]{:S(2)}) collective-permute-start(bf16[32,1024]{1,0:T(8,128)(2,1)S(1)} %get-tuple-element.24.after), channel_id=1, source_target_pairs={{0,16},{4,20},{8,24},{12,28},{16,0},{20,4},{24,8},{28,12},{32,48},... | collective-permute-start | bytes 196616 | tf_op jit(solution)/shard_map/ppermute | solution.py:267
  60.3 4.9 %collective-permute-start.5 = (bf16[32,1024]{1,0:T(8,128)(2,1)S(1)}, bf16[32,1024]{1,0:T(8,128)(2,1)S(1)}, u32[]{:S(2)}, u32[]{:S(2)}) collective-permute-start(bf16[32,1024]{1,0:T(8,128)(2,1)S(1)} %get-tuple-element.24.after), channel_id=1, source_target_pairs={{0,8},{4,12},{8,0},{12,4},{16,24},{20,28},{24,16},{28,20},{32,40},... | collective-permute-start | bytes 196616 | tf_op jit(solution)/shard_map/ppermute | solution.py:267
  61.0 4.3 %collective-permute-start.4 = (bf16[32,1024]{1,0:T(8,128)(2,1)S(1)}, bf16[32,1024]{1,0:T(8,128)(2,1)S(1)}, u32[]{:S(2)}, u32[]{:S(2)}) collective-permute-start(bf16[32,1024]{1,0:T(8,128)(2,1)S(1)} %get-tuple-element.24.after), channel_id=1, source_target_pairs={{0,24},{4,28},{8,16},{12,20},{16,8},{20,12},{24,0},{28,4},{32,56},... | collective-permute-start | bytes 196616 | tf_op jit(solution)/shard_map/ppermute | solution.py:267
  65.3 4.2 %collective-permute-start.7 = (bf16[32,1024]{1,0:T(8,128)(2,1)S(1)}, bf16[32,1024]{1,0:T(8,128)(2,1)S(1)}, u32[]{:S(2)}, u32[]{:S(2)}) collective-permute-start(bf16[32,1024]{1,0:T(8,128)(2,1)S(1)} %add_parts.5.own), channel_id=1, source_target_pairs={{0,4},{4,0},{8,12},{12,8},{16,20},{20,16},{24,28},{28,24},{32,36},... | collective-permute-start | bytes 196616 | tf_op jit(solution)/shard_map/ppermute | solution.py:267

commit v6 on v5

--- a/solution.py
+++ b/solution.py
@@ -26,6 +26,7 @@
 HBM = pl.BlockSpec(memory_space=pl.ANY)
 SMEM = pl.BlockSpec(memory_space=pltpu.SMEM)
 VMEM = pl.BlockSpec(memory_space=pltpu.VMEM)
+AHEAD = 4
 
 
 def params(mib):
@@ -50,18 +51,10 @@
     owner_copy.start()
     block_copy.start()
     load_copy = pltpu.make_async_copy(loads, loads_v, load_sem)
-    copies = [pltpu.make_async_copy(ops.at[s], ops_v.at[s], sem.at[s]) for s in range(NSUB - 1)]
-    copies += [
-        pltpu.make_async_copy(
-            ops.at[NSUB - 1, pl.ds(h * (L // 2), L // 2)],
-            ops_v.at[NSUB - 1, pl.ds(h * (L // 2), L // 2)],
-            sem.at[NSUB - 1 + h],
-        )
-        for h in range(2)
-    ]
+    copies = [pltpu.make_async_copy(ops.at[s], ops_v.at[s], sem.at[s]) for s in range(NSUB)]
     load_copy.start()
-    for c in copies:
-        c.start()
+    for s in range(AHEAD):
+        copies[s].start()
 
     def zero(i, c):
         count[i] = 0
@@ -89,15 +82,9 @@
     load_copy.wait()
     for s in range(NSUB):
         copies[s].wait()
-        if s < NSUB - 1:
-            prod = jnp.dot(loads_v[s], ops_v[s], preferred_element_type=F32)
-        else:
-            half = L // 2
-            prod = jnp.dot(loads_v[s, :, :half], ops_v[s, :half], preferred_element_type=F32)
-            copies[s + 1].wait()
-            prod = prod + jnp.dot(
-                loads_v[s, :, half:], ops_v[s, half:], preferred_element_type=F32
-            )
+        if s + AHEAD < NSUB:
+            copies[s + AHEAD].start()
+        prod = jnp.dot(loads_v[s], ops_v[s], preferred_element_type=F32)
         for j in range(BPS):
             slot(out, pos[s * BPS + j])[...] = prod[:, j * BLK : (j + 1) * BLK].astype(BF)
 
@@ -117,7 +104,7 @@
             pltpu.SMEM((NBLK,), jnp.int32),
             pltpu.SMEM((PEERS,), jnp.int32),
             pltpu.VMEM((NSUB, COLS, L), BF),
-            pltpu.SemaphoreType.DMA((NSUB + 1,)),
+            pltpu.SemaphoreType.DMA((NSUB,)),
             pltpu.SemaphoreType.DMA,
             pltpu.SemaphoreType.DMA((2,)),
         ],

time: 142 us -> 140 us (0.986)
  Pallas kernels: 24.7 us -> 22 us
    pallas_call x1, Pallas kernels: 10.2 us -> 7.47 us  [first_apply(): pl.pallas_call(first_kernel, out_shape=(pltpu.VMEM((PEERS, SLOTROWS + IDR...]
where the time goes in v6:
time: 140 us
  blocking collectives  103 us (74%)
  Pallas kernels  22 us (16%)
  starting transfers between devices  10.5 us (8%)
  waiting for transfers between devices  2.72 us (2%)
    all_to_all x3, blocking collectives, exchange(): lax.all_to_all(values, 'sub', split_axis=0, concat_axis=0, tiled=True)  103 us
    ppermute x8, starting transfers between devices, swapped(): return lax.ppermute(values, 'sub', pairs)  10.5 us
    pallas_call x1, Pallas kernels, first_apply(): pl.pallas_call(first_kernel, out_shape=(pltpu.VMEM((PEERS, SLOTROWS + IDR...  7.47 us
    pallas_call x2, Pallas kernels, merge(): pl.pallas_call(functools.partial(merge_kernel, part), out_shape=pltpu.VME...  4.74 us
    pallas_call x1, Pallas kernels, second_apply(): pl.pallas_call(second_kernel, out_shape=pltpu.VMEM((PEERS, SLOTROWS, BLK)...  3.61 us
  transfers between devices with their start and end apart: 8, of which 4 were waited for; matrix products, arithmetic and copies ran while one was open for 0% of the time, Pallas kernels for 3%

profile of v6, /device:TPU:1, one launch (start us, length us, event | category | flops | bytes accessed | tf_op | source)
XLA Modules:
  0.0 139.6 jit_solution(18277760078018836032)
XLA Ops:
  0.6 7.5 %first_apply.1 = (bf16[32,264,128]{2,1,0:T(8,128)(2,1)S(1)}, s32[64]{0:T(128)S(1)}, bf16[8,1024,1024]{2,1,0:T(8,128)(2,1)S(1)}) custom-call(s32[64]{0:T(128)} %bitcast.4, s32[64]{0:T(128)} %block_h.1, bf16[8,64,1024]{2,1,0:T(8,128)(2,1)} %loads.1, bf16[8,1024,1024]{2,1,0:T(8,128)(2,1)} %ops.1), custom_call_target="tpu_custom_call" | custom-call | tf_op jit(solution)/shard_map/first_apply/pallas_call | solution.py:93
  8.1 0.0 copy-start
  8.1 0.0 copy-start.1
  8.1 38.3 %all_to_all.15.received = bf16[32,264,128]{2,1,0:T(8,128)(2,1)S(1)} all-to-all(bf16[32,264,128]{2,1,0:T(8,128)(2,1)S(1)} %get-tuple-element.16), channel_id=1, replica_groups=mesh['sub'=32,'rep'=4] {'sub'}, dimensions={0} | all-to-all | bytes 4325376 | tf_op jit(solution)/shard_map/all_to_all | solution.py:369
  46.4 0.0 copy-done
  46.4 0.0 copy-done.1
  46.4 2.4 %project.1 = (f32[16,64,128]{2,1,0:T(8,128)S(1)}, f32[32,1024]{1,0:T(8,128)S(1)}, f32[32,1024]{1,0:T(8,128)S(1)}, s32[32,128]{1,0:T(8,128)S(1)}, bf16[1024,1024]{1,0:T(8,128)(2,1)S(1)}) custom-call(bf16[32,264,128]{2,1,0:T(8,128)(2,1)S(1)} %all_to_all.15.received, s32[16,128]{1,0:T(8,128)S(1)} %bitcast.2, bf16[2048,1024]{1,0:T(8,128)(2,1)S(1)} %copy-done, ...), custom_call_target="tpu_custom_call" | custom-call | tf_op jit(solution)/shard_map/project/pallas_call | solution.py:206
  48.8 0.5 collective-permute-start
  49.3 1.0 collective-permute-done.refs_1_
  50.3 1.0 collective-permute-start.3
  51.3 0.5 collective-permute-start.2
  51.8 1.8 %collective-permute-start.1 = (bf16[32,1024]{1,0:T(8,128)(2,1)S(1)}, bf16[32,1024]{1,0:T(8,128)(2,1)S(1)}, u32[]{:S(2)}, u32[]{:S(2)}) collective-permute-start(bf16[32,1024]{1,0:T(8,128)(2,1)S(1)} %get-tuple-element.21.after), channel_id=1, source_target_pairs={{0,96},{4,100},{8,104},{12,108},{16,112},{20,116},{24,120},{28,124... | collective-permute-start | bytes 196616 | tf_op jit(solution)/shard_map/ppermute | solution.py:254
  53.6 2.4 %merge.2.refs_4_.first = bf16[1024,1024]{1,0:T(8,128)(2,1)S(1)} custom-call(bf16[1024,1024]{1,0:T(8,128)(2,1)S(1)} %get-tuple-element.22.coarse, bf16[2048,1024]{1,0:T(8,128)(2,1)S(1)} %copy-done, bf16[32,1024]{1,0:T(8,128)(2,1)S(1)} %get-tuple-element.21.after), custom_call_target="tpu_custom_call" | custom-call | tf_op jit(solution)/shard_map/merge/pallas_call | solution.py:147
  56.0 0.0 collective-permute-done.3.refs_3_
  56.0 0.0 collective-permute-done.2.refs_2_
  56.0 0.7 collective-permute-done.1.refs_1_
  56.7 0.8 collective-permute-start.6
  57.6 0.7 collective-permute-start.5
  58.3 1.8 %collective-permute-start.4 = (bf16[32,1024]{1,0:T(8,128)(2,1)S(1)}, bf16[32,1024]{1,0:T(8,128)(2,1)S(1)}, u32[]{:S(2)}, u32[]{:S(2)}) collective-permute-start(bf16[32,1024]{1,0:T(8,128)(2,1)S(1)} %get-tuple-element.24.after), channel_id=1, source_target_pairs={{0,24},{4,28},{8,16},{12,20},{16,8},{20,12},{24,0},{28,4},{32,56},... | collective-permute-start | bytes 196616 | tf_op jit(solution)/shard_map/ppermute | solution.py:254
  60.1 2.4 %merge.3.refs_4_.second = bf16[1024,1024]{1,0:T(8,128)(2,1)S(1)} custom-call(bf16[1024,1024]{1,0:T(8,128)(2,1)S(1)} %get-tuple-element.22.coarse, bf16[2048,1024]{1,0:T(8,128)(2,1)S(1)} %copy-done, bf16[32,1024]{1,0:T(8,128)(2,1)S(1)} %get-tuple-element.24.after), custom_call_target="tpu_custom_call" | custom-call | tf_op jit(solution)/shard_map/merge/pallas_call | solution.py:147
  62.4 0.0 collective-permute-done.6.refs_3_
  62.5 0.0 collective-permute-done.5.refs_2_
  62.5 0.1 collective-permute-done.4.refs_1_
  62.6 3.3 %collective-permute-start.7 = (bf16[32,1024]{1,0:T(8,128)(2,1)S(1)}, bf16[32,1024]{1,0:T(8,128)(2,1)S(1)}, u32[]{:S(2)}, u32[]{:S(2)}) collective-permute-start(bf16[32,1024]{1,0:T(8,128)(2,1)S(1)} %add_parts.5.own), channel_id=1, source_target_pairs={{0,4},{4,0},{8,12},{12,8},{16,20},{20,16},{24,28},{28,24},{32,36},... | collective-permute-start | bytes 196616 | tf_op jit(solution)/shard_map/ppermute | solution.py:254
  66.0 0.9 collective-permute-done.7.other
  66.9 1.7 %start_values.1 = (f32[64,2048]{1,0:T(8,128)}, bf16[32,256,128]{2,1,0:T(8,128)(2,1)S(1)}) custom-call(s32[32,128]{1,0:T(8,128)S(1)} %get-tuple-element.17.ids_v, bf16[32,1024]{1,0:T(8,128)(2,1)S(1)} %add_parts.5.own, bf16[32,1024]{1,0:T(8,128)(2,1)S(1)} %collective-permute-done.7.other, bf16[1024,1024]{1,0:T(8,128)(2,1)S(1)} %merge.2.refs_4_.first, ...), custom_call_target="tpu_custom_call" | custom-call | tf_op jit(solution)/shard_map/start_values/pallas_call | solution.py:306
  68.6 33.3 %all_to_all.16.back = bf16[32,256,128]{2,1,0:T(8,128)(2,1)S(1)} all-to-all(bf16[32,256,128]{2,1,0:T(8,128)(2,1)S(1)} %get-tuple-element.27), channel_id=1, replica_groups=mesh['sub'=32,'rep'=4] {'sub'}, dimensions={0} | all-to-all | bytes 4194304 | tf_op jit(solution)/shard_map/all_to_all | solution.py:369
  101.8 3.6 %second_apply.1 = bf16[32,256,128]{2,1,0:T(8,128)(2,1)S(1)} custom-call(s32[64]{0:T(128)S(1)} %get-tuple-element.26.pos, bf16[32,256,128]{2,1,0:T(8,128)(2,1)S(1)} %all_to_all.16.back, bf16[8,1024,1024]{2,1,0:T(8,128)(2,1)S(1)} %get-tuple-element.28.ops), custom_call_target="tpu_custom_call" | custom-call | tf_op jit(solution)/shard_map/second_apply/pallas_call | solution.py:127
  105.5 31.9 %all_to_all.17.received = bf16[32,256,128]{2,1,0:T(8,128)(2,1)S(1)} all-to-all(bf16[32,256,128]{2,1,0:T(8,128)(2,1)S(1)} %second_apply.1), channel_id=1, replica_groups=mesh['sub'=32,'rep'=4] {'sub'}, dimensions={0} | all-to-all | bytes 4194304 | tf_op jit(solution)/shard_map/all_to_all | solution.py:369
  137.4 2.1 %residual.1 = f32[64,2048]{1,0:T(8,128)} custom-call(s32[32,128]{1,0:T(8,128)S(1)} %get-tuple-element.17.ids_v, bf16[32,256,128]{2,1,0:T(8,128)(2,1)S(1)} %all_to_all.17.received, s32[16,128]{1,0:T(8,128)S(1)} %bitcast.3, f32[16,64,128]{2,1,0:T(8,128)S(1)} %get-tuple-element.29.dual), custom_call_target="tpu_custom_call" | custom-call | tf_op jit(solution)/shard_map/residual/pallas_call | solution.py:351
  (3 shorter events, 0.1 us)
Async XLA Ops:
  8.1 38.3 %copy-start = (bf16[2048,1024]{1,0:T(8,128)(2,1)S(1)}, bf16[2048,1024]{1,0:T(8,128)(2,1)}, u32[]{:S(2)}) copy-start(bf16[2048,1024]{1,0:T(8,128)(2,1)} %basis.5) | copy-start | bytes 12582916
  8.1 38.3 %copy-start.1 = (s32[2048]{0:T(1024)S(1)}, s32[2048]{0:T(1024)}, u32[]{:S(2)}) copy-start(s32[2048]{0:T(1024)} %param.11) | copy-start | bytes 24580
  48.8 1.5 %collective-permute-start = (f32[32,1024]{1,0:T(8,128)S(1)}, f32[32,1024]{1,0:T(8,128)S(1)}, u32[]{:S(2)}, u32[]{:S(2)}) collective-permute-start(f32[32,1024]{1,0:T(8,128)S(1)} %get-tuple-element.19), channel_id=1, source_target_pairs={{0,4},{4,0},{8,12},{12,8},{16,20},{20,16},{24,28},{28,24},{32,36},... | collective-permute-start | bytes 393224 | tf_op jit(solution)/shard_map/ppermute | solution.py:254
  50.3 5.7 %collective-permute-start.3 = (bf16[32,1024]{1,0:T(8,128)(2,1)S(1)}, bf16[32,1024]{1,0:T(8,128)(2,1)S(1)}, u32[]{:S(2)}, u32[]{:S(2)}) collective-permute-start(bf16[32,1024]{1,0:T(8,128)(2,1)S(1)} %get-tuple-element.21.after), channel_id=1, source_target_pairs={{0,64},{4,68},{8,72},{12,76},{16,80},{20,84},{24,88},{28,92},{32,9... | collective-permute-start | bytes 196616 | tf_op jit(solution)/shard_map/ppermute | solution.py:254
  51.3 4.7 %collective-permute-start.2 = (bf16[32,1024]{1,0:T(8,128)(2,1)S(1)}, bf16[32,1024]{1,0:T(8,128)(2,1)S(1)}, u32[]{:S(2)}, u32[]{:S(2)}) collective-permute-start(bf16[32,1024]{1,0:T(8,128)(2,1)S(1)} %get-tuple-element.21.after), channel_id=1, source_target_pairs={{0,32},{4,36},{8,40},{12,44},{16,48},{20,52},{24,56},{28,60},{32,0... | collective-permute-start | bytes 196616 | tf_op jit(solution)/shard_map/ppermute | solution.py:254
  51.8 4.9 %collective-permute-start.1 = (bf16[32,1024]{1,0:T(8,128)(2,1)S(1)}, bf16[32,1024]{1,0:T(8,128)(2,1)S(1)}, u32[]{:S(2)}, u32[]{:S(2)}) collective-permute-start(bf16[32,1024]{1,0:T(8,128)(2,1)S(1)} %get-tuple-element.21.after), channel_id=1, source_target_pairs={{0,96},{4,100},{8,104},{12,108},{16,112},{20,116},{24,120},{28,124... | collective-permute-start | bytes 196616 | tf_op jit(solution)/shard_map/ppermute | solution.py:254
  56.7 5.7 %collective-permute-start.6 = (bf16[32,1024]{1,0:T(8,128)(2,1)S(1)}, bf16[32,1024]{1,0:T(8,128)(2,1)S(1)}, u32[]{:S(2)}, u32[]{:S(2)}) collective-permute-start(bf16[32,1024]{1,0:T(8,128)(2,1)S(1)} %get-tuple-element.24.after), channel_id=1, source_target_pairs={{0,16},{4,20},{8,24},{12,28},{16,0},{20,4},{24,8},{28,12},{32,48},... | collective-permute-start | bytes 196616 | tf_op jit(solution)/shard_map/ppermute | solution.py:254
  57.6 4.9 %collective-permute-start.5 = (bf16[32,1024]{1,0:T(8,128)(2,1)S(1)}, bf16[32,1024]{1,0:T(8,128)(2,1)S(1)}, u32[]{:S(2)}, u32[]{:S(2)}) collective-permute-start(bf16[32,1024]{1,0:T(8,128)(2,1)S(1)} %get-tuple-element.24.after), channel_id=1, source_target_pairs={{0,8},{4,12},{8,0},{12,4},{16,24},{20,28},{24,16},{28,20},{32,40},... | collective-permute-start | bytes 196616 | tf_op jit(solution)/shard_map/ppermute | solution.py:254
  58.3 4.3 %collective-permute-start.4 = (bf16[32,1024]{1,0:T(8,128)(2,1)S(1)}, bf16[32,1024]{1,0:T(8,128)(2,1)S(1)}, u32[]{:S(2)}, u32[]{:S(2)}) collective-permute-start(bf16[32,1024]{1,0:T(8,128)(2,1)S(1)} %get-tuple-element.24.after), channel_id=1, source_target_pairs={{0,24},{4,28},{8,16},{12,20},{16,8},{20,12},{24,0},{28,4},{32,56},... | collective-permute-start | bytes 196616 | tf_op jit(solution)/shard_map/ppermute | solution.py:254
  62.6 4.2 %collective-permute-start.7 = (bf16[32,1024]{1,0:T(8,128)(2,1)S(1)}, bf16[32,1024]{1,0:T(8,128)(2,1)S(1)}, u32[]{:S(2)}, u32[]{:S(2)}) collective-permute-start(bf16[32,1024]{1,0:T(8,128)(2,1)S(1)} %add_parts.5.own), channel_id=1, source_target_pairs={{0,4},{4,0},{8,12},{12,8},{16,20},{20,16},{24,28},{28,24},{32,36},... | collective-permute-start | bytes 196616 | tf_op jit(solution)/shard_map/ppermute | solution.py:254

commit v7 on v6

--- a/solution.py
+++ b/solution.py
@@ -19,7 +19,6 @@
 OB = 16
 MERGE = OB * BLK // 2
 NB = 1024
-IDROWS = 8
 SLOTROWS = CAP * COLS
 BF = jnp.bfloat16
 F32 = jnp.float32
@@ -45,11 +44,15 @@
     return ref.at[p // CAP, pl.ds(pl.multiple_of((p % CAP) * COLS, COLS), COLS)]
 
 
-def first_kernel(owner_h, block_h, loads, ops, out, pos, ops_v, owner, dual_block, count, loads_v, sem, load_sem, idx_sem):
+def block_copy(blocks, out, pos, sem, i):
+    return pltpu.make_async_copy(blocks.at[i], slot(out, pos[i]), sem.at[i])
+
+
+def first_kernel(owner_h, block_h, loads, ops, out, pos, codes, owner, dual_block, count, loads_v, ops_v, blocks, sem, load_sem, idx_sem, out_sem):
     owner_copy = pltpu.make_async_copy(owner_h, owner, idx_sem.at[0])
-    block_copy = pltpu.make_async_copy(block_h, dual_block, idx_sem.at[1])
+    block_id_copy = pltpu.make_async_copy(block_h, dual_block, idx_sem.at[1])
     owner_copy.start()
-    block_copy.start()
+    block_id_copy.start()
     load_copy = pltpu.make_async_copy(loads, loads_v, load_sem)
     copies = [pltpu.make_async_copy(ops.at[s], ops_v.at[s], sem.at[s]) for s in range(NSUB)]
     load_copy.start()
@@ -62,10 +65,8 @@
 
     lax.fori_loop(0, PEERS, zero, 0)
     owner_copy.wait()
-    block_copy.wait()
-    row = lax.broadcasted_iota(jnp.int32, (PEERS, BLK), 0)
-    lane = lax.broadcasted_iota(jnp.int32, (PEERS, BLK), 1)
-    flat = jnp.where(lane < CAP, row * CAP + lane, -1)
+    block_id_copy.wait()
+    lane = lax.broadcasted_iota(jnp.int32, (8, BLK), 1)
 
     def rank(i, ids):
         d = owner[i]
@@ -73,12 +74,10 @@
         count[d] = r + 1
         p = d * CAP + r
         pos[i] = p
-        return jnp.where(flat == p, dual_block[i], ids)
-
-    ids = lax.fori_loop(0, NBLK, rank, jnp.full((PEERS, BLK), -1, jnp.int32))
-    out[:, SLOTROWS : SLOTROWS + IDROWS, :] = jnp.broadcast_to(
-        ids.astype(F32)[:, None, :], (PEERS, IDROWS, BLK)
-    ).astype(BF)
+        return jnp.where(lane == p, dual_block[i], ids)
+
+    ids = lax.fori_loop(0, NBLK, rank, jnp.full((8, BLK), -1, jnp.int32))
+    codes[...] = ids.astype(F32)
     load_copy.wait()
     for s in range(NSUB):
         copies[s].wait()
@@ -86,31 +85,87 @@
             copies[s + AHEAD].start()
         prod = jnp.dot(loads_v[s], ops_v[s], preferred_element_type=F32)
         for j in range(BPS):
-            slot(out, pos[s * BPS + j])[...] = prod[:, j * BLK : (j + 1) * BLK].astype(BF)
+            blocks[s * BPS + j] = prod[:, j * BLK : (j + 1) * BLK].astype(BF)
+        for j in range(BPS):
+            block_copy(blocks, out, pos, out_sem, s * BPS + j).start()
+
+    def finish(i, c):
+        block_copy(blocks, out, pos, out_sem, i).wait()
+        return c
+
+    lax.fori_loop(0, NBLK, finish, 0)
 
 
 def first_apply(owner, dual_block, loads, operators):
     return pl.pallas_call(
         first_kernel,
         out_shape=(
-            pltpu.VMEM((PEERS, SLOTROWS + IDROWS, BLK), BF),
+            pltpu.HBM((PEERS, SLOTROWS, BLK), BF),
             jax.ShapeDtypeStruct((NBLK,), jnp.int32),
-            pltpu.VMEM((NSUB, L, L), BF),
+            jax.ShapeDtypeStruct((8, BLK), F32),
         ),
         in_specs=[HBM] * 4,
-        out_specs=[VMEM, SMEM, VMEM],
+        out_specs=[HBM, SMEM, VMEM],
         scratch_shapes=[
             pltpu.SMEM((NBLK,), jnp.int32),
             pltpu.SMEM((NBLK,), jnp.int32),
             pltpu.SMEM((PEERS,), jnp.int32),
             pltpu.VMEM((NSUB, COLS, L), BF),
+            pltpu.VMEM((NSUB, L, L), BF),
+            pltpu.VMEM((NBLK, COLS, BLK), BF),
             pltpu.SemaphoreType.DMA((NSUB,)),
             pltpu.SemaphoreType.DMA,
             pltpu.SemaphoreType.DMA((2,)),
+            pltpu.SemaphoreType.DMA((NBLK,)),
         ],
-        compiler_params=params(8),
+        compiler_params=params(26),
         name="first_apply",
     )(in_hbm(owner), in_hbm(dual_block), in_hbm(loads), in_hbm(operators))
+
+
+def stack_kernel(*refs):
+    for i, ref in enumerate(refs[:-1]):
+        rows = ref.shape[0]
+        refs[-1][i * rows : (i + 1) * rows] = ref[...]
+
+
+def stack(parts):
+    rows = len(parts) * parts[0].shape[0]
+    return pl.pallas_call(
+        stack_kernel,
+        out_shape=jax.ShapeDtypeStruct((rows, BLK), F32),
+        in_specs=[VMEM] * len(parts),
+        out_specs=VMEM,
+        compiler_params=params(2),
+        name="stack",
+    )(*parts)
+
+
+def pick_kernel(*refs):
+    me = lax.axis_index("sub")
+    row = lax.broadcasted_iota(jnp.int32, (BLK, BLK), 0)
+    lane = lax.broadcasted_iota(jnp.int32, (BLK, BLK), 1)
+    chosen = jnp.where((row == me * CAP + lane) & (lane < CAP), 1.0, 0.0).astype(BF)
+    for ky in range(4):
+        picked = jnp.dot(refs[ky][...].astype(BF), chosen, preferred_element_type=F32)
+        for kx in range(4):
+            for kc in range(2):
+                k = kx * 8 + ky * 2 + kc
+                r = (kx * 2 + kc) * 8
+                refs[4][k : k + 1, :] = picked[r : r + 1, :].astype(jnp.int32)
+
+
+def gather_ids(codes):
+    codes = stack([codes, swapped(codes, 0, 0, 1)])
+    codes = stack([codes] + [swapped(codes, k, 0, 0) for k in (1, 2, 3)])
+    return pl.pallas_call(
+        pick_kernel,
+        out_shape=jax.ShapeDtypeStruct((PEERS, BLK), jnp.int32),
+        in_specs=[VMEM] * 4,
+        out_specs=VMEM,
+        compiler_params=params(2),
+        name="pick",
+    )(codes, *[swapped(codes, 0, k, 0) for k in (1, 2, 3)])
 
 
 def second_kernel(pos, back, ops, out, local):
@@ -160,9 +215,11 @@
 
 
 def add_slots(received, ids, totals):
+    me = lax.axis_index("sub")
+
     def peer(p, c):
         for q in range(CAP):
-            g = ids[p, q]
+            g = ids[p ^ me, q]
             g = jnp.where(g < 0, OB, g)
             totals[q][g] = totals[q][g] + received[p, q * COLS : (q + 1) * COLS, :].astype(F32)
         return c
@@ -177,14 +234,13 @@
 TOTALS = [pltpu.VMEM((OB + 1, COLS, BLK), F32)] * CAP
 
 
-def project_kernel(received, scale, basis, coarse, dual, keep, send, ids_out, coarse_v, t0, t1, t2, t3, narrow, coeff, idv, ids, sem, coarse_sem):
+def project_kernel(ids_v, received, scale, basis, coarse, dual, keep, send, basis_v, coarse_v, t0, t1, t2, t3, narrow, coeff, ids, sem, basis_sem, coarse_sem):
+    basis_copy = pltpu.make_async_copy(basis, basis_v, basis_sem)
+    basis_copy.start()
     coarse_copy = pltpu.make_async_copy(coarse, coarse_v, coarse_sem)
-    coarse_copy.start()
     totals = (t0, t1, t2, t3)
-    idv[...] = received[:, SLOTROWS : SLOTROWS + IDROWS, :].astype(F32)[:, 0, :].astype(jnp.int32)
-    ids_copy = pltpu.make_async_copy(idv, ids, sem)
+    ids_copy = pltpu.make_async_copy(ids_v, ids, sem)
     ids_copy.start()
-    ids_out[...] = idv[...]
     zero_totals(totals)
     ids_copy.wait()
     add_slots(received, ids, totals)
@@ -193,7 +249,9 @@
         owned = sum_totals(totals, b) * weight[b : b + 1, :]
         dual[b] = owned
         narrow[:, b * BLK : (b + 1) * BLK] = owned.astype(BF)
-    product = jnp.dot(narrow[...], basis[...], preferred_element_type=F32)
+    basis_copy.wait()
+    coarse_copy.start()
+    product = jnp.dot(narrow[...], basis_v[...], preferred_element_type=F32)
     coeff[0] = product[:HALF]
     coeff[1] = product[HALF:]
     core = lax.axis_index("sub") % 2
@@ -202,30 +260,30 @@
     coarse_copy.wait()
 
 
-def project(received, scale, basis, coarse):
+def project(ids, received, scale, basis, coarse):
     return pl.pallas_call(
         project_kernel,
         out_shape=(
             pltpu.VMEM((OB, COLS, BLK), F32),
             pltpu.VMEM((HALF, NB), F32),
             pltpu.VMEM((HALF, NB), F32),
-            pltpu.VMEM((PEERS, BLK), jnp.int32),
+            pltpu.VMEM((OB * BLK, NB), BF),
             pltpu.VMEM((NB, NB), BF),
         ),
-        in_specs=[VMEM] * 3 + [HBM],
+        in_specs=[VMEM] * 3 + [HBM] * 2,
         out_specs=[VMEM] * 5,
         scratch_shapes=TOTALS
         + [
             pltpu.VMEM((COLS, OB * BLK), BF),
             pltpu.VMEM((2, HALF, NB), F32),
-            pltpu.VMEM((PEERS, BLK), jnp.int32),
             pltpu.SMEM((PEERS, BLK), jnp.int32),
+            pltpu.SemaphoreType.DMA,
             pltpu.SemaphoreType.DMA,
             pltpu.SemaphoreType.DMA,
         ],
         compiler_params=params(8),
         name="project",
-    )(in_vmem(received), scale, in_vmem(basis), in_hbm(coarse))
+    )(in_vmem(ids), in_vmem(received), scale, in_hbm(basis), in_hbm(coarse))
 
 
 def add_kernel(count, inputs, *refs):
@@ -273,7 +331,8 @@
 def start_kernel(ids_v, own, other, first, second, start, out, coeff, blocks, value, ids, sem, ids_sem):
     ids_copy = pltpu.make_async_copy(ids_v, ids, ids_sem)
     ids_copy.start()
-    core = lax.axis_index("sub") % 2
+    me = lax.axis_index("sub")
+    core = me % 2
     coeff[core] = own[...]
     coeff[1 - core] = other[...]
     copies = []
@@ -293,7 +352,7 @@
 
     def peer(p, c):
         for q in range(CAP):
-            g = jnp.maximum(ids[p, q], 0)
+            g = jnp.maximum(ids[p ^ me, q], 0)
             out[p, q * COLS : (q + 1) * COLS, :] = blocks[g]
         return c
 
@@ -371,12 +430,13 @@
 
 def per_device(loads, operators, owner, dual_block, scale_index, basis, coarse):
     scale = scale_index.reshape(OB, BLK)
-    packed, pos, ops_v = first_apply(owner.reshape(NBLK), dual_block, loads, operators)
+    packed, pos, codes = first_apply(owner.reshape(NBLK), dual_block, loads, operators)
+    ids = gather_ids(codes)
     received = exchange(packed)
-    dual, keep, send, ids, coarse_v = project(received, scale, basis, coarse)
-    own, other, first, second = sum_over_owners(keep, send, coarse_v, basis)
+    dual, keep, send, basis_v, coarse_v = project(ids, received, scale, basis, coarse)
+    own, other, first, second = sum_over_owners(keep, send, coarse_v, basis_v)
     start, requested = start_values(ids, own, other, first, second)
-    again = second_apply(pos, exchange(requested), ops_v)
+    again = second_apply(pos, exchange(requested), operators)
     return (start, residual(ids, exchange(again), scale, dual))
 
 

time: 140 us -> 149 us (1.064)
  blocking collectives: 103 us -> 65 us
  waiting for transfers between devices: 2.72 us -> 29.3 us
  starting transfers between devices: 10.5 us -> 28.1 us
  Pallas kernels: 22 us -> 25.5 us
    all_to_all x3 -> x2, blocking collectives: 103 us -> 65 us  [exchange(): lax.all_to_all(values, 'sub', split_axis=0, concat_axis=0, tiled=True)]
    ppermute x8 -> x15, waiting for transfers between devices: 2.72 us -> 29.2 us  [swapped(): return lax.ppermute(values, 'sub', pairs)]
    ppermute x8 -> x15, starting transfers between devices: 10.5 us -> 19.5 us  [swapped(): return lax.ppermute(values, 'sub', pairs)]
    all_to_all x0 -> x1, starting transfers between devices: none -> 8.61 us  [exchange(): lax.all_to_all(values, 'sub', split_axis=0, concat_axis=0, tiled=True)]
    pallas_call x1 -> x4, Pallas kernels: 7.47 us -> 9.56 us  [the longest x1 9.4 us: first_apply(): pl.pallas_call(first_kernel, out_shape=(pltpu.HBM((PEERS, SLOTROWS, BLK),...]
  transfers between devices with their start and end apart: 8 -> 16, of which waited for: 4 -> 9; matrix products, arithmetic and copies ran while one was open for 0% -> 0% of each run, Pallas kernels for 3% -> 3%
where the time goes in v7:
time: 149 us
  blocking collectives  65 us (44%)
  waiting for transfers between devices  29.3 us (20%)
  starting transfers between devices  28.1 us (19%)
  Pallas kernels  25.5 us (17%)
    all_to_all x2, blocking collectives, exchange(): lax.all_to_all(values, 'sub', split_axis=0, concat_axis=0, tiled=True)  65 us
    ppermute x15, waiting for transfers between devices, swapped(): return lax.ppermute(values, 'sub', pairs)  29.2 us
    ppermute x15, starting transfers between devices, swapped(): return lax.ppermute(values, 'sub', pairs)  19.5 us
    pallas_call x1, Pallas kernels, first_apply(): pl.pallas_call(first_kernel, out_shape=(pltpu.HBM((PEERS, SLOTROWS, BLK),...  9.4 us
    all_to_all x1, starting transfers between devices, exchange(): lax.all_to_all(values, 'sub', split_axis=0, concat_axis=0, tiled=True)  8.61 us
    pallas_call x2, Pallas kernels, merge(): pl.pallas_call(functools.partial(merge_kernel, part), out_shape=pltpu.VME...  4.73 us
    pallas_call x1, Pallas kernels, project(): pl.pallas_call(project_kernel, out_shape=(pltpu.VMEM((OB, COLS, BLK), F32...  3.81 us
    pallas_call x1, Pallas kernels, second_apply(): pl.pallas_call(second_kernel, out_shape=pltpu.VMEM((PEERS, SLOTROWS, BLK)...  3.62 us
  transfers between devices with their start and end apart: 16, of which 9 were waited for; matrix products, arithmetic and copies ran while one was open for 0% of the time, Pallas kernels for 3%

profile of v7, /device:TPU:1, one launch (start us, length us, event | category | flops | bytes accessed | tf_op | source)
XLA Modules:
  0.0 148.8 jit_solution(12199595648488946292)
XLA Ops:
  0.6 9.4 %first_apply.1 = (bf16[32,256,128]{2,1,0:T(8,128)(2,1)}, s32[64]{0:T(128)S(1)}, f32[8,128]{1,0:T(8,128)S(1)}) custom-call(s32[64]{0:T(128)} %bitcast.6, s32[64]{0:T(128)} %block_h.1, bf16[8,64,1024]{2,1,0:T(8,128)(2,1)} %loads.1, bf16[8,1024,1024]{2,1,0:T(8,128)(2,1)} %ops.3), custom_call_target="tpu_custom_call" | custom-call | tf_op jit(solution)/shard_map/first_apply/pallas_call | solution.py:100
  10.0 0.0 copy-start
  10.0 8.6 %all-to-all-start = ((bf16[32,256,128]{2,1,0:T(8,128)(2,1)}), bf16[32,256,128]{2,1,0:T(8,128)(2,1)S(1)}, u32[]{:S(2)}, u32[]{:S(2)}) async-start(bf16[32,256,128]{2,1,0:T(8,128)(2,1)} %get-tuple-element.17), calls=%async_computation | async-start | bytes 4194304 | tf_op jit(solution)/shard_map/all_to_all | solution.py:428
  18.7 0.3 collective-permute-start
  19.0 0.9 collective-permute-done.refs_1_
  19.9 2.7 %collective-permute-start.3 = (f32[16,128]{1,0:T(8,128)S(1)}, f32[16,128]{1,0:T(8,128)S(1)}, u32[]{:S(2)}, u32[]{:S(2)}) collective-permute-start(f32[16,128]{1,0:T(8,128)S(1)} %stack.2.refs_0_), channel_id=1, source_target_pairs={{0,96},{4,100},{8,104},{12,108},{16,112},{20,116},{24,120},{28,124... | collective-permute-start | bytes 24584 | tf_op jit(solution)/shard_map/ppermute | solution.py:312
  22.6 0.5 collective-permute-start.2
  23.1 0.1 collective-permute-start.1
  23.2 18.8 %collective-permute-done.3.refs_3_ = f32[16,128]{1,0:T(8,128)S(1)} collective-permute-done((f32[16,128]{1,0:T(8,128)S(1)}, f32[16,128]{1,0:T(8,128)S(1)}, u32[]{:S(2)}, u32[]{:S(2)}) %collective-permute-start.3) | collective-permute-done | bytes 8224 | tf_op jit(solution)/shard_map/ppermute | solution.py:312
  42.0 3.2 %collective-permute-done.2.refs_2_ = f32[16,128]{1,0:T(8,128)S(1)} collective-permute-done((f32[16,128]{1,0:T(8,128)S(1)}, f32[16,128]{1,0:T(8,128)S(1)}, u32[]{:S(2)}, u32[]{:S(2)}) %collective-permute-start.2) | collective-permute-done | bytes 8224 | tf_op jit(solution)/shard_map/ppermute | solution.py:312
  45.2 0.0 collective-permute-done.1.refs_1_
  45.2 2.4 %collective-permute-start.6 = (f32[64,128]{1,0:T(8,128)S(1)}, f32[64,128]{1,0:T(8,128)S(1)}, u32[]{:S(2)}, u32[]{:S(2)}) collective-permute-start(f32[64,128]{1,0:T(8,128)S(1)} %stack.3.refs_0_), channel_id=1, source_target_pairs={{0,24},{4,28},{8,16},{12,20},{16,8},{20,12},{24,0},{28,4},{32,56},... | collective-permute-start | bytes 98312 | tf_op jit(solution)/shard_map/ppermute | solution.py:312
  47.6 0.8 collective-permute-start.5
  48.4 0.0 collective-permute-start.4
  48.4 0.7 collective-permute-done.6.refs_3_
  49.1 2.7 %collective-permute-done.5.refs_2_ = f32[64,128]{1,0:T(8,128)S(1)} collective-permute-done((f32[64,128]{1,0:T(8,128)S(1)}, f32[64,128]{1,0:T(8,128)S(1)}, u32[]{:S(2)}, u32[]{:S(2)}) %collective-permute-start.5) | collective-permute-done | bytes 32800 | tf_op jit(solution)/shard_map/ppermute | solution.py:312
  51.9 0.0 collective-permute-done.4.refs_1_
  51.9 0.2 pick.1.ids_v
  52.0 0.0 all-to-all-done.received
  52.0 0.0 copy-done
  52.0 3.8 %project.1 = (f32[16,64,128]{2,1,0:T(8,128)S(1)}, f32[32,1024]{1,0:T(8,128)S(1)}, f32[32,1024]{1,0:T(8,128)S(1)}, bf16[2048,1024]{1,0:T(8,128)(2,1)S(1)}, bf16[1024,1024]{1,0:T(8,128)(2,1)S(1)}) custom-call(s32[32,128]{1,0:T(8,128)S(1)} %pick.1.ids_v, bf16[32,256,128]{2,1,0:T(8,128)(2,1)S(1)} %all-to-all-done.received, s32[16,128]{1,0:T(8,128)S(1)} %bitcast.4, ...), custom_call_target="tpu_custom_call" | custom-call | tf_op jit(solution)/shard_map/project/pallas_call | solution.py:264
  55.9 2.5 %collective-permute-start.7 = (f32[32,1024]{1,0:T(8,128)S(1)}, f32[32,1024]{1,0:T(8,128)S(1)}, u32[]{:S(2)}, u32[]{:S(2)}) collective-permute-start(f32[32,1024]{1,0:T(8,128)S(1)} %get-tuple-element.19), channel_id=1, source_target_pairs={{0,4},{4,0},{8,12},{12,8},{16,20},{20,16},{24,28},{28,24},{32,36},... | collective-permute-start | bytes 393224 | tf_op jit(solution)/shard_map/ppermute | solution.py:312
  58.3 1.0 collective-permute-done.7.refs_1_
  59.3 1.4 collective-permute-start.10
  60.8 0.3 collective-permute-start.9
  61.1 1.6 %collective-permute-start.8 = (bf16[32,1024]{1,0:T(8,128)(2,1)S(1)}, bf16[32,1024]{1,0:T(8,128)(2,1)S(1)}, u32[]{:S(2)}, u32[]{:S(2)}) collective-permute-start(bf16[32,1024]{1,0:T(8,128)(2,1)S(1)} %get-tuple-element.21.after), channel_id=1, source_target_pairs={{0,96},{4,100},{8,104},{12,108},{16,112},{20,116},{24,120},{28,124... | collective-permute-start | bytes 196616 | tf_op jit(solution)/shard_map/ppermute | solution.py:312
  62.7 0.0 slice-start
  62.7 0.0 slice-start.1
  62.7 2.4 %merge.2.refs_4_.first = bf16[1024,1024]{1,0:T(8,128)(2,1)S(1)} custom-call(bf16[1024,1024]{1,0:T(8,128)(2,1)S(1)} %get-tuple-element.22.coarse, bf16[2048,1024]{1,0:T(8,128)(2,1)S(1)} %get-tuple-element.23.basis, bf16[32,1024]{1,0:T(8,128)(2,1)S(1)} %get-tuple-element.21.after), custom_call_target="tpu_custom_call" | custom-call | tf_op jit(solution)/shard_map/merge/pallas_call | solution.py:202
  65.1 0.0 collective-permute-done.10.refs_3_
  65.1 0.0 collective-permute-done.9.refs_2_
  65.1 0.6 collective-permute-done.8.refs_1_
  65.7 0.0 slice-start.2
  65.7 1.8 %collective-permute-start.13 = (bf16[32,1024]{1,0:T(8,128)(2,1)S(1)}, bf16[32,1024]{1,0:T(8,128)(2,1)S(1)}, u32[]{:S(2)}, u32[]{:S(2)}) collective-permute-start(bf16[32,1024]{1,0:T(8,128)(2,1)S(1)} %get-tuple-element.25.after), channel_id=1, source_target_pairs={{0,16},{4,20},{8,24},{12,28},{16,0},{20,4},{24,8},{28,12},{32,48},... | collective-permute-start | bytes 196616 | tf_op jit(solution)/shard_map/ppermute | solution.py:312
  67.5 0.0 collective-permute-start.12
  67.5 1.5 %collective-permute-start.11 = (bf16[32,1024]{1,0:T(8,128)(2,1)S(1)}, bf16[32,1024]{1,0:T(8,128)(2,1)S(1)}, u32[]{:S(2)}, u32[]{:S(2)}) collective-permute-start(bf16[32,1024]{1,0:T(8,128)(2,1)S(1)} %get-tuple-element.25.after), channel_id=1, source_target_pairs={{0,24},{4,28},{8,16},{12,20},{16,8},{20,12},{24,0},{28,4},{32,56},... | collective-permute-start | bytes 196616 | tf_op jit(solution)/shard_map/ppermute | solution.py:312
  69.0 2.4 %merge.3.refs_4_.second = bf16[1024,1024]{1,0:T(8,128)(2,1)S(1)} custom-call(bf16[1024,1024]{1,0:T(8,128)(2,1)S(1)} %get-tuple-element.22.coarse, bf16[2048,1024]{1,0:T(8,128)(2,1)S(1)} %get-tuple-element.23.basis, bf16[32,1024]{1,0:T(8,128)(2,1)S(1)} %get-tuple-element.25.after), custom_call_target="tpu_custom_call" | custom-call | tf_op jit(solution)/shard_map/merge/pallas_call | solution.py:202
  71.4 0.0 collective-permute-done.13.refs_3_
  71.4 0.0 collective-permute-done.12.refs_2_
  71.4 0.4 collective-permute-done.11.refs_1_
  71.9 0.0 slice-start.3
  71.9 3.5 %collective-permute-start.14 = (bf16[32,1024]{1,0:T(8,128)(2,1)S(1)}, bf16[32,1024]{1,0:T(8,128)(2,1)S(1)}, u32[]{:S(2)}, u32[]{:S(2)}) collective-permute-start(bf16[32,1024]{1,0:T(8,128)(2,1)S(1)} %add_parts.5.own), channel_id=1, source_target_pairs={{0,4},{4,0},{8,12},{12,8},{16,20},{20,16},{24,28},{28,24},{32,36},... | collective-permute-start | bytes 196616 | tf_op jit(solution)/shard_map/ppermute | solution.py:312
  75.4 0.9 collective-permute-done.14.other
  76.3 1.6 %start_values.1 = (f32[64,2048]{1,0:T(8,128)}, bf16[32,256,128]{2,1,0:T(8,128)(2,1)S(1)}) custom-call(s32[32,128]{1,0:T(8,128)S(1)} %pick.1.ids_v, bf16[32,1024]{1,0:T(8,128)(2,1)S(1)} %add_parts.5.own, bf16[32,1024]{1,0:T(8,128)(2,1)S(1)} %collective-permute-done.14.other, bf16[1024,1024]{1,0:T(8,128)(2,1)S(1)} %merge.2.refs_4_.first, ...), custom_call_target="tpu_custom_call" | custom-call | tf_op jit(solution)/shard_map/start_values/pallas_call | solution.py:365
  77.9 33.1 %all_to_all.15.back = bf16[32,256,128]{2,1,0:T(8,128)(2,1)S(1)} all-to-all(bf16[32,256,128]{2,1,0:T(8,128)(2,1)S(1)} %get-tuple-element.28), channel_id=1, replica_groups=mesh['sub'=32,'rep'=4] {'sub'}, dimensions={0} | all-to-all | bytes 4194304 | tf_op jit(solution)/shard_map/all_to_all | solution.py:428
  111.0 0.0 slice-done
  111.0 0.0 slice-done.1
  111.0 0.0 slice-done.2
  111.0 0.0 slice-done.3
  111.0 3.6 %second_apply.1 = bf16[32,256,128]{2,1,0:T(8,128)(2,1)S(1)} custom-call(s32[64]{0:T(128)S(1)} %get-tuple-element.27.pos, bf16[32,256,128]{2,1,0:T(8,128)(2,1)S(1)} %all_to_all.15.back, bf16[8,1024,1024]{2,1,0:T(8,128)(2,1)S(1)} %bitcast.3), custom_call_target="tpu_custom_call" | custom-call | tf_op jit(solution)/shard_map/second_apply/pallas_call | solution.py:182
  114.7 31.9 %all_to_all.16.received = bf16[32,256,128]{2,1,0:T(8,128)(2,1)S(1)} all-to-all(bf16[32,256,128]{2,1,0:T(8,128)(2,1)S(1)} %second_apply.1), channel_id=1, replica_groups=mesh['sub'=32,'rep'=4] {'sub'}, dimensions={0} | all-to-all | bytes 4194304 | tf_op jit(solution)/shard_map/all_to_all | solution.py:428
  146.6 2.1 %residual.1 = f32[64,2048]{1,0:T(8,128)} custom-call(s32[32,128]{1,0:T(8,128)S(1)} %pick.1.ids_v, bf16[32,256,128]{2,1,0:T(8,128)(2,1)S(1)} %all_to_all.16.received, s32[16,128]{1,0:T(8,128)S(1)} %bitcast.5, f32[16,64,128]{2,1,0:T(8,128)S(1)} %get-tuple-element.29.dual), custom_call_target="tpu_custom_call" | custom-call | tf_op jit(solution)/shard_map/residual/pallas_call | solution.py:410
  (6 shorter events, 0.1 us)
Async XLA Ops:
  10.0 42.0 %copy-start = (s32[2048]{0:T(1024)S(1)}, s32[2048]{0:T(1024)}, u32[]{:S(2)}) copy-start(s32[2048]{0:T(1024)} %param.11) | copy-start | bytes 24580
  10.0 42.0 %all-to-all-start = ((bf16[32,256,128]{2,1,0:T(8,128)(2,1)}), bf16[32,256,128]{2,1,0:T(8,128)(2,1)S(1)}, u32[]{:S(2)}, u32[]{:S(2)}) async-start(bf16[32,256,128]{2,1,0:T(8,128)(2,1)} %get-tuple-element.17), calls=%async_computation | async-start | bytes 4194304 | tf_op jit(solution)/shard_map/all_to_all | solution.py:428
  18.7 1.2 collective-permute-start
  19.9 22.1 %collective-permute-start.3 = (f32[16,128]{1,0:T(8,128)S(1)}, f32[16,128]{1,0:T(8,128)S(1)}, u32[]{:S(2)}, u32[]{:S(2)}) collective-permute-start(f32[16,128]{1,0:T(8,128)S(1)} %stack.2.refs_0_), channel_id=1, source_target_pairs={{0,96},{4,100},{8,104},{12,108},{16,112},{20,116},{24,120},{28,124... | collective-permute-start | bytes 24584 | tf_op jit(solution)/shard_map/ppermute | solution.py:312
  22.6 22.6 %collective-permute-start.2 = (f32[16,128]{1,0:T(8,128)S(1)}, f32[16,128]{1,0:T(8,128)S(1)}, u32[]{:S(2)}, u32[]{:S(2)}) collective-permute-start(f32[16,128]{1,0:T(8,128)S(1)} %stack.2.refs_0_), channel_id=1, source_target_pairs={{0,64},{4,68},{8,72},{12,76},{16,80},{20,84},{24,88},{28,92},{32,9... | collective-permute-start | bytes 24584 | tf_op jit(solution)/shard_map/ppermute | solution.py:312
  23.1 22.1 %collective-permute-start.1 = (f32[16,128]{1,0:T(8,128)S(1)}, f32[16,128]{1,0:T(8,128)S(1)}, u32[]{:S(2)}, u32[]{:S(2)}) collective-permute-start(f32[16,128]{1,0:T(8,128)S(1)} %stack.2.refs_0_), channel_id=1, source_target_pairs={{0,32},{4,36},{8,40},{12,44},{16,48},{20,52},{24,56},{28,60},{32,0... | collective-permute-start | bytes 24584 | tf_op jit(solution)/shard_map/ppermute | solution.py:312
  45.2 4.0 %collective-permute-start.6 = (f32[64,128]{1,0:T(8,128)S(1)}, f32[64,128]{1,0:T(8,128)S(1)}, u32[]{:S(2)}, u32[]{:S(2)}) collective-permute-start(f32[64,128]{1,0:T(8,128)S(1)} %stack.3.refs_0_), channel_id=1, source_target_pairs={{0,24},{4,28},{8,16},{12,20},{16,8},{20,12},{24,0},{28,4},{32,56},... | collective-permute-start | bytes 98312 | tf_op jit(solution)/shard_map/ppermute | solution.py:312
  47.6 4.3 %collective-permute-start.5 = (f32[64,128]{1,0:T(8,128)S(1)}, f32[64,128]{1,0:T(8,128)S(1)}, u32[]{:S(2)}, u32[]{:S(2)}) collective-permute-start(f32[64,128]{1,0:T(8,128)S(1)} %stack.3.refs_0_), channel_id=1, source_target_pairs={{0,16},{4,20},{8,24},{12,28},{16,0},{20,4},{24,8},{28,12},{32,48},... | collective-permute-start | bytes 98312 | tf_op jit(solution)/shard_map/ppermute | solution.py:312
  48.4 3.4 %collective-permute-start.4 = (f32[64,128]{1,0:T(8,128)S(1)}, f32[64,128]{1,0:T(8,128)S(1)}, u32[]{:S(2)}, u32[]{:S(2)}) collective-permute-start(f32[64,128]{1,0:T(8,128)S(1)} %stack.3.refs_0_), channel_id=1, source_target_pairs={{0,8},{4,12},{8,0},{12,4},{16,24},{20,28},{24,16},{28,20},{32,40},... | collective-permute-start | bytes 98312 | tf_op jit(solution)/shard_map/ppermute | solution.py:312
  55.9 3.5 %collective-permute-start.7 = (f32[32,1024]{1,0:T(8,128)S(1)}, f32[32,1024]{1,0:T(8,128)S(1)}, u32[]{:S(2)}, u32[]{:S(2)}) collective-permute-start(f32[32,1024]{1,0:T(8,128)S(1)} %get-tuple-element.19), channel_id=1, source_target_pairs={{0,4},{4,0},{8,12},{12,8},{16,20},{20,16},{24,28},{28,24},{32,36},... | collective-permute-start | bytes 393224 | tf_op jit(solution)/shard_map/ppermute | solution.py:312
  59.3 5.7 %collective-permute-start.10 = (bf16[32,1024]{1,0:T(8,128)(2,1)S(1)}, bf16[32,1024]{1,0:T(8,128)(2,1)S(1)}, u32[]{:S(2)}, u32[]{:S(2)}) collective-permute-start(bf16[32,1024]{1,0:T(8,128)(2,1)S(1)} %get-tuple-element.21.after), channel_id=1, source_target_pairs={{0,64},{4,68},{8,72},{12,76},{16,80},{20,84},{24,88},{28,92},{32,9... | collective-permute-start | bytes 196616 | tf_op jit(solution)/shard_map/ppermute | solution.py:312
  60.8 4.3 %collective-permute-start.9 = (bf16[32,1024]{1,0:T(8,128)(2,1)S(1)}, bf16[32,1024]{1,0:T(8,128)(2,1)S(1)}, u32[]{:S(2)}, u32[]{:S(2)}) collective-permute-start(bf16[32,1024]{1,0:T(8,128)(2,1)S(1)} %get-tuple-element.21.after), channel_id=1, source_target_pairs={{0,32},{4,36},{8,40},{12,44},{16,48},{20,52},{24,56},{28,60},{32,0... | collective-permute-start | bytes 196616 | tf_op jit(solution)/shard_map/ppermute | solution.py:312
  61.1 4.6 %collective-permute-start.8 = (bf16[32,1024]{1,0:T(8,128)(2,1)S(1)}, bf16[32,1024]{1,0:T(8,128)(2,1)S(1)}, u32[]{:S(2)}, u32[]{:S(2)}) collective-permute-start(bf16[32,1024]{1,0:T(8,128)(2,1)S(1)} %get-tuple-element.21.after), channel_id=1, source_target_pairs={{0,96},{4,100},{8,104},{12,108},{16,112},{20,116},{24,120},{28,124... | collective-permute-start | bytes 196616 | tf_op jit(solution)/shard_map/ppermute | solution.py:312
  62.7 48.3 %slice-start = ((s8[16777216]{0:T(1024)(128)(4,1)}), s8[4194304]{0:T(1024)(128)(4,1)S(1)}, s32[]{:S(2)}) async-start(s8[16777216]{0:T(1024)(128)(4,1)} %bitcast.2), calls=%async_computation.3 | async-start | bytes 8388608
  62.7 48.3 %slice-start.1 = ((s8[16777216]{0:T(1024)(128)(4,1)}), s8[4194304]{0:T(1024)(128)(4,1)S(1)}, s32[]{:S(2)}) async-start(s8[16777216]{0:T(1024)(128)(4,1)} %bitcast.2), calls=%async_computation.4 | async-start | bytes 8388608
  65.7 45.3 %slice-start.2 = ((s8[16777216]{0:T(1024)(128)(4,1)}), s8[4194304]{0:T(1024)(128)(4,1)S(1)}, s32[]{:S(2)}) async-start(s8[16777216]{0:T(1024)(128)(4,1)} %bitcast.2), calls=%async_computation.5 | async-start | bytes 8388608
  65.7 5.7 %collective-permute-start.13 = (bf16[32,1024]{1,0:T(8,128)(2,1)S(1)}, bf16[32,1024]{1,0:T(8,128)(2,1)S(1)}, u32[]{:S(2)}, u32[]{:S(2)}) collective-permute-start(bf16[32,1024]{1,0:T(8,128)(2,1)S(1)} %get-tuple-element.25.after), channel_id=1, source_target_pairs={{0,16},{4,20},{8,24},{12,28},{16,0},{20,4},{24,8},{28,12},{32,48},... | collective-permute-start | bytes 196616 | tf_op jit(solution)/shard_map/ppermute | solution.py:312
  67.5 3.9 %collective-permute-start.12 = (bf16[32,1024]{1,0:T(8,128)(2,1)S(1)}, bf16[32,1024]{1,0:T(8,128)(2,1)S(1)}, u32[]{:S(2)}, u32[]{:S(2)}) collective-permute-start(bf16[32,1024]{1,0:T(8,128)(2,1)S(1)} %get-tuple-element.25.after), channel_id=1, source_target_pairs={{0,8},{4,12},{8,0},{12,4},{16,24},{20,28},{24,16},{28,20},{32,40},... | collective-permute-start | bytes 196616 | tf_op jit(solution)/shard_map/ppermute | solution.py:312
  67.5 4.3 %collective-permute-start.11 = (bf16[32,1024]{1,0:T(8,128)(2,1)S(1)}, bf16[32,1024]{1,0:T(8,128)(2,1)S(1)}, u32[]{:S(2)}, u32[]{:S(2)}) collective-permute-start(bf16[32,1024]{1,0:T(8,128)(2,1)S(1)} %get-tuple-element.25.after), channel_id=1, source_target_pairs={{0,24},{4,28},{8,16},{12,20},{16,8},{20,12},{24,0},{28,4},{32,56},... | collective-permute-start | bytes 196616 | tf_op jit(solution)/shard_map/ppermute | solution.py:312
  71.9 39.1 %slice-start.3 = ((s8[16777216]{0:T(1024)(128)(4,1)}), s8[4194304]{0:T(1024)(128)(4,1)S(1)}, s32[]{:S(2)}) async-start(s8[16777216]{0:T(1024)(128)(4,1)} %bitcast.2), calls=%async_computation.6 | async-start | bytes 8388608
  71.9 4.4 %collective-permute-start.14 = (bf16[32,1024]{1,0:T(8,128)(2,1)S(1)}, bf16[32,1024]{1,0:T(8,128)(2,1)S(1)}, u32[]{:S(2)}, u32[]{:S(2)}) collective-permute-start(bf16[32,1024]{1,0:T(8,128)(2,1)S(1)} %add_parts.5.own), channel_id=1, source_target_pairs={{0,4},{4,0},{8,12},{12,8},{16,20},{20,16},{24,28},{28,24},{32,36},... | collective-permute-start | bytes 196616 | tf_op jit(solution)/shard_map/ppermute | solution.py:312

commit v8 on v6

--- a/solution.py
+++ b/solution.py
@@ -26,7 +26,7 @@
 HBM = pl.BlockSpec(memory_space=pl.ANY)
 SMEM = pl.BlockSpec(memory_space=pltpu.SMEM)
 VMEM = pl.BlockSpec(memory_space=pltpu.VMEM)
-AHEAD = 4
+AHEAD = 5
 
 
 def params(mib):
@@ -50,10 +50,12 @@
     block_copy = pltpu.make_async_copy(block_h, dual_block, idx_sem.at[1])
     owner_copy.start()
     block_copy.start()
-    load_copy = pltpu.make_async_copy(loads, loads_v, load_sem)
+    load_copies = [
+        pltpu.make_async_copy(loads.at[s], loads_v.at[s], load_sem.at[s]) for s in range(NSUB)
+    ]
     copies = [pltpu.make_async_copy(ops.at[s], ops_v.at[s], sem.at[s]) for s in range(NSUB)]
-    load_copy.start()
     for s in range(AHEAD):
+        load_copies[s].start()
         copies[s].start()
 
     def zero(i, c):
@@ -79,10 +81,11 @@
     out[:, SLOTROWS : SLOTROWS + IDROWS, :] = jnp.broadcast_to(
         ids.astype(F32)[:, None, :], (PEERS, IDROWS, BLK)
     ).astype(BF)
-    load_copy.wait()
     for s in range(NSUB):
+        load_copies[s].wait()
         copies[s].wait()
         if s + AHEAD < NSUB:
+            load_copies[s + AHEAD].start()
             copies[s + AHEAD].start()
         prod = jnp.dot(loads_v[s], ops_v[s], preferred_element_type=F32)
         for j in range(BPS):
@@ -105,7 +108,7 @@
             pltpu.SMEM((PEERS,), jnp.int32),
             pltpu.VMEM((NSUB, COLS, L), BF),
             pltpu.SemaphoreType.DMA((NSUB,)),
-            pltpu.SemaphoreType.DMA,
+            pltpu.SemaphoreType.DMA((NSUB,)),
             pltpu.SemaphoreType.DMA((2,)),
         ],
         compiler_params=params(8),
@@ -113,12 +116,10 @@
     )(in_hbm(owner), in_hbm(dual_block), in_hbm(loads), in_hbm(operators))
 
 
-def second_kernel(pos, back, ops, out, local):
+def second_kernel(pos, back, ops, out):
     for s in range(NSUB):
-        for j in range(BPS):
-            local[s, :, j * BLK : (j + 1) * BLK] = slot(back, pos[s * BPS + j])[...]
-    for s in range(NSUB):
-        prod = jnp.dot(local[s], ops[s], preferred_element_type=F32)
+        local = jnp.concatenate([slot(back, pos[s * BPS + j])[...] for j in range(BPS)], axis=1)
+        prod = jnp.dot(local, ops[s], preferred_element_type=F32)
         for j in range(BPS):
             slot(out, pos[s * BPS + j])[...] = prod[:, j * BLK : (j + 1) * BLK].astype(BF)
 
@@ -129,7 +130,6 @@
         out_shape=pltpu.VMEM((PEERS, SLOTROWS, BLK), BF),
         in_specs=[SMEM, VMEM, VMEM],
         out_specs=VMEM,
-        scratch_shapes=[pltpu.VMEM((NSUB, COLS, L), BF)],
         compiler_params=params(8),
         name="second_apply",
     )(pos, in_vmem(back), in_vmem(operators))

time: 140 us -> 139 us (level)
  no operation moved by 1% of the time
where the time goes in v8:
time: 139 us
  blocking collectives  103 us (74%)
  Pallas kernels  21.6 us (16%)
  starting transfers between devices  10.5 us (8%)
  waiting for transfers between devices  2.72 us (2%)
    all_to_all x3, blocking collectives, exchange(): lax.all_to_all(values, 'sub', split_axis=0, concat_axis=0, tiled=True)  103 us
    ppermute x8, starting transfers between devices, swapped(): return lax.ppermute(values, 'sub', pairs)  10.5 us
    pallas_call x1, Pallas kernels, first_apply(): pl.pallas_call(first_kernel, out_shape=(pltpu.VMEM((PEERS, SLOTROWS + IDR...  7.15 us
    pallas_call x2, Pallas kernels, merge(): pl.pallas_call(functools.partial(merge_kernel, part), out_shape=pltpu.VME...  4.74 us
    pallas_call x1, Pallas kernels, second_apply(): pl.pallas_call(second_kernel, out_shape=pltpu.VMEM((PEERS, SLOTROWS, BLK)...  3.54 us
  transfers between devices with their start and end apart: 8, of which 4 were waited for; matrix products, arithmetic and copies ran while one was open for 0% of the time, Pallas kernels for 3%

profile of v8, /device:TPU:1, one launch (start us, length us, event | category | flops | bytes accessed | tf_op | source)
XLA Modules:
  0.0 139.2 jit_solution(2036784480574686499)
XLA Ops:
  0.6 7.1 %first_apply.1 = (bf16[32,264,128]{2,1,0:T(8,128)(2,1)S(1)}, s32[64]{0:T(128)S(1)}, bf16[8,1024,1024]{2,1,0:T(8,128)(2,1)S(1)}) custom-call(s32[64]{0:T(128)} %bitcast.4, s32[64]{0:T(128)} %block_h.1, bf16[8,64,1024]{2,1,0:T(8,128)(2,1)} %loads.1, bf16[8,1024,1024]{2,1,0:T(8,128)(2,1)} %ops.1), custom_call_target="tpu_custom_call" | custom-call | tf_op jit(solution)/shard_map/first_apply/pallas_call | solution.py:96
  7.8 0.0 copy-start
  7.8 0.0 copy-start.1
  7.8 38.3 %all_to_all.15.received = bf16[32,264,128]{2,1,0:T(8,128)(2,1)S(1)} all-to-all(bf16[32,264,128]{2,1,0:T(8,128)(2,1)S(1)} %get-tuple-element.16), channel_id=1, replica_groups=mesh['sub'=32,'rep'=4] {'sub'}, dimensions={0} | all-to-all | bytes 4325376 | tf_op jit(solution)/shard_map/all_to_all | solution.py:369
  46.1 0.0 copy-done
  46.1 0.0 copy-done.1
  46.1 2.4 %project.1 = (f32[16,64,128]{2,1,0:T(8,128)S(1)}, f32[32,1024]{1,0:T(8,128)S(1)}, f32[32,1024]{1,0:T(8,128)S(1)}, s32[32,128]{1,0:T(8,128)S(1)}, bf16[1024,1024]{1,0:T(8,128)(2,1)S(1)}) custom-call(bf16[32,264,128]{2,1,0:T(8,128)(2,1)S(1)} %all_to_all.15.received, s32[16,128]{1,0:T(8,128)S(1)} %bitcast.2, bf16[2048,1024]{1,0:T(8,128)(2,1)S(1)} %copy-done, ...), custom_call_target="tpu_custom_call" | custom-call | tf_op jit(solution)/shard_map/project/pallas_call | solution.py:206
  48.5 0.5 collective-permute-start
  49.0 1.0 collective-permute-done.refs_1_
  50.0 1.0 collective-permute-start.3
  51.0 0.5 collective-permute-start.2
  51.5 1.8 %collective-permute-start.1 = (bf16[32,1024]{1,0:T(8,128)(2,1)S(1)}, bf16[32,1024]{1,0:T(8,128)(2,1)S(1)}, u32[]{:S(2)}, u32[]{:S(2)}) collective-permute-start(bf16[32,1024]{1,0:T(8,128)(2,1)S(1)} %get-tuple-element.21.after), channel_id=1, source_target_pairs={{0,96},{4,100},{8,104},{12,108},{16,112},{20,116},{24,120},{28,124... | collective-permute-start | bytes 196616 | tf_op jit(solution)/shard_map/ppermute | solution.py:254
  53.3 2.4 %merge.2.refs_4_.first = bf16[1024,1024]{1,0:T(8,128)(2,1)S(1)} custom-call(bf16[1024,1024]{1,0:T(8,128)(2,1)S(1)} %get-tuple-element.22.coarse, bf16[2048,1024]{1,0:T(8,128)(2,1)S(1)} %copy-done, bf16[32,1024]{1,0:T(8,128)(2,1)S(1)} %get-tuple-element.21.after), custom_call_target="tpu_custom_call" | custom-call | tf_op jit(solution)/shard_map/merge/pallas_call | solution.py:147
  55.7 0.0 collective-permute-done.3.refs_3_
  55.7 0.0 collective-permute-done.2.refs_2_
  55.7 0.7 collective-permute-done.1.refs_1_
  56.4 0.8 collective-permute-start.6
  57.3 0.7 collective-permute-start.5
  58.0 1.8 %collective-permute-start.4 = (bf16[32,1024]{1,0:T(8,128)(2,1)S(1)}, bf16[32,1024]{1,0:T(8,128)(2,1)S(1)}, u32[]{:S(2)}, u32[]{:S(2)}) collective-permute-start(bf16[32,1024]{1,0:T(8,128)(2,1)S(1)} %get-tuple-element.24.after), channel_id=1, source_target_pairs={{0,24},{4,28},{8,16},{12,20},{16,8},{20,12},{24,0},{28,4},{32,56},... | collective-permute-start | bytes 196616 | tf_op jit(solution)/shard_map/ppermute | solution.py:254
  59.8 2.4 %merge.3.refs_4_.second = bf16[1024,1024]{1,0:T(8,128)(2,1)S(1)} custom-call(bf16[1024,1024]{1,0:T(8,128)(2,1)S(1)} %get-tuple-element.22.coarse, bf16[2048,1024]{1,0:T(8,128)(2,1)S(1)} %copy-done, bf16[32,1024]{1,0:T(8,128)(2,1)S(1)} %get-tuple-element.24.after), custom_call_target="tpu_custom_call" | custom-call | tf_op jit(solution)/shard_map/merge/pallas_call | solution.py:147
  62.1 0.0 collective-permute-done.6.refs_3_
  62.1 0.0 collective-permute-done.5.refs_2_
  62.1 0.1 collective-permute-done.4.refs_1_
  62.3 3.3 %collective-permute-start.7 = (bf16[32,1024]{1,0:T(8,128)(2,1)S(1)}, bf16[32,1024]{1,0:T(8,128)(2,1)S(1)}, u32[]{:S(2)}, u32[]{:S(2)}) collective-permute-start(bf16[32,1024]{1,0:T(8,128)(2,1)S(1)} %add_parts.5.own), channel_id=1, source_target_pairs={{0,4},{4,0},{8,12},{12,8},{16,20},{20,16},{24,28},{28,24},{32,36},... | collective-permute-start | bytes 196616 | tf_op jit(solution)/shard_map/ppermute | solution.py:254
  65.7 0.9 collective-permute-done.7.other
  66.6 1.7 %start_values.1 = (f32[64,2048]{1,0:T(8,128)}, bf16[32,256,128]{2,1,0:T(8,128)(2,1)S(1)}) custom-call(s32[32,128]{1,0:T(8,128)S(1)} %get-tuple-element.17.ids_v, bf16[32,1024]{1,0:T(8,128)(2,1)S(1)} %add_parts.5.own, bf16[32,1024]{1,0:T(8,128)(2,1)S(1)} %collective-permute-done.7.other, bf16[1024,1024]{1,0:T(8,128)(2,1)S(1)} %merge.2.refs_4_.first, ...), custom_call_target="tpu_custom_call" | custom-call | tf_op jit(solution)/shard_map/start_values/pallas_call | solution.py:306
  68.2 33.3 %all_to_all.16.back = bf16[32,256,128]{2,1,0:T(8,128)(2,1)S(1)} all-to-all(bf16[32,256,128]{2,1,0:T(8,128)(2,1)S(1)} %get-tuple-element.27), channel_id=1, replica_groups=mesh['sub'=32,'rep'=4] {'sub'}, dimensions={0} | all-to-all | bytes 4194304 | tf_op jit(solution)/shard_map/all_to_all | solution.py:369
  101.5 3.5 %second_apply.1 = bf16[32,256,128]{2,1,0:T(8,128)(2,1)S(1)} custom-call(s32[64]{0:T(128)S(1)} %get-tuple-element.26.pos, bf16[32,256,128]{2,1,0:T(8,128)(2,1)S(1)} %all_to_all.16.back, bf16[8,1024,1024]{2,1,0:T(8,128)(2,1)S(1)} %get-tuple-element.28.ops), custom_call_target="tpu_custom_call" | custom-call | tf_op jit(solution)/shard_map/second_apply/pallas_call | solution.py:128
  105.1 31.9 %all_to_all.17.received = bf16[32,256,128]{2,1,0:T(8,128)(2,1)S(1)} all-to-all(bf16[32,256,128]{2,1,0:T(8,128)(2,1)S(1)} %second_apply.1), channel_id=1, replica_groups=mesh['sub'=32,'rep'=4] {'sub'}, dimensions={0} | all-to-all | bytes 4194304 | tf_op jit(solution)/shard_map/all_to_all | solution.py:369
  137.0 2.1 %residual.1 = f32[64,2048]{1,0:T(8,128)} custom-call(s32[32,128]{1,0:T(8,128)S(1)} %get-tuple-element.17.ids_v, bf16[32,256,128]{2,1,0:T(8,128)(2,1)S(1)} %all_to_all.17.received, s32[16,128]{1,0:T(8,128)S(1)} %bitcast.3, f32[16,64,128]{2,1,0:T(8,128)S(1)} %get-tuple-element.29.dual), custom_call_target="tpu_custom_call" | custom-call | tf_op jit(solution)/shard_map/residual/pallas_call | solution.py:351
  (3 shorter events, 0.1 us)
Async XLA Ops:
  7.8 38.3 %copy-start = (bf16[2048,1024]{1,0:T(8,128)(2,1)S(1)}, bf16[2048,1024]{1,0:T(8,128)(2,1)}, u32[]{:S(2)}) copy-start(bf16[2048,1024]{1,0:T(8,128)(2,1)} %basis.5) | copy-start | bytes 12582916
  7.8 38.3 %copy-start.1 = (s32[2048]{0:T(1024)S(1)}, s32[2048]{0:T(1024)}, u32[]{:S(2)}) copy-start(s32[2048]{0:T(1024)} %param.11) | copy-start | bytes 24580
  48.5 1.5 %collective-permute-start = (f32[32,1024]{1,0:T(8,128)S(1)}, f32[32,1024]{1,0:T(8,128)S(1)}, u32[]{:S(2)}, u32[]{:S(2)}) collective-permute-start(f32[32,1024]{1,0:T(8,128)S(1)} %get-tuple-element.19), channel_id=1, source_target_pairs={{0,4},{4,0},{8,12},{12,8},{16,20},{20,16},{24,28},{28,24},{32,36},... | collective-permute-start | bytes 393224 | tf_op jit(solution)/shard_map/ppermute | solution.py:254
  50.0 5.7 %collective-permute-start.3 = (bf16[32,1024]{1,0:T(8,128)(2,1)S(1)}, bf16[32,1024]{1,0:T(8,128)(2,1)S(1)}, u32[]{:S(2)}, u32[]{:S(2)}) collective-permute-start(bf16[32,1024]{1,0:T(8,128)(2,1)S(1)} %get-tuple-element.21.after), channel_id=1, source_target_pairs={{0,64},{4,68},{8,72},{12,76},{16,80},{20,84},{24,88},{28,92},{32,9... | collective-permute-start | bytes 196616 | tf_op jit(solution)/shard_map/ppermute | solution.py:254
  51.0 4.7 %collective-permute-start.2 = (bf16[32,1024]{1,0:T(8,128)(2,1)S(1)}, bf16[32,1024]{1,0:T(8,128)(2,1)S(1)}, u32[]{:S(2)}, u32[]{:S(2)}) collective-permute-start(bf16[32,1024]{1,0:T(8,128)(2,1)S(1)} %get-tuple-element.21.after), channel_id=1, source_target_pairs={{0,32},{4,36},{8,40},{12,44},{16,48},{20,52},{24,56},{28,60},{32,0... | collective-permute-start | bytes 196616 | tf_op jit(solution)/shard_map/ppermute | solution.py:254
  51.5 4.9 %collective-permute-start.1 = (bf16[32,1024]{1,0:T(8,128)(2,1)S(1)}, bf16[32,1024]{1,0:T(8,128)(2,1)S(1)}, u32[]{:S(2)}, u32[]{:S(2)}) collective-permute-start(bf16[32,1024]{1,0:T(8,128)(2,1)S(1)} %get-tuple-element.21.after), channel_id=1, source_target_pairs={{0,96},{4,100},{8,104},{12,108},{16,112},{20,116},{24,120},{28,124... | collective-permute-start | bytes 196616 | tf_op jit(solution)/shard_map/ppermute | solution.py:254
  56.4 5.7 %collective-permute-start.6 = (bf16[32,1024]{1,0:T(8,128)(2,1)S(1)}, bf16[32,1024]{1,0:T(8,128)(2,1)S(1)}, u32[]{:S(2)}, u32[]{:S(2)}) collective-permute-start(bf16[32,1024]{1,0:T(8,128)(2,1)S(1)} %get-tuple-element.24.after), channel_id=1, source_target_pairs={{0,16},{4,20},{8,24},{12,28},{16,0},{20,4},{24,8},{28,12},{32,48},... | collective-permute-start | bytes 196616 | tf_op jit(solution)/shard_map/ppermute | solution.py:254
  57.3 4.9 %collective-permute-start.5 = (bf16[32,1024]{1,0:T(8,128)(2,1)S(1)}, bf16[32,1024]{1,0:T(8,128)(2,1)S(1)}, u32[]{:S(2)}, u32[]{:S(2)}) collective-permute-start(bf16[32,1024]{1,0:T(8,128)(2,1)S(1)} %get-tuple-element.24.after), channel_id=1, source_target_pairs={{0,8},{4,12},{8,0},{12,4},{16,24},{20,28},{24,16},{28,20},{32,40},... | collective-permute-start | bytes 196616 | tf_op jit(solution)/shard_map/ppermute | solution.py:254
  58.0 4.3 %collective-permute-start.4 = (bf16[32,1024]{1,0:T(8,128)(2,1)S(1)}, bf16[32,1024]{1,0:T(8,128)(2,1)S(1)}, u32[]{:S(2)}, u32[]{:S(2)}) collective-permute-start(bf16[32,1024]{1,0:T(8,128)(2,1)S(1)} %get-tuple-element.24.after), channel_id=1, source_target_pairs={{0,24},{4,28},{8,16},{12,20},{16,8},{20,12},{24,0},{28,4},{32,56},... | collective-permute-start | bytes 196616 | tf_op jit(solution)/shard_map/ppermute | solution.py:254
  62.3 4.2 %collective-permute-start.7 = (bf16[32,1024]{1,0:T(8,128)(2,1)S(1)}, bf16[32,1024]{1,0:T(8,128)(2,1)S(1)}, u32[]{:S(2)}, u32[]{:S(2)}) collective-permute-start(bf16[32,1024]{1,0:T(8,128)(2,1)S(1)} %add_parts.5.own), channel_id=1, source_target_pairs={{0,4},{4,0},{8,12},{12,8},{16,20},{20,16},{24,28},{28,24},{32,36},... | collective-permute-start | bytes 196616 | tf_op jit(solution)/shard_map/ppermute | solution.py:254

commit v9 on v8

--- a/solution.py
+++ b/solution.py
@@ -266,7 +266,7 @@
     return narrow, swapped(narrow, 0, 0, 1), first, second
 
 
-PIECES = 4
+PIECES = 2
 PIECE = OB * BLK // PIECES
 
 
@@ -278,11 +278,8 @@
     coeff[1 - core] = other[...]
     copies = []
     for n in range(PIECES):
-        merged = (first, second)[n // 2]
-        cols = slice(n % 2 * PIECE, (n % 2 + 1) * PIECE)
-        value[n] = jnp.dot(
-            coeff[...].reshape(COLS, NB), merged[:, cols], preferred_element_type=F32
-        )
+        merged = (first, second)[n]
+        value[n] = jnp.dot(coeff[...].reshape(COLS, NB), merged[...], preferred_element_type=F32)
         copies.append(
             pltpu.make_async_copy(value.at[n], start.at[:, pl.ds(n * PIECE, PIECE)], sem.at[n])
         )

time: 139 us -> 139 us (level)
  no operation moved by 1% of the time
where the time goes in v9:
time: 139 us
  blocking collectives  103 us (74%)
  Pallas kernels  21.6 us (16%)
  starting transfers between devices  10.5 us (8%)
  waiting for transfers between devices  2.72 us (2%)
    all_to_all x3, blocking collectives, exchange(): lax.all_to_all(values, 'sub', split_axis=0, concat_axis=0, tiled=True)  103 us
    ppermute x8, starting transfers between devices, swapped(): return lax.ppermute(values, 'sub', pairs)  10.5 us
    pallas_call x1, Pallas kernels, first_apply(): pl.pallas_call(first_kernel, out_shape=(pltpu.VMEM((PEERS, SLOTROWS + IDR...  7.15 us
    pallas_call x2, Pallas kernels, merge(): pl.pallas_call(functools.partial(merge_kernel, part), out_shape=pltpu.VME...  4.74 us
    pallas_call x1, Pallas kernels, second_apply(): pl.pallas_call(second_kernel, out_shape=pltpu.VMEM((PEERS, SLOTROWS, BLK)...  3.54 us
  transfers between devices with their start and end apart: 8, of which 4 were waited for; matrix products, arithmetic and copies ran while one was open for 0% of the time, Pallas kernels for 3%

profile of v9, /device:TPU:1, one launch (start us, length us, event | category | flops | bytes accessed | tf_op | source)
XLA Modules:
  0.0 139.2 jit_solution(3373099418137255550)
XLA Ops:
  0.6 7.1 %first_apply.1 = (bf16[32,264,128]{2,1,0:T(8,128)(2,1)S(1)}, s32[64]{0:T(128)S(1)}, bf16[8,1024,1024]{2,1,0:T(8,128)(2,1)S(1)}) custom-call(s32[64]{0:T(128)} %bitcast.4, s32[64]{0:T(128)} %block_h.1, bf16[8,64,1024]{2,1,0:T(8,128)(2,1)} %loads.1, bf16[8,1024,1024]{2,1,0:T(8,128)(2,1)} %ops.1), custom_call_target="tpu_custom_call" | custom-call | tf_op jit(solution)/shard_map/first_apply/pallas_call | solution.py:96
  7.8 0.0 copy-start
  7.8 0.0 copy-start.1
  7.8 38.3 %all_to_all.15.received = bf16[32,264,128]{2,1,0:T(8,128)(2,1)S(1)} all-to-all(bf16[32,264,128]{2,1,0:T(8,128)(2,1)S(1)} %get-tuple-element.16), channel_id=1, replica_groups=mesh['sub'=32,'rep'=4] {'sub'}, dimensions={0} | all-to-all | bytes 4325376 | tf_op jit(solution)/shard_map/all_to_all | solution.py:366
  46.1 0.0 copy-done
  46.1 0.0 copy-done.1
  46.1 2.4 %project.1 = (f32[16,64,128]{2,1,0:T(8,128)S(1)}, f32[32,1024]{1,0:T(8,128)S(1)}, f32[32,1024]{1,0:T(8,128)S(1)}, s32[32,128]{1,0:T(8,128)S(1)}, bf16[1024,1024]{1,0:T(8,128)(2,1)S(1)}) custom-call(bf16[32,264,128]{2,1,0:T(8,128)(2,1)S(1)} %all_to_all.15.received, s32[16,128]{1,0:T(8,128)S(1)} %bitcast.2, bf16[2048,1024]{1,0:T(8,128)(2,1)S(1)} %copy-done, ...), custom_call_target="tpu_custom_call" | custom-call | tf_op jit(solution)/shard_map/project/pallas_call | solution.py:206
  48.5 0.5 collective-permute-start
  49.0 1.0 collective-permute-done.refs_1_
  50.0 1.0 collective-permute-start.3
  51.0 0.5 collective-permute-start.2
  51.5 1.8 %collective-permute-start.1 = (bf16[32,1024]{1,0:T(8,128)(2,1)S(1)}, bf16[32,1024]{1,0:T(8,128)(2,1)S(1)}, u32[]{:S(2)}, u32[]{:S(2)}) collective-permute-start(bf16[32,1024]{1,0:T(8,128)(2,1)S(1)} %get-tuple-element.21.after), channel_id=1, source_target_pairs={{0,96},{4,100},{8,104},{12,108},{16,112},{20,116},{24,120},{28,124... | collective-permute-start | bytes 196616 | tf_op jit(solution)/shard_map/ppermute | solution.py:254
  53.3 2.4 %merge.2.refs_4_.first = bf16[1024,1024]{1,0:T(8,128)(2,1)S(1)} custom-call(bf16[1024,1024]{1,0:T(8,128)(2,1)S(1)} %get-tuple-element.22.coarse, bf16[2048,1024]{1,0:T(8,128)(2,1)S(1)} %copy-done, bf16[32,1024]{1,0:T(8,128)(2,1)S(1)} %get-tuple-element.21.after), custom_call_target="tpu_custom_call" | custom-call | tf_op jit(solution)/shard_map/merge/pallas_call | solution.py:147
  55.7 0.0 collective-permute-done.3.refs_3_
  55.7 0.0 collective-permute-done.2.refs_2_
  55.7 0.7 collective-permute-done.1.refs_1_
  56.4 0.8 collective-permute-start.6
  57.3 0.7 collective-permute-start.5
  58.0 1.8 %collective-permute-start.4 = (bf16[32,1024]{1,0:T(8,128)(2,1)S(1)}, bf16[32,1024]{1,0:T(8,128)(2,1)S(1)}, u32[]{:S(2)}, u32[]{:S(2)}) collective-permute-start(bf16[32,1024]{1,0:T(8,128)(2,1)S(1)} %get-tuple-element.24.after), channel_id=1, source_target_pairs={{0,24},{4,28},{8,16},{12,20},{16,8},{20,12},{24,0},{28,4},{32,56},... | collective-permute-start | bytes 196616 | tf_op jit(solution)/shard_map/ppermute | solution.py:254
  59.8 2.4 %merge.3.refs_4_.second = bf16[1024,1024]{1,0:T(8,128)(2,1)S(1)} custom-call(bf16[1024,1024]{1,0:T(8,128)(2,1)S(1)} %get-tuple-element.22.coarse, bf16[2048,1024]{1,0:T(8,128)(2,1)S(1)} %copy-done, bf16[32,1024]{1,0:T(8,128)(2,1)S(1)} %get-tuple-element.24.after), custom_call_target="tpu_custom_call" | custom-call | tf_op jit(solution)/shard_map/merge/pallas_call | solution.py:147
  62.1 0.0 collective-permute-done.6.refs_3_
  62.1 0.0 collective-permute-done.5.refs_2_
  62.1 0.1 collective-permute-done.4.refs_1_
  62.3 3.3 %collective-permute-start.7 = (bf16[32,1024]{1,0:T(8,128)(2,1)S(1)}, bf16[32,1024]{1,0:T(8,128)(2,1)S(1)}, u32[]{:S(2)}, u32[]{:S(2)}) collective-permute-start(bf16[32,1024]{1,0:T(8,128)(2,1)S(1)} %add_parts.5.own), channel_id=1, source_target_pairs={{0,4},{4,0},{8,12},{12,8},{16,20},{20,16},{24,28},{28,24},{32,36},... | collective-permute-start | bytes 196616 | tf_op jit(solution)/shard_map/ppermute | solution.py:254
  65.7 0.9 collective-permute-done.7.other
  66.6 1.6 %start_values.1 = (f32[64,2048]{1,0:T(8,128)}, bf16[32,256,128]{2,1,0:T(8,128)(2,1)S(1)}) custom-call(s32[32,128]{1,0:T(8,128)S(1)} %get-tuple-element.17.ids_v, bf16[32,1024]{1,0:T(8,128)(2,1)S(1)} %add_parts.5.own, bf16[32,1024]{1,0:T(8,128)(2,1)S(1)} %collective-permute-done.7.other, bf16[1024,1024]{1,0:T(8,128)(2,1)S(1)} %merge.2.refs_4_.first, ...), custom_call_target="tpu_custom_call" | custom-call | tf_op jit(solution)/shard_map/start_values/pallas_call | solution.py:303
  68.1 33.3 %all_to_all.16.back = bf16[32,256,128]{2,1,0:T(8,128)(2,1)S(1)} all-to-all(bf16[32,256,128]{2,1,0:T(8,128)(2,1)S(1)} %get-tuple-element.27), channel_id=1, replica_groups=mesh['sub'=32,'rep'=4] {'sub'}, dimensions={0} | all-to-all | bytes 4194304 | tf_op jit(solution)/shard_map/all_to_all | solution.py:366
  101.4 3.5 %second_apply.1 = bf16[32,256,128]{2,1,0:T(8,128)(2,1)S(1)} custom-call(s32[64]{0:T(128)S(1)} %get-tuple-element.26.pos, bf16[32,256,128]{2,1,0:T(8,128)(2,1)S(1)} %all_to_all.16.back, bf16[8,1024,1024]{2,1,0:T(8,128)(2,1)S(1)} %get-tuple-element.28.ops), custom_call_target="tpu_custom_call" | custom-call | tf_op jit(solution)/shard_map/second_apply/pallas_call | solution.py:128
  105.0 31.9 %all_to_all.17.received = bf16[32,256,128]{2,1,0:T(8,128)(2,1)S(1)} all-to-all(bf16[32,256,128]{2,1,0:T(8,128)(2,1)S(1)} %second_apply.1), channel_id=1, replica_groups=mesh['sub'=32,'rep'=4] {'sub'}, dimensions={0} | all-to-all | bytes 4194304 | tf_op jit(solution)/shard_map/all_to_all | solution.py:366
  136.9 2.1 %residual.1 = f32[64,2048]{1,0:T(8,128)} custom-call(s32[32,128]{1,0:T(8,128)S(1)} %get-tuple-element.17.ids_v, bf16[32,256,128]{2,1,0:T(8,128)(2,1)S(1)} %all_to_all.17.received, s32[16,128]{1,0:T(8,128)S(1)} %bitcast.3, f32[16,64,128]{2,1,0:T(8,128)S(1)} %get-tuple-element.29.dual), custom_call_target="tpu_custom_call" | custom-call | tf_op jit(solution)/shard_map/residual/pallas_call | solution.py:348
  (3 shorter events, 0.1 us)
Async XLA Ops:
  7.8 38.3 %copy-start = (bf16[2048,1024]{1,0:T(8,128)(2,1)S(1)}, bf16[2048,1024]{1,0:T(8,128)(2,1)}, u32[]{:S(2)}) copy-start(bf16[2048,1024]{1,0:T(8,128)(2,1)} %basis.5) | copy-start | bytes 12582916
  7.8 38.3 %copy-start.1 = (s32[2048]{0:T(1024)S(1)}, s32[2048]{0:T(1024)}, u32[]{:S(2)}) copy-start(s32[2048]{0:T(1024)} %param.11) | copy-start | bytes 24580
  48.5 1.5 %collective-permute-start = (f32[32,1024]{1,0:T(8,128)S(1)}, f32[32,1024]{1,0:T(8,128)S(1)}, u32[]{:S(2)}, u32[]{:S(2)}) collective-permute-start(f32[32,1024]{1,0:T(8,128)S(1)} %get-tuple-element.19), channel_id=1, source_target_pairs={{0,4},{4,0},{8,12},{12,8},{16,20},{20,16},{24,28},{28,24},{32,36},... | collective-permute-start | bytes 393224 | tf_op jit(solution)/shard_map/ppermute | solution.py:254
  50.0 5.7 %collective-permute-start.3 = (bf16[32,1024]{1,0:T(8,128)(2,1)S(1)}, bf16[32,1024]{1,0:T(8,128)(2,1)S(1)}, u32[]{:S(2)}, u32[]{:S(2)}) collective-permute-start(bf16[32,1024]{1,0:T(8,128)(2,1)S(1)} %get-tuple-element.21.after), channel_id=1, source_target_pairs={{0,64},{4,68},{8,72},{12,76},{16,80},{20,84},{24,88},{28,92},{32,9... | collective-permute-start | bytes 196616 | tf_op jit(solution)/shard_map/ppermute | solution.py:254
  51.0 4.7 %collective-permute-start.2 = (bf16[32,1024]{1,0:T(8,128)(2,1)S(1)}, bf16[32,1024]{1,0:T(8,128)(2,1)S(1)}, u32[]{:S(2)}, u32[]{:S(2)}) collective-permute-start(bf16[32,1024]{1,0:T(8,128)(2,1)S(1)} %get-tuple-element.21.after), channel_id=1, source_target_pairs={{0,32},{4,36},{8,40},{12,44},{16,48},{20,52},{24,56},{28,60},{32,0... | collective-permute-start | bytes 196616 | tf_op jit(solution)/shard_map/ppermute | solution.py:254
  51.5 4.9 %collective-permute-start.1 = (bf16[32,1024]{1,0:T(8,128)(2,1)S(1)}, bf16[32,1024]{1,0:T(8,128)(2,1)S(1)}, u32[]{:S(2)}, u32[]{:S(2)}) collective-permute-start(bf16[32,1024]{1,0:T(8,128)(2,1)S(1)} %get-tuple-element.21.after), channel_id=1, source_target_pairs={{0,96},{4,100},{8,104},{12,108},{16,112},{20,116},{24,120},{28,124... | collective-permute-start | bytes 196616 | tf_op jit(solution)/shard_map/ppermute | solution.py:254
  56.4 5.7 %collective-permute-start.6 = (bf16[32,1024]{1,0:T(8,128)(2,1)S(1)}, bf16[32,1024]{1,0:T(8,128)(2,1)S(1)}, u32[]{:S(2)}, u32[]{:S(2)}) collective-permute-start(bf16[32,1024]{1,0:T(8,128)(2,1)S(1)} %get-tuple-element.24.after), channel_id=1, source_target_pairs={{0,16},{4,20},{8,24},{12,28},{16,0},{20,4},{24,8},{28,12},{32,48},... | collective-permute-start | bytes 196616 | tf_op jit(solution)/shard_map/ppermute | solution.py:254
  57.3 4.9 %collective-permute-start.5 = (bf16[32,1024]{1,0:T(8,128)(2,1)S(1)}, bf16[32,1024]{1,0:T(8,128)(2,1)S(1)}, u32[]{:S(2)}, u32[]{:S(2)}) collective-permute-start(bf16[32,1024]{1,0:T(8,128)(2,1)S(1)} %get-tuple-element.24.after), channel_id=1, source_target_pairs={{0,8},{4,12},{8,0},{12,4},{16,24},{20,28},{24,16},{28,20},{32,40},... | collective-permute-start | bytes 196616 | tf_op jit(solution)/shard_map/ppermute | solution.py:254
  58.0 4.3 %collective-permute-start.4 = (bf16[32,1024]{1,0:T(8,128)(2,1)S(1)}, bf16[32,1024]{1,0:T(8,128)(2,1)S(1)}, u32[]{:S(2)}, u32[]{:S(2)}) collective-permute-start(bf16[32,1024]{1,0:T(8,128)(2,1)S(1)} %get-tuple-element.24.after), channel_id=1, source_target_pairs={{0,24},{4,28},{8,16},{12,20},{16,8},{20,12},{24,0},{28,4},{32,56},... | collective-permute-start | bytes 196616 | tf_op jit(solution)/shard_map/ppermute | solution.py:254
  62.3 4.2 %collective-permute-start.7 = (bf16[32,1024]{1,0:T(8,128)(2,1)S(1)}, bf16[32,1024]{1,0:T(8,128)(2,1)S(1)}, u32[]{:S(2)}, u32[]{:S(2)}) collective-permute-start(bf16[32,1024]{1,0:T(8,128)(2,1)S(1)} %add_parts.5.own), channel_id=1, source_target_pairs={{0,4},{4,0},{8,12},{12,8},{16,20},{20,16},{24,28},{28,24},{32,36},... | collective-permute-start | bytes 196616 | tf_op jit(solution)/shard_map/ppermute | solution.py:254

commit v10 on v9

--- a/solution.py
+++ b/solution.py
@@ -177,7 +177,7 @@
 TOTALS = [pltpu.VMEM((OB + 1, COLS, BLK), F32)] * CAP
 
 
-def project_kernel(received, scale, basis, coarse, dual, keep, send, ids_out, coarse_v, t0, t1, t2, t3, narrow, coeff, idv, ids, sem, coarse_sem):
+def project_kernel(received, scale, basis, coarse, dual, keep, send, ids_out, coarse_v, t0, t1, t2, t3, narrow, idv, ids, sem, coarse_sem):
     coarse_copy = pltpu.make_async_copy(coarse, coarse_v, coarse_sem)
     coarse_copy.start()
     totals = (t0, t1, t2, t3)
@@ -194,11 +194,9 @@
         dual[b] = owned
         narrow[:, b * BLK : (b + 1) * BLK] = owned.astype(BF)
     product = jnp.dot(narrow[...], basis[...], preferred_element_type=F32)
-    coeff[0] = product[:HALF]
-    coeff[1] = product[HALF:]
-    core = lax.axis_index("sub") % 2
-    keep[...] = coeff[core]
-    send[...] = coeff[1 - core]
+    even = lax.axis_index("sub") % 2 == 0
+    keep[...] = jnp.where(even, product[:HALF], product[HALF:])
+    send[...] = jnp.where(even, product[HALF:], product[:HALF])
     coarse_copy.wait()
 
 
@@ -217,7 +215,6 @@
         scratch_shapes=TOTALS
         + [
             pltpu.VMEM((COLS, OB * BLK), BF),
-            pltpu.VMEM((2, HALF, NB), F32),
             pltpu.VMEM((PEERS, BLK), jnp.int32),
             pltpu.SMEM((PEERS, BLK), jnp.int32),
             pltpu.SemaphoreType.DMA,
@@ -270,16 +267,17 @@
 PIECE = OB * BLK // PIECES
 
 
-def start_kernel(ids_v, own, other, first, second, start, out, coeff, blocks, value, ids, sem, ids_sem):
+def start_kernel(ids_v, own, other, first, second, start, out, blocks, value, ids, sem, ids_sem):
     ids_copy = pltpu.make_async_copy(ids_v, ids, ids_sem)
     ids_copy.start()
-    core = lax.axis_index("sub") % 2
-    coeff[core] = own[...]
-    coeff[1 - core] = other[...]
+    even = lax.axis_index("sub") % 2 == 0
+    coeff = jnp.concatenate(
+        [jnp.where(even, own[...], other[...]), jnp.where(even, other[...], own[...])], axis=0
+    )
     copies = []
     for n in range(PIECES):
         merged = (first, second)[n]
-        value[n] = jnp.dot(coeff[...].reshape(COLS, NB), merged[...], preferred_element_type=F32)
+        value[n] = jnp.dot(coeff, merged[...], preferred_element_type=F32)
         copies.append(
             pltpu.make_async_copy(value.at[n], start.at[:, pl.ds(n * PIECE, PIECE)], sem.at[n])
         )
@@ -309,7 +307,6 @@
         in_specs=[VMEM] * 5,
         out_specs=[HBM, VMEM],
         scratch_shapes=[
-            pltpu.VMEM((2, HALF, NB), BF),
             pltpu.VMEM((OB, COLS, BLK), BF),
             pltpu.VMEM((PIECES, COLS, PIECE), F32),
             pltpu.SMEM((PEERS, BLK), jnp.int32),

time: 139 us -> 139 us (level)
  no operation moved by 1% of the time
where the time goes in v10:
time: 139 us
  blocking collectives  103 us (74%)
  Pallas kernels  21.5 us (15%)
  starting transfers between devices  10.5 us (8%)
  waiting for transfers between devices  2.73 us (2%)
    all_to_all x3, blocking collectives, exchange(): lax.all_to_all(values, 'sub', split_axis=0, concat_axis=0, tiled=True)  103 us
    ppermute x8, starting transfers between devices, swapped(): return lax.ppermute(values, 'sub', pairs)  10.5 us
    pallas_call x1, Pallas kernels, first_apply(): pl.pallas_call(first_kernel, out_shape=(pltpu.VMEM((PEERS, SLOTROWS + IDR...  7.15 us
    pallas_call x2, Pallas kernels, merge(): pl.pallas_call(functools.partial(merge_kernel, part), out_shape=pltpu.VME...  4.73 us
    pallas_call x1, Pallas kernels, second_apply(): pl.pallas_call(second_kernel, out_shape=pltpu.VMEM((PEERS, SLOTROWS, BLK)...  3.54 us
  transfers between devices with their start and end apart: 8, of which 4 were waited for; matrix products, arithmetic and copies ran while one was open for 0% of the time, Pallas kernels for 3%

profile of v10, /device:TPU:1, one launch (start us, length us, event | category | flops | bytes accessed | tf_op | source)
XLA Modules:
  0.0 139.1 jit_solution(5598128852532667366)
XLA Ops:
  0.6 7.1 %first_apply.1 = (bf16[32,264,128]{2,1,0:T(8,128)(2,1)S(1)}, s32[64]{0:T(128)S(1)}, bf16[8,1024,1024]{2,1,0:T(8,128)(2,1)S(1)}) custom-call(s32[64]{0:T(128)} %bitcast.4, s32[64]{0:T(128)} %block_h.1, bf16[8,64,1024]{2,1,0:T(8,128)(2,1)} %loads.1, bf16[8,1024,1024]{2,1,0:T(8,128)(2,1)} %ops.1), custom_call_target="tpu_custom_call" | custom-call | tf_op jit(solution)/shard_map/first_apply/pallas_call | solution.py:96
  7.8 0.0 copy-start
  7.8 0.0 copy-start.1
  7.8 38.3 %all_to_all.15.received = bf16[32,264,128]{2,1,0:T(8,128)(2,1)S(1)} all-to-all(bf16[32,264,128]{2,1,0:T(8,128)(2,1)S(1)} %get-tuple-element.16), channel_id=1, replica_groups=mesh['sub'=32,'rep'=4] {'sub'}, dimensions={0} | all-to-all | bytes 4325376 | tf_op jit(solution)/shard_map/all_to_all | solution.py:363
  46.1 0.0 copy-done
  46.1 0.0 copy-done.1
  46.1 2.3 %project.1 = (f32[16,64,128]{2,1,0:T(8,128)S(1)}, f32[32,1024]{1,0:T(8,128)S(1)}, f32[32,1024]{1,0:T(8,128)S(1)}, s32[32,128]{1,0:T(8,128)S(1)}, bf16[1024,1024]{1,0:T(8,128)(2,1)S(1)}) custom-call(bf16[32,264,128]{2,1,0:T(8,128)(2,1)S(1)} %all_to_all.15.received, s32[16,128]{1,0:T(8,128)S(1)} %bitcast.2, bf16[2048,1024]{1,0:T(8,128)(2,1)S(1)} %copy-done, ...), custom_call_target="tpu_custom_call" | custom-call | tf_op jit(solution)/shard_map/project/pallas_call | solution.py:204
  48.5 0.5 collective-permute-start
  48.9 1.0 collective-permute-done.refs_1_
  49.9 1.0 collective-permute-start.3
  51.0 0.5 collective-permute-start.2
  51.5 1.8 %collective-permute-start.1 = (bf16[32,1024]{1,0:T(8,128)(2,1)S(1)}, bf16[32,1024]{1,0:T(8,128)(2,1)S(1)}, u32[]{:S(2)}, u32[]{:S(2)}) collective-permute-start(bf16[32,1024]{1,0:T(8,128)(2,1)S(1)} %get-tuple-element.21.after), channel_id=1, source_target_pairs={{0,96},{4,100},{8,104},{12,108},{16,112},{20,116},{24,120},{28,124... | collective-permute-start | bytes 196616 | tf_op jit(solution)/shard_map/ppermute | solution.py:251
  53.3 2.4 %merge.2.refs_4_.first = bf16[1024,1024]{1,0:T(8,128)(2,1)S(1)} custom-call(bf16[1024,1024]{1,0:T(8,128)(2,1)S(1)} %get-tuple-element.22.coarse, bf16[2048,1024]{1,0:T(8,128)(2,1)S(1)} %copy-done, bf16[32,1024]{1,0:T(8,128)(2,1)S(1)} %get-tuple-element.21.after), custom_call_target="tpu_custom_call" | custom-call | tf_op jit(solution)/shard_map/merge/pallas_call | solution.py:147
  55.7 0.0 collective-permute-done.3.refs_3_
  55.7 0.0 collective-permute-done.2.refs_2_
  55.7 0.7 collective-permute-done.1.refs_1_
  56.4 0.8 collective-permute-start.6
  57.2 0.7 collective-permute-start.5
  57.9 1.8 %collective-permute-start.4 = (bf16[32,1024]{1,0:T(8,128)(2,1)S(1)}, bf16[32,1024]{1,0:T(8,128)(2,1)S(1)}, u32[]{:S(2)}, u32[]{:S(2)}) collective-permute-start(bf16[32,1024]{1,0:T(8,128)(2,1)S(1)} %get-tuple-element.24.after), channel_id=1, source_target_pairs={{0,24},{4,28},{8,16},{12,20},{16,8},{20,12},{24,0},{28,4},{32,56},... | collective-permute-start | bytes 196616 | tf_op jit(solution)/shard_map/ppermute | solution.py:251
  59.7 2.4 %merge.3.refs_4_.second = bf16[1024,1024]{1,0:T(8,128)(2,1)S(1)} custom-call(bf16[1024,1024]{1,0:T(8,128)(2,1)S(1)} %get-tuple-element.22.coarse, bf16[2048,1024]{1,0:T(8,128)(2,1)S(1)} %copy-done, bf16[32,1024]{1,0:T(8,128)(2,1)S(1)} %get-tuple-element.24.after), custom_call_target="tpu_custom_call" | custom-call | tf_op jit(solution)/shard_map/merge/pallas_call | solution.py:147
  62.1 0.0 collective-permute-done.6.refs_3_
  62.1 0.0 collective-permute-done.5.refs_2_
  62.1 0.1 collective-permute-done.4.refs_1_
  62.3 3.3 %collective-permute-start.7 = (bf16[32,1024]{1,0:T(8,128)(2,1)S(1)}, bf16[32,1024]{1,0:T(8,128)(2,1)S(1)}, u32[]{:S(2)}, u32[]{:S(2)}) collective-permute-start(bf16[32,1024]{1,0:T(8,128)(2,1)S(1)} %add_parts.5.own), channel_id=1, source_target_pairs={{0,4},{4,0},{8,12},{12,8},{16,20},{20,16},{24,28},{28,24},{32,36},... | collective-permute-start | bytes 196616 | tf_op jit(solution)/shard_map/ppermute | solution.py:251
  65.6 0.9 collective-permute-done.7.other
  66.5 1.6 %start_values.1 = (f32[64,2048]{1,0:T(8,128)}, bf16[32,256,128]{2,1,0:T(8,128)(2,1)S(1)}) custom-call(s32[32,128]{1,0:T(8,128)S(1)} %get-tuple-element.17.ids_v, bf16[32,1024]{1,0:T(8,128)(2,1)S(1)} %add_parts.5.own, bf16[32,1024]{1,0:T(8,128)(2,1)S(1)} %collective-permute-done.7.other, bf16[1024,1024]{1,0:T(8,128)(2,1)S(1)} %merge.2.refs_4_.first, ...), custom_call_target="tpu_custom_call" | custom-call | tf_op jit(solution)/shard_map/start_values/pallas_call | solution.py:301
  68.1 33.3 %all_to_all.16.back = bf16[32,256,128]{2,1,0:T(8,128)(2,1)S(1)} all-to-all(bf16[32,256,128]{2,1,0:T(8,128)(2,1)S(1)} %get-tuple-element.27), channel_id=1, replica_groups=mesh['sub'=32,'rep'=4] {'sub'}, dimensions={0} | all-to-all | bytes 4194304 | tf_op jit(solution)/shard_map/all_to_all | solution.py:363
  101.4 3.5 %second_apply.1 = bf16[32,256,128]{2,1,0:T(8,128)(2,1)S(1)} custom-call(s32[64]{0:T(128)S(1)} %get-tuple-element.26.pos, bf16[32,256,128]{2,1,0:T(8,128)(2,1)S(1)} %all_to_all.16.back, bf16[8,1024,1024]{2,1,0:T(8,128)(2,1)S(1)} %get-tuple-element.28.ops), custom_call_target="tpu_custom_call" | custom-call | tf_op jit(solution)/shard_map/second_apply/pallas_call | solution.py:128
  105.0 31.9 %all_to_all.17.received = bf16[32,256,128]{2,1,0:T(8,128)(2,1)S(1)} all-to-all(bf16[32,256,128]{2,1,0:T(8,128)(2,1)S(1)} %second_apply.1), channel_id=1, replica_groups=mesh['sub'=32,'rep'=4] {'sub'}, dimensions={0} | all-to-all | bytes 4194304 | tf_op jit(solution)/shard_map/all_to_all | solution.py:363
  136.9 2.1 %residual.1 = f32[64,2048]{1,0:T(8,128)} custom-call(s32[32,128]{1,0:T(8,128)S(1)} %get-tuple-element.17.ids_v, bf16[32,256,128]{2,1,0:T(8,128)(2,1)S(1)} %all_to_all.17.received, s32[16,128]{1,0:T(8,128)S(1)} %bitcast.3, f32[16,64,128]{2,1,0:T(8,128)S(1)} %get-tuple-element.29.dual), custom_call_target="tpu_custom_call" | custom-call | tf_op jit(solution)/shard_map/residual/pallas_call | solution.py:345
  (3 shorter events, 0.1 us)
Async XLA Ops:
  7.8 38.3 %copy-start = (bf16[2048,1024]{1,0:T(8,128)(2,1)S(1)}, bf16[2048,1024]{1,0:T(8,128)(2,1)}, u32[]{:S(2)}) copy-start(bf16[2048,1024]{1,0:T(8,128)(2,1)} %basis.5) | copy-start | bytes 12582916
  7.8 38.3 %copy-start.1 = (s32[2048]{0:T(1024)S(1)}, s32[2048]{0:T(1024)}, u32[]{:S(2)}) copy-start(s32[2048]{0:T(1024)} %param.11) | copy-start | bytes 24580
  48.5 1.5 %collective-permute-start = (f32[32,1024]{1,0:T(8,128)S(1)}, f32[32,1024]{1,0:T(8,128)S(1)}, u32[]{:S(2)}, u32[]{:S(2)}) collective-permute-start(f32[32,1024]{1,0:T(8,128)S(1)} %get-tuple-element.19), channel_id=1, source_target_pairs={{0,4},{4,0},{8,12},{12,8},{16,20},{20,16},{24,28},{28,24},{32,36},... | collective-permute-start | bytes 393224 | tf_op jit(solution)/shard_map/ppermute | solution.py:251
  49.9 5.7 %collective-permute-start.3 = (bf16[32,1024]{1,0:T(8,128)(2,1)S(1)}, bf16[32,1024]{1,0:T(8,128)(2,1)S(1)}, u32[]{:S(2)}, u32[]{:S(2)}) collective-permute-start(bf16[32,1024]{1,0:T(8,128)(2,1)S(1)} %get-tuple-element.21.after), channel_id=1, source_target_pairs={{0,64},{4,68},{8,72},{12,76},{16,80},{20,84},{24,88},{28,92},{32,9... | collective-permute-start | bytes 196616 | tf_op jit(solution)/shard_map/ppermute | solution.py:251
  51.0 4.7 %collective-permute-start.2 = (bf16[32,1024]{1,0:T(8,128)(2,1)S(1)}, bf16[32,1024]{1,0:T(8,128)(2,1)S(1)}, u32[]{:S(2)}, u32[]{:S(2)}) collective-permute-start(bf16[32,1024]{1,0:T(8,128)(2,1)S(1)} %get-tuple-element.21.after), channel_id=1, source_target_pairs={{0,32},{4,36},{8,40},{12,44},{16,48},{20,52},{24,56},{28,60},{32,0... | collective-permute-start | bytes 196616 | tf_op jit(solution)/shard_map/ppermute | solution.py:251
  51.5 4.9 %collective-permute-start.1 = (bf16[32,1024]{1,0:T(8,128)(2,1)S(1)}, bf16[32,1024]{1,0:T(8,128)(2,1)S(1)}, u32[]{:S(2)}, u32[]{:S(2)}) collective-permute-start(bf16[32,1024]{1,0:T(8,128)(2,1)S(1)} %get-tuple-element.21.after), channel_id=1, source_target_pairs={{0,96},{4,100},{8,104},{12,108},{16,112},{20,116},{24,120},{28,124... | collective-permute-start | bytes 196616 | tf_op jit(solution)/shard_map/ppermute | solution.py:251
  56.4 5.7 %collective-permute-start.6 = (bf16[32,1024]{1,0:T(8,128)(2,1)S(1)}, bf16[32,1024]{1,0:T(8,128)(2,1)S(1)}, u32[]{:S(2)}, u32[]{:S(2)}) collective-permute-start(bf16[32,1024]{1,0:T(8,128)(2,1)S(1)} %get-tuple-element.24.after), channel_id=1, source_target_pairs={{0,16},{4,20},{8,24},{12,28},{16,0},{20,4},{24,8},{28,12},{32,48},... | collective-permute-start | bytes 196616 | tf_op jit(solution)/shard_map/ppermute | solution.py:251
  57.2 4.9 %collective-permute-start.5 = (bf16[32,1024]{1,0:T(8,128)(2,1)S(1)}, bf16[32,1024]{1,0:T(8,128)(2,1)S(1)}, u32[]{:S(2)}, u32[]{:S(2)}) collective-permute-start(bf16[32,1024]{1,0:T(8,128)(2,1)S(1)} %get-tuple-element.24.after), channel_id=1, source_target_pairs={{0,8},{4,12},{8,0},{12,4},{16,24},{20,28},{24,16},{28,20},{32,40},... | collective-permute-start | bytes 196616 | tf_op jit(solution)/shard_map/ppermute | solution.py:251
  57.9 4.3 %collective-permute-start.4 = (bf16[32,1024]{1,0:T(8,128)(2,1)S(1)}, bf16[32,1024]{1,0:T(8,128)(2,1)S(1)}, u32[]{:S(2)}, u32[]{:S(2)}) collective-permute-start(bf16[32,1024]{1,0:T(8,128)(2,1)S(1)} %get-tuple-element.24.after), channel_id=1, source_target_pairs={{0,24},{4,28},{8,16},{12,20},{16,8},{20,12},{24,0},{28,4},{32,56},... | collective-permute-start | bytes 196616 | tf_op jit(solution)/shard_map/ppermute | solution.py:251
  62.3 4.2 %collective-permute-start.7 = (bf16[32,1024]{1,0:T(8,128)(2,1)S(1)}, bf16[32,1024]{1,0:T(8,128)(2,1)S(1)}, u32[]{:S(2)}, u32[]{:S(2)}) collective-permute-start(bf16[32,1024]{1,0:T(8,128)(2,1)S(1)} %add_parts.5.own), channel_id=1, source_target_pairs={{0,4},{4,0},{8,12},{12,8},{16,20},{20,16},{24,28},{28,24},{32,36},... | collective-permute-start | bytes 196616 | tf_op jit(solution)/shard_map/ppermute | solution.py:251

commit v11 on v10

--- a/solution.py
+++ b/solution.py
@@ -167,7 +167,7 @@
             totals[q][g] = totals[q][g] + received[p, q * COLS : (q + 1) * COLS, :].astype(F32)
         return c
 
-    lax.fori_loop(0, PEERS, peer, 0, unroll=2)
+    lax.fori_loop(0, PEERS, peer, 0, unroll=4)
 
 
 def sum_totals(totals, b):
@@ -292,7 +292,7 @@
             out[p, q * COLS : (q + 1) * COLS, :] = blocks[g]
         return c
 
-    lax.fori_loop(0, PEERS, peer, 0, unroll=2)
+    lax.fori_loop(0, PEERS, peer, 0, unroll=4)
     for c in copies:
         c.wait()
 

time: 139 us -> 139 us (level)
  no operation moved by 1% of the time
where the time goes in v11:
time: 139 us
  blocking collectives  103 us (74%)
  Pallas kernels  21.5 us (15%)
  starting transfers between devices  10.5 us (8%)
  waiting for transfers between devices  2.73 us (2%)
    all_to_all x3, blocking collectives, exchange(): lax.all_to_all(values, 'sub', split_axis=0, concat_axis=0, tiled=True)  103 us
    ppermute x8, starting transfers between devices, swapped(): return lax.ppermute(values, 'sub', pairs)  10.5 us
    pallas_call x1, Pallas kernels, first_apply(): pl.pallas_call(first_kernel, out_shape=(pltpu.VMEM((PEERS, SLOTROWS + IDR...  7.15 us
    pallas_call x2, Pallas kernels, merge(): pl.pallas_call(functools.partial(merge_kernel, part), out_shape=pltpu.VME...  4.73 us
    pallas_call x1, Pallas kernels, second_apply(): pl.pallas_call(second_kernel, out_shape=pltpu.VMEM((PEERS, SLOTROWS, BLK)...  3.54 us
  transfers between devices with their start and end apart: 8, of which 4 were waited for; matrix products, arithmetic and copies ran while one was open for 0% of the time, Pallas kernels for 3%

profile of v11, /device:TPU:1, one launch (start us, length us, event | category | flops | bytes accessed | tf_op | source)
XLA Modules:
  0.0 139.1 jit_solution(7363577698468337597)
XLA Ops:
  0.6 7.1 %first_apply.1 = (bf16[32,264,128]{2,1,0:T(8,128)(2,1)S(1)}, s32[64]{0:T(128)S(1)}, bf16[8,1024,1024]{2,1,0:T(8,128)(2,1)S(1)}) custom-call(s32[64]{0:T(128)} %bitcast.4, s32[64]{0:T(128)} %block_h.1, bf16[8,64,1024]{2,1,0:T(8,128)(2,1)} %loads.1, bf16[8,1024,1024]{2,1,0:T(8,128)(2,1)} %ops.1), custom_call_target="tpu_custom_call" | custom-call | tf_op jit(solution)/shard_map/first_apply/pallas_call | solution.py:96
  7.8 0.0 copy-start
  7.8 0.0 copy-start.1
  7.8 38.3 %all_to_all.15.received = bf16[32,264,128]{2,1,0:T(8,128)(2,1)S(1)} all-to-all(bf16[32,264,128]{2,1,0:T(8,128)(2,1)S(1)} %get-tuple-element.16), channel_id=1, replica_groups=mesh['sub'=32,'rep'=4] {'sub'}, dimensions={0} | all-to-all | bytes 4325376 | tf_op jit(solution)/shard_map/all_to_all | solution.py:363
  46.1 0.0 copy-done
  46.1 0.0 copy-done.1
  46.1 2.3 %project.1 = (f32[16,64,128]{2,1,0:T(8,128)S(1)}, f32[32,1024]{1,0:T(8,128)S(1)}, f32[32,1024]{1,0:T(8,128)S(1)}, s32[32,128]{1,0:T(8,128)S(1)}, bf16[1024,1024]{1,0:T(8,128)(2,1)S(1)}) custom-call(bf16[32,264,128]{2,1,0:T(8,128)(2,1)S(1)} %all_to_all.15.received, s32[16,128]{1,0:T(8,128)S(1)} %bitcast.2, bf16[2048,1024]{1,0:T(8,128)(2,1)S(1)} %copy-done, ...), custom_call_target="tpu_custom_call" | custom-call | tf_op jit(solution)/shard_map/project/pallas_call | solution.py:204
  48.4 0.5 collective-permute-start
  48.9 1.0 collective-permute-done.refs_1_
  49.9 1.0 collective-permute-start.3
  51.0 0.5 collective-permute-start.2
  51.4 1.8 %collective-permute-start.1 = (bf16[32,1024]{1,0:T(8,128)(2,1)S(1)}, bf16[32,1024]{1,0:T(8,128)(2,1)S(1)}, u32[]{:S(2)}, u32[]{:S(2)}) collective-permute-start(bf16[32,1024]{1,0:T(8,128)(2,1)S(1)} %get-tuple-element.21.after), channel_id=1, source_target_pairs={{0,96},{4,100},{8,104},{12,108},{16,112},{20,116},{24,120},{28,124... | collective-permute-start | bytes 196616 | tf_op jit(solution)/shard_map/ppermute | solution.py:251
  53.2 2.4 %merge.2.refs_4_.first = bf16[1024,1024]{1,0:T(8,128)(2,1)S(1)} custom-call(bf16[1024,1024]{1,0:T(8,128)(2,1)S(1)} %get-tuple-element.22.coarse, bf16[2048,1024]{1,0:T(8,128)(2,1)S(1)} %copy-done, bf16[32,1024]{1,0:T(8,128)(2,1)S(1)} %get-tuple-element.21.after), custom_call_target="tpu_custom_call" | custom-call | tf_op jit(solution)/shard_map/merge/pallas_call | solution.py:147
  55.6 0.0 collective-permute-done.3.refs_3_
  55.6 0.0 collective-permute-done.2.refs_2_
  55.6 0.7 collective-permute-done.1.refs_1_
  56.4 0.8 collective-permute-start.6
  57.2 0.7 collective-permute-start.5
  57.9 1.8 %collective-permute-start.4 = (bf16[32,1024]{1,0:T(8,128)(2,1)S(1)}, bf16[32,1024]{1,0:T(8,128)(2,1)S(1)}, u32[]{:S(2)}, u32[]{:S(2)}) collective-permute-start(bf16[32,1024]{1,0:T(8,128)(2,1)S(1)} %get-tuple-element.24.after), channel_id=1, source_target_pairs={{0,24},{4,28},{8,16},{12,20},{16,8},{20,12},{24,0},{28,4},{32,56},... | collective-permute-start | bytes 196616 | tf_op jit(solution)/shard_map/ppermute | solution.py:251
  59.7 2.4 %merge.3.refs_4_.second = bf16[1024,1024]{1,0:T(8,128)(2,1)S(1)} custom-call(bf16[1024,1024]{1,0:T(8,128)(2,1)S(1)} %get-tuple-element.22.coarse, bf16[2048,1024]{1,0:T(8,128)(2,1)S(1)} %copy-done, bf16[32,1024]{1,0:T(8,128)(2,1)S(1)} %get-tuple-element.24.after), custom_call_target="tpu_custom_call" | custom-call | tf_op jit(solution)/shard_map/merge/pallas_call | solution.py:147
  62.1 0.0 collective-permute-done.6.refs_3_
  62.1 0.0 collective-permute-done.5.refs_2_
  62.1 0.1 collective-permute-done.4.refs_1_
  62.3 3.3 %collective-permute-start.7 = (bf16[32,1024]{1,0:T(8,128)(2,1)S(1)}, bf16[32,1024]{1,0:T(8,128)(2,1)S(1)}, u32[]{:S(2)}, u32[]{:S(2)}) collective-permute-start(bf16[32,1024]{1,0:T(8,128)(2,1)S(1)} %add_parts.5.own), channel_id=1, source_target_pairs={{0,4},{4,0},{8,12},{12,8},{16,20},{20,16},{24,28},{28,24},{32,36},... | collective-permute-start | bytes 196616 | tf_op jit(solution)/shard_map/ppermute | solution.py:251
  65.6 0.9 collective-permute-done.7.other
  66.5 1.6 %start_values.1 = (f32[64,2048]{1,0:T(8,128)}, bf16[32,256,128]{2,1,0:T(8,128)(2,1)S(1)}) custom-call(s32[32,128]{1,0:T(8,128)S(1)} %get-tuple-element.17.ids_v, bf16[32,1024]{1,0:T(8,128)(2,1)S(1)} %add_parts.5.own, bf16[32,1024]{1,0:T(8,128)(2,1)S(1)} %collective-permute-done.7.other, bf16[1024,1024]{1,0:T(8,128)(2,1)S(1)} %merge.2.refs_4_.first, ...), custom_call_target="tpu_custom_call" | custom-call | tf_op jit(solution)/shard_map/start_values/pallas_call | solution.py:301
  68.1 33.3 %all_to_all.16.back = bf16[32,256,128]{2,1,0:T(8,128)(2,1)S(1)} all-to-all(bf16[32,256,128]{2,1,0:T(8,128)(2,1)S(1)} %get-tuple-element.27), channel_id=1, replica_groups=mesh['sub'=32,'rep'=4] {'sub'}, dimensions={0} | all-to-all | bytes 4194304 | tf_op jit(solution)/shard_map/all_to_all | solution.py:363
  101.4 3.5 %second_apply.1 = bf16[32,256,128]{2,1,0:T(8,128)(2,1)S(1)} custom-call(s32[64]{0:T(128)S(1)} %get-tuple-element.26.pos, bf16[32,256,128]{2,1,0:T(8,128)(2,1)S(1)} %all_to_all.16.back, bf16[8,1024,1024]{2,1,0:T(8,128)(2,1)S(1)} %get-tuple-element.28.ops), custom_call_target="tpu_custom_call" | custom-call | tf_op jit(solution)/shard_map/second_apply/pallas_call | solution.py:128
  104.9 31.9 %all_to_all.17.received = bf16[32,256,128]{2,1,0:T(8,128)(2,1)S(1)} all-to-all(bf16[32,256,128]{2,1,0:T(8,128)(2,1)S(1)} %second_apply.1), channel_id=1, replica_groups=mesh['sub'=32,'rep'=4] {'sub'}, dimensions={0} | all-to-all | bytes 4194304 | tf_op jit(solution)/shard_map/all_to_all | solution.py:363
  136.8 2.1 %residual.1 = f32[64,2048]{1,0:T(8,128)} custom-call(s32[32,128]{1,0:T(8,128)S(1)} %get-tuple-element.17.ids_v, bf16[32,256,128]{2,1,0:T(8,128)(2,1)S(1)} %all_to_all.17.received, s32[16,128]{1,0:T(8,128)S(1)} %bitcast.3, f32[16,64,128]{2,1,0:T(8,128)S(1)} %get-tuple-element.29.dual), custom_call_target="tpu_custom_call" | custom-call | tf_op jit(solution)/shard_map/residual/pallas_call | solution.py:345
  (3 shorter events, 0.1 us)
Async XLA Ops:
  7.8 38.3 %copy-start = (bf16[2048,1024]{1,0:T(8,128)(2,1)S(1)}, bf16[2048,1024]{1,0:T(8,128)(2,1)}, u32[]{:S(2)}) copy-start(bf16[2048,1024]{1,0:T(8,128)(2,1)} %basis.5) | copy-start | bytes 12582916
  7.8 38.3 %copy-start.1 = (s32[2048]{0:T(1024)S(1)}, s32[2048]{0:T(1024)}, u32[]{:S(2)}) copy-start(s32[2048]{0:T(1024)} %param.11) | copy-start | bytes 24580
  48.4 1.5 %collective-permute-start = (f32[32,1024]{1,0:T(8,128)S(1)}, f32[32,1024]{1,0:T(8,128)S(1)}, u32[]{:S(2)}, u32[]{:S(2)}) collective-permute-start(f32[32,1024]{1,0:T(8,128)S(1)} %get-tuple-element.19), channel_id=1, source_target_pairs={{0,4},{4,0},{8,12},{12,8},{16,20},{20,16},{24,28},{28,24},{32,36},... | collective-permute-start | bytes 393224 | tf_op jit(solution)/shard_map/ppermute | solution.py:251
  49.9 5.7 %collective-permute-start.3 = (bf16[32,1024]{1,0:T(8,128)(2,1)S(1)}, bf16[32,1024]{1,0:T(8,128)(2,1)S(1)}, u32[]{:S(2)}, u32[]{:S(2)}) collective-permute-start(bf16[32,1024]{1,0:T(8,128)(2,1)S(1)} %get-tuple-element.21.after), channel_id=1, source_target_pairs={{0,64},{4,68},{8,72},{12,76},{16,80},{20,84},{24,88},{28,92},{32,9... | collective-permute-start | bytes 196616 | tf_op jit(solution)/shard_map/ppermute | solution.py:251
  51.0 4.7 %collective-permute-start.2 = (bf16[32,1024]{1,0:T(8,128)(2,1)S(1)}, bf16[32,1024]{1,0:T(8,128)(2,1)S(1)}, u32[]{:S(2)}, u32[]{:S(2)}) collective-permute-start(bf16[32,1024]{1,0:T(8,128)(2,1)S(1)} %get-tuple-element.21.after), channel_id=1, source_target_pairs={{0,32},{4,36},{8,40},{12,44},{16,48},{20,52},{24,56},{28,60},{32,0... | collective-permute-start | bytes 196616 | tf_op jit(solution)/shard_map/ppermute | solution.py:251
  51.4 4.9 %collective-permute-start.1 = (bf16[32,1024]{1,0:T(8,128)(2,1)S(1)}, bf16[32,1024]{1,0:T(8,128)(2,1)S(1)}, u32[]{:S(2)}, u32[]{:S(2)}) collective-permute-start(bf16[32,1024]{1,0:T(8,128)(2,1)S(1)} %get-tuple-element.21.after), channel_id=1, source_target_pairs={{0,96},{4,100},{8,104},{12,108},{16,112},{20,116},{24,120},{28,124... | collective-permute-start | bytes 196616 | tf_op jit(solution)/shard_map/ppermute | solution.py:251
  56.4 5.7 %collective-permute-start.6 = (bf16[32,1024]{1,0:T(8,128)(2,1)S(1)}, bf16[32,1024]{1,0:T(8,128)(2,1)S(1)}, u32[]{:S(2)}, u32[]{:S(2)}) collective-permute-start(bf16[32,1024]{1,0:T(8,128)(2,1)S(1)} %get-tuple-element.24.after), channel_id=1, source_target_pairs={{0,16},{4,20},{8,24},{12,28},{16,0},{20,4},{24,8},{28,12},{32,48},... | collective-permute-start | bytes 196616 | tf_op jit(solution)/shard_map/ppermute | solution.py:251
  57.2 4.9 %collective-permute-start.5 = (bf16[32,1024]{1,0:T(8,128)(2,1)S(1)}, bf16[32,1024]{1,0:T(8,128)(2,1)S(1)}, u32[]{:S(2)}, u32[]{:S(2)}) collective-permute-start(bf16[32,1024]{1,0:T(8,128)(2,1)S(1)} %get-tuple-element.24.after), channel_id=1, source_target_pairs={{0,8},{4,12},{8,0},{12,4},{16,24},{20,28},{24,16},{28,20},{32,40},... | collective-permute-start | bytes 196616 | tf_op jit(solution)/shard_map/ppermute | solution.py:251
  57.9 4.3 %collective-permute-start.4 = (bf16[32,1024]{1,0:T(8,128)(2,1)S(1)}, bf16[32,1024]{1,0:T(8,128)(2,1)S(1)}, u32[]{:S(2)}, u32[]{:S(2)}) collective-permute-start(bf16[32,1024]{1,0:T(8,128)(2,1)S(1)} %get-tuple-element.24.after), channel_id=1, source_target_pairs={{0,24},{4,28},{8,16},{12,20},{16,8},{20,12},{24,0},{28,4},{32,56},... | collective-permute-start | bytes 196616 | tf_op jit(solution)/shard_map/ppermute | solution.py:251
  62.3 4.2 %collective-permute-start.7 = (bf16[32,1024]{1,0:T(8,128)(2,1)S(1)}, bf16[32,1024]{1,0:T(8,128)(2,1)S(1)}, u32[]{:S(2)}, u32[]{:S(2)}) collective-permute-start(bf16[32,1024]{1,0:T(8,128)(2,1)S(1)} %add_parts.5.own), channel_id=1, source_target_pairs={{0,4},{4,0},{8,12},{12,8},{16,20},{20,16},{24,28},{28,24},{32,36},... | collective-permute-start | bytes 196616 | tf_op jit(solution)/shard_map/ppermute | solution.py:251
